TPU v7x, 32 devices: a whole 2x2x4 slice. The times are simulated.
32 devices in a mesh: prow: 4 (over y, core), pcol: 8 (over z, x).
Axes of the slice: x: 2, y: 2, z: 4, core: 2. Of those that a mesh axis runs over, the one named last changes fastest.
Arguments:
- right_side: float32 [8, 256, 128], P(None, 'prow'), may hold values from -6 to 6
- lower_prev: float32 [8, 256, 129024], P(None, 'prow', 'pcol'), may hold values from -0.015625 to 0.015625
- solved_prev: float32 [129024, 128], P('pcol'), may hold values from -6 to 6
- lower_window: float32 [8, 256, 2048], P(None, 'prow', 'pcol'), may hold values from -0.1875 to 0.1875
- inverse_diag: float32 [8, 256, 256], P(None, 'prow'), may hold values from -0.25 to 1.4, as said below
Outputs:
- solution: float32 [8, 256, 128], P(None, 'prow')
Inputs may be any that keep to these rules, and one draw needn't show every extreme that they name: `inverse_diag`: each block is lower triangular: zero above its diagonal, with diagonal entries of 0.7 to 1.4.
All inputs are finite; a program needn't handle non-finite values.
Results may differ from a plain program's by a relative error of at most 0.00011.
Values sent between devices are 32-bit elements; how exact they have to be, the bound alone decides.
No kernel may reach another device: no remote copies, remote signals or barrier semaphores. Data moves between devices by JAX's collectives and lax.ppermute only.
A program may use at most 128 MiB of HBM per device.

v0:
```python
import jax
import jax.numpy as jnp
from jax import lax
from jax.sharding import PartitionSpec as P


def local(right_side, lower_prev, solved_prev, lower_window, inverse_diag):
    highest = lax.Precision.HIGHEST
    blocks = right_side.shape[0]
    local_rows = right_side.shape[1]
    columns = right_side.shape[2]
    block_rows = inverse_diag.shape[2]
    row_start = lax.axis_index("prow") * local_rows
    solved = jnp.zeros((blocks * block_rows, columns), jnp.float32)
    pieces = []
    full_inverse = lax.all_gather(inverse_diag, "prow", axis=1, tiled=True)
    full_window = lax.all_gather(lower_window, "pcol", axis=2, tiled=True)
    for row_block in range(blocks):
        window_term = jnp.dot(
            full_window[row_block], solved, precision=highest, preferred_element_type=jnp.float32
        )
        earlier_part = jnp.dot(
            lower_prev[row_block],
            solved_prev,
            precision=highest,
            preferred_element_type=jnp.float32,
        )
        earlier_here = lax.psum(earlier_part, "pcol")
        local_residual = right_side[row_block] - (earlier_here + window_term)
        residual = lax.all_gather(local_residual, "prow", axis=0, tiled=True)
        whole_rows = jnp.dot(
            full_inverse[row_block], residual, precision=highest, preferred_element_type=jnp.float32
        )
        pieces.append(lax.dynamic_slice_in_dim(whole_rows, row_start, local_rows, 0))
        solved = lax.dynamic_update_slice_in_dim(solved, whole_rows, row_block * block_rows, 0)
    return jnp.stack(pieces)


def solution(mesh):
    in_specs = (
        P(None, "prow", None),
        P(None, "prow", "pcol"),
        P("pcol", None),
        P(None, "prow", "pcol"),
        P(None, "prow", None),
    )
    out_specs = P(None, "prow", None)
    return jax.shard_map(local, mesh=mesh, in_specs=in_specs, out_specs=out_specs, check_vma=False)
```

profile of v0, /device:TPU:0, one launch (start us, length us, event | category | flops | bytes accessed | tf_op | source)
XLA Modules:
  0.0 249.4 jit_solution(15784132453054589347)
XLA Ops:
  6.5 0.0 all-gather.3.cloned.1.call-start
  6.5 0.7 all-gather.3.cloned.1.call-update
  7.3 0.0 all-reduce.4.cloned.1.call-start
  7.3 0.0 copy-start
  7.3 10.7 %fusion.4 = f32[64,128]{1,0:T(8,128)} fusion(f32[16128,128]{1,0:T(8,128)} %param.7, f32[8,64,16128]{2,1,0:T(8,128)} %param.6), kind=kOutput, calls=%fused_computation.4 | convolution fusion | flops 1585446912 | bytes 12419072 | tf_op jit(solution)/shard_map/dot_general | solution.py:22
  18.0 0.0 copy-done
  18.0 8.2 %fusion.6 = f32[64,128]{1,0:T(8,128)} fusion(f32[16128,128]{1,0:T(8,128)S(1)} %copy-done, f32[8,64,16128]{2,1,0:T(8,128)} %param.6), kind=kOutput, calls=%fused_computation.6 | convolution fusion | flops 1585446912 | bytes 12419072 | tf_op jit(solution)/shard_map/dot_general | solution.py:22
  26.2 7.9 %fusion.8 = f32[64,128]{1,0:T(8,128)} fusion(f32[16128,128]{1,0:T(8,128)S(1)} %copy-done, f32[8,64,16128]{2,1,0:T(8,128)} %param.6), kind=kOutput, calls=%fused_computation.8 | convolution fusion | flops 1585446912 | bytes 12419072 | tf_op jit(solution)/shard_map/dot_general | solution.py:22
  34.1 8.1 %fusion.10 = f32[64,128]{1,0:T(8,128)} fusion(f32[16128,128]{1,0:T(8,128)S(1)} %copy-done, f32[8,64,16128]{2,1,0:T(8,128)} %param.6), kind=kOutput, calls=%fused_computation.10 | convolution fusion | flops 1585446912 | bytes 12419072 | tf_op jit(solution)/shard_map/dot_general | solution.py:22
  42.2 7.9 %fusion.12 = f32[64,128]{1,0:T(8,128)} fusion(f32[16128,128]{1,0:T(8,128)S(1)} %copy-done, f32[8,64,16128]{2,1,0:T(8,128)} %param.6), kind=kOutput, calls=%fused_computation.12 | convolution fusion | flops 1585446912 | bytes 12419072 | tf_op jit(solution)/shard_map/dot_general | solution.py:22
  50.1 8.2 %fusion.14 = f32[64,128]{1,0:T(8,128)} fusion(f32[16128,128]{1,0:T(8,128)S(1)} %copy-done, f32[8,64,16128]{2,1,0:T(8,128)} %param.6), kind=kOutput, calls=%fused_computation.14 | convolution fusion | flops 1585446912 | bytes 12419072 | tf_op jit(solution)/shard_map/dot_general | solution.py:22
  58.3 7.9 %fusion = f32[64,128]{1,0:T(8,128)} fusion(f32[16128,128]{1,0:T(8,128)S(1)} %copy-done, f32[8,64,16128]{2,1,0:T(8,128)} %param.6), kind=kOutput, calls=%fused_computation | convolution fusion | flops 1585446912 | bytes 12419072 | tf_op jit(solution)/shard_map/dot_general | solution.py:22
  66.3 0.0 copy-start.3
  66.3 8.4 %fusion.2 = f32[64,128]{1,0:T(8,128)} fusion(f32[16128,128]{1,0:T(8,128)S(1)} %copy-done, f32[8,64,16128]{2,1,0:T(8,128)} %param.6), kind=kOutput, calls=%fused_computation.2 | convolution fusion | flops 1585446912 | bytes 12419072 | tf_op jit(solution)/shard_map/dot_general | solution.py:22
  74.7 0.0 all-reduce.4.cloned.1.call-update
  74.7 0.0 all-gather.5.cloned.1.call-start
  74.7 0.7 all-gather.5.cloned.1.call-update
  75.4 11.7 %all-gather.3.cloned.1.call-done = f32[8,64,2048]{2,1,0:T(8,128)} async-done(((f32[8,64,256]{2,1,0:T(8,128)}), f32[8,64,2048]{2,1,0:T(8,128)}) %all-gather.3.cloned.1.call-update) | async-done | bytes 4194320 | tf_op jit(solution)/shard_map/all_gather | solution.py:17
  87.2 1.2 fusion.38
  88.3 73.8 %all-reduce.4.cloned.1.call-done = (f32[64,128]{1,0:T(8,128)}, f32[64,128]{1,0:T(8,128)}, f32[64,128]{1,0:T(8,128)}, f32[64,128]{1,0:T(8,128)}, f32[64,128]{1,0:...) async-done(((f32[64,128]{1,0:T(8,128)}, f32[64,128]{1,0:T(8,128)}, f32[64,128]{1,0:T(8,128)}, f32[64,128]{1,0:T(8,128)}, f32[64,128]{1,0:T(8,128)}, ...) | async-done | bytes 262160 | tf_op jit(solution)/shard_map/psum | solution.py:28
  162.1 0.0 copy-done.3
  162.1 0.8 bitcast_subtract_fusion
  163.0 5.4 %all_gather.31 = f32[256,128]{1,0:T(8,128)S(1)} all-gather(f32[64,128]{1,0:T(8,128)S(1)} %bitcast_subtract_fusion), channel_id=1, replica_groups=mesh['prow'=4,'pcol'=8] {'prow'}, dimensions={0}, use_global_device_ids=true | all-gather | bytes 163840 | tf_op jit(solution)/shard_map/all_gather | solution.py:30
  168.4 17.4 %all-gather.5.cloned.1.call-done = f32[8,256,256]{2,1,0:T(8,128)} async-done(((f32[8,64,256]{2,1,0:T(8,128)}), f32[8,256,256]{2,1,0:T(8,128)}) %all-gather.5.cloned.1.call-update) | async-done | bytes 2097168 | tf_op jit(solution)/shard_map/all_gather | solution.py:16
  185.8 1.5 fusion.47
  187.3 2.1 fusion.25
  189.4 5.4 %all_gather.33 = f32[256,128]{1,0:T(8,128)S(1)} all-gather(f32[64,128]{1,0:T(8,128)S(1)} %fusion.25), channel_id=1, replica_groups=mesh['prow'=4,'pcol'=8] {'prow'}, dimensions={0}, use_global_device_ids=true | all-gather | bytes 163840 | tf_op jit(solution)/shard_map/all_gather | solution.py:30
  194.8 0.1 bitcast_dynamic-update-slice_fusion.13
  194.9 0.1 dynamic_update_slice.21
  195.0 0.0 copy-start.6
  195.0 1.4 bitcast_dynamic-update-slice_fusion.5
  196.4 2.3 fusion.27
  198.7 5.4 %all_gather.34 = f32[256,128]{1,0:T(8,128)S(1)} all-gather(f32[64,128]{1,0:T(8,128)S(1)} %fusion.27), channel_id=1, replica_groups=mesh['prow'=4,'pcol'=8] {'prow'}, dimensions={0}, use_global_device_ids=true | all-gather | bytes 163840 | tf_op jit(solution)/shard_map/all_gather | solution.py:30
  204.1 1.4 bitcast_dynamic-update-slice_fusion.4
  205.5 0.0 copy-done.8
  205.5 0.0 copy-done.1
  205.5 1.2 fusion.29
  206.7 5.6 %all_gather.35 = f32[256,128]{1,0:T(8,128)S(1)} all-gather(f32[64,128]{1,0:T(8,128)S(1)} %fusion.29), channel_id=1, replica_groups=mesh['prow'=4,'pcol'=8] {'prow'}, dimensions={0}, use_global_device_ids=true | all-gather | bytes 163840 | tf_op jit(solution)/shard_map/all_gather | solution.py:30
  212.3 0.0 copy-done.2
  212.3 0.4 bitcast_dynamic-update-slice_fusion.3
  212.7 0.0 copy-done.7
  212.7 1.2 fusion.31
  213.9 5.4 %all_gather.36 = f32[256,128]{1,0:T(8,128)S(1)} all-gather(f32[64,128]{1,0:T(8,128)S(1)} %fusion.31), channel_id=1, replica_groups=mesh['prow'=4,'pcol'=8] {'prow'}, dimensions={0}, use_global_device_ids=true | all-gather | bytes 163840 | tf_op jit(solution)/shard_map/all_gather | solution.py:30
  219.4 0.4 bitcast_dynamic-update-slice_fusion.2
  219.8 0.0 copy-done.6
  219.8 1.2 fusion.33
  221.0 5.4 %all_gather.37 = f32[256,128]{1,0:T(8,128)S(1)} all-gather(f32[64,128]{1,0:T(8,128)S(1)} %fusion.33), channel_id=1, replica_groups=mesh['prow'=4,'pcol'=8] {'prow'}, dimensions={0}, use_global_device_ids=true | all-gather | bytes 163840 | tf_op jit(solution)/shard_map/all_gather | solution.py:30
  226.4 0.4 bitcast_dynamic-update-slice_fusion.1
  226.9 0.0 copy-done.5
  226.9 1.2 fusion.35
  228.1 5.6 %all_gather.38 = f32[256,128]{1,0:T(8,128)S(1)} all-gather(f32[64,128]{1,0:T(8,128)S(1)} %fusion.35), channel_id=1, replica_groups=mesh['prow'=4,'pcol'=8] {'prow'}, dimensions={0}, use_global_device_ids=true | all-gather | bytes 163840 | tf_op jit(solution)/shard_map/all_gather | solution.py:30
  233.7 0.4 bitcast_dynamic-update-slice_fusion
  234.1 0.0 copy-done.4
  234.1 1.2 fusion.37
  235.3 5.4 %all_gather.39 = f32[256,128]{1,0:T(8,128)S(1)} all-gather(f32[64,128]{1,0:T(8,128)S(1)} %fusion.37), channel_id=1, replica_groups=mesh['prow'=4,'pcol'=8] {'prow'}, dimensions={0}, use_global_device_ids=true | all-gather | bytes 163840 | tf_op jit(solution)/shard_map/all_gather | solution.py:30
  240.8 0.1 bitcast_dynamic-update-slice_fusion.12
  240.8 0.1 bitcast_dynamic-update-slice_fusion.11
  240.9 0.1 bitcast_dynamic-update-slice_fusion.10
  241.0 0.1 bitcast_dynamic-update-slice_fusion.9
  241.1 0.1 bitcast_dynamic-update-slice_fusion.8
  241.2 0.1 bitcast_dynamic-update-slice_fusion.7
  241.3 0.4 fusion.40
  241.7 0.1 bitcast_dynamic-update-slice_fusion.6
  241.8 0.9 copy.7
  (6 shorter events, 0.0 us)
Async XLA Ops:
  6.5 80.6 %all-gather.3.cloned.1.call-start = ((), (), s32[]{:S(2)}) async-start(), calls=%async_computation | async-start | bytes 4718592 | tf_op jit(solution)/shard_map/all_gather | solution.py:17
  7.3 154.9 %all-reduce.4.cloned.1.call-start = ((), (), s32[]{:S(2)}) async-start(), calls=%async_computation.2 | async-start | bytes 524288 | tf_op jit(solution)/shard_map/psum | solution.py:28
  7.3 10.7 %copy-start = (f32[16128,128]{1,0:T(8,128)S(1)}, f32[16128,128]{1,0:T(8,128)}, u32[]{:S(2)}) copy-start(f32[16128,128]{1,0:T(8,128)} %param.7) | copy-start | bytes 24772612
  66.3 95.8 %copy-start.3 = (f32[8,64,128]{2,1,0:T(8,128)S(1)}, f32[8,64,128]{2,1,0:T(8,128)}, u32[]{:S(2)}) copy-start(f32[8,64,128]{2,1,0:T(8,128)} %param.5) | copy-start | bytes 786436
  74.7 111.1 %all-gather.5.cloned.1.call-start = ((), (), s32[]{:S(2)}) async-start(), calls=%async_computation.1 | async-start | bytes 2621440 | tf_op jit(solution)/shard_map/all_gather | solution.py:16
  162.1 43.4 %copy-start.8 = (f32[64,128]{1,0:T(8,128)S(1)}, f32[64,128]{1,0:T(8,128)}, u32[]{:S(2)}) copy-start(f32[64,128]{1,0:T(8,128)} %get-tuple-element.8) | copy-start | bytes 98308
  168.4 44.4 %copy-start.7 = (f32[64,128]{1,0:T(8,128)S(1)}, f32[64,128]{1,0:T(8,128)}, u32[]{:S(2)}) copy-start(f32[64,128]{1,0:T(8,128)} %get-tuple-element.9) | copy-start | bytes 98308
  185.8 19.7 %copy-start.1 = (f32[8,64,2048]{2,1,0:T(8,128)S(1)}, f32[8,64,2048]{2,1,0:T(8,128)}, u32[]{:S(2)}) copy-start(f32[8,64,2048]{2,1,0:T(8,128)} %all-gather.3.cloned.1.call-done) | copy-start | bytes 12582916
  185.8 26.5 %copy-start.2 = (f32[8,256,256]{2,1,0:T(8,128)S(1)}, f32[8,256,256]{2,1,0:T(8,128)}, u32[]{:S(2)}) copy-start(f32[8,256,256]{2,1,0:T(8,128)} %all-gather.5.cloned.1.call-done) | copy-start | bytes 6291460
  195.0 24.8 %copy-start.6 = (f32[64,128]{1,0:T(8,128)S(1)}, f32[64,128]{1,0:T(8,128)}, u32[]{:S(2)}) copy-start(f32[64,128]{1,0:T(8,128)} %get-tuple-element.10) | copy-start | bytes 98308
  198.7 28.2 %copy-start.5 = (f32[64,128]{1,0:T(8,128)S(1)}, f32[64,128]{1,0:T(8,128)}, u32[]{:S(2)}) copy-start(f32[64,128]{1,0:T(8,128)} %get-tuple-element.11) | copy-start | bytes 98308
  206.7 27.4 %copy-start.4 = (f32[64,128]{1,0:T(8,128)S(1)}, f32[64,128]{1,0:T(8,128)}, u32[]{:S(2)}) copy-start(f32[64,128]{1,0:T(8,128)} %get-tuple-element.12) | copy-start | bytes 98308
Sparse Core Ops, SparseCore 0:
  9.4 77.7 all-gather.2
  91.4 70.6 all-reduce.3
  163.8 21.9 all-gather.4
where the time goes:
time: 253 us; the launch traced here: 249 us
  waiting for transfers between devices  104 us (41%)
  matrix products  84.1 us (33%)
  blocking collectives  43.7 us (17%)
  between operations  13.5 us (5%)
    psum x1, waiting for transfers between devices, local(): earlier_here = lax.psum(earlier_part, 'pcol')  73.8 us
    dot_general x8, matrix products, local(): jnp.dot(lower_prev[row_block], solved_prev, precision=highest, preferred_...  67.3 us
    all_gather x8, blocking collectives, local(): residual = lax.all_gather(local_residual, 'prow', axis=0, tiled=True)  43.7 us
    all_gather x1, waiting for transfers between devices, local(): full_inverse = lax.all_gather(inverse_diag, 'prow', axis=1, tiled=True)  17.4 us
    all_gather x1, waiting for transfers between devices, local(): full_window = lax.all_gather(lower_window, 'pcol', axis=2, tiled=True)  11.7 us
    dot_general x7, matrix products, local(): jnp.dot(full_window[row_block], solved, precision=highest, preferred_elem...  10.4 us
    dot_general x8, matrix products, local(): jnp.dot(full_inverse[row_block], residual, precision=highest, preferred_e...  6.33 us
  transfers between devices with their start and end apart: 3, of which 3 were waited for; matrix products, arithmetic and copies ran while one was open for 28% of the time, Pallas kernels for 0%

commit v1 on v0

v1 whole, which is shorter than its diff:
```python
import functools

import jax
import jax.numpy as jnp
from jax import lax
from jax.experimental import pallas as pl
from jax.experimental.pallas import tpu as pltpu
from jax.sharding import Mesh, PartitionSpec as P

F32 = jnp.float32
BF16 = jnp.bfloat16
EVERY = ("z", "y", "core", "x")
SWAP = [(0, 1), (1, 0)]
PLANES = 4
RHS_PART = 16
SUPER = 512
VMEM_LIMIT = 56 << 20


def halves(value):
    high = value.astype(BF16)
    low = (value - high.astype(F32)).astype(BF16)
    return high, low


def dot_f32(a, b):
    return jnp.dot(a, b, preferred_element_type=F32)


def dot_rows(a, b):
    return lax.dot_general(a, b, (((1,), (1,)), ((), ())), preferred_element_type=F32)


def add_products(factor_ref, solved_ref, total):
    factor_high, factor_low = halves(factor_ref[...])
    solved_both = jnp.concatenate(halves(solved_ref[...]), axis=1)
    total[...] += dot_f32(factor_high, solved_both) + dot_f32(factor_low, solved_both)


def earlier_first(factor_ref, solved_ref, total_ref):
    @pl.when(pl.program_id(0) == 0)
    def _():
        total_ref[...] = jnp.zeros_like(total_ref)

    add_products(factor_ref, solved_ref, total_ref)


def earlier_last(first_ref, factor_ref, solved_ref, total_in, right_ref, out_ref, total):
    step = pl.program_id(0)

    @pl.when(step == 0)
    def _():
        total[...] = total_in[...]

    add_products(factor_ref, solved_ref, total)

    @pl.when(step == pl.num_programs(0) - 1)
    def _():
        keep = first_ref[0] == 0
        width = right_ref.shape[1]
        for part in range(PLANES):
            rows = slice(part * 128, part * 128 + 128)
            earlier = total[rows, :width] + total[rows, width:]
            right = jnp.where(keep, right_ref[rows, :], 0.0)
            out_ref[part] = (right - earlier).T


def earlier_sums(first, factor, solved, right, tile, head):
    rows, depth = factor.shape
    columns = solved.shape[1]
    steps = depth // tile

    def cost(count):
        return pl.CostEstimate(
            flops=8 * rows * columns * tile * count,
            bytes_accessed=4 * (rows + columns) * tile * count,
            transcendentals=0,
        )

    total = pl.pallas_call(
        earlier_first,
        out_shape=jax.ShapeDtypeStruct((rows, 2 * columns), F32),
        grid=(head,),
        in_specs=[
            pl.BlockSpec((rows, tile), lambda k: (0, k)),
            pl.BlockSpec((tile, columns), lambda k: (k, 0)),
        ],
        out_specs=pl.BlockSpec((rows, 2 * columns), lambda k: (0, 0)),
        compiler_params=pltpu.CompilerParams(vmem_limit_bytes=VMEM_LIMIT),
        cost_estimate=cost(head),
        name="earlier_first",
    )(factor, solved)

    def finish(total):
        return pl.pallas_call(
            earlier_last,
            out_shape=jax.ShapeDtypeStruct((PLANES, columns, 128), F32),
            grid=(steps - head,),
            in_specs=[
                pl.BlockSpec(memory_space=pltpu.SMEM),
                pl.BlockSpec((rows, tile), lambda k: (0, k + head)),
                pl.BlockSpec((tile, columns), lambda k: (k + head, 0)),
                pl.BlockSpec((rows, 2 * columns), lambda k: (0, 0)),
                pl.BlockSpec((rows, columns), lambda k: (0, 0)),
            ],
            out_specs=pl.BlockSpec((PLANES, columns, 128), lambda k: (0, 0, 0)),
            scratch_shapes=[pltpu.VMEM((rows, 2 * columns), F32)],
            compiler_params=pltpu.CompilerParams(vmem_limit_bytes=VMEM_LIMIT),
            cost_estimate=cost(steps - head),
            name="earlier_last",
        )(first, factor, solved, total, right)

    return total, finish


def arrange(place_ref, *refs):
    pieces, out_ref = refs[:-1], refs[-1]
    y, core, x = place_ref[0], place_ref[1], place_ref[2]
    for index, (dy, dx, start, count) in enumerate(PIECES):
        for other in range(2):
            piece = pieces[2 * index + other]
            row_part = 2 * (y + dy - 2 * y * dy) + (core + other - 2 * core * other)
            column = x + dx - 2 * x * dx
            for j in range(count):
                block = start + j
                apart, b = block // 2, block % 2
                if apart == 0:
                    b = column if block == 0 else 1 - column
                row = pl.multiple_of(b * 256 + row_part * 64, 64)
                high, low = halves(piece[j])
                where = (pl.ds(row, 64), pl.ds(pl.multiple_of(column * 256, 256), 256))
                out_ref[(apart, 0) + where] = high
                out_ref[(apart, 1) + where] = low


PIECES = ((0, 0, 0, 8), (0, 1, 0, 8), (1, 0, 0, 8), (1, 1, 0, 4), (1, 1, 4, 4))


def apply(value, weight_ref, apart, rows, columns):
    high, low = halves(value)
    both = jnp.concatenate([high, low], axis=0)
    first = dot_rows(both, weight_ref[apart, 0, rows, columns])
    count = value.shape[0]
    return first[:count] + first[count:] + dot_rows(high, weight_ref[apart, 1, rows, columns])


def solve(residual, weight_ref):
    top, bottom = slice(0, 256), slice(256, 512)
    solved_top = apply(residual[:, :256], weight_ref, 0, top, top)
    rest = residual[:, 256:] - apply(solved_top, weight_ref, 0, bottom, top)
    return jnp.concatenate([solved_top, apply(rest, weight_ref, 0, bottom, bottom)], axis=1)


def push(solved, weight_ref, received, out_ref):
    for apart in range(1, out_ref.shape[0] + 1):
        term = apply(solved, weight_ref, apart, slice(0, SUPER), slice(0, SUPER))
        out_ref[apart - 1] = term if received is None else received[apart] + term


def chain_first(parts_ref, weight_ref, residual_ref, out_ref):
    by_rows = []
    for row_part in range(4):
        terms = [parts_ref[z, row_part, x] for z in range(PLANES) for x in range(2)]
        while len(terms) > 1:
            terms = [terms[i] + terms[i + 1] for i in range(0, len(terms), 2)]
        by_rows.append(terms[0])
    residual = jnp.concatenate([t[:, :64] for t in by_rows] + [t[:, 64:] for t in by_rows], axis=1)
    residual_ref[...] = residual
    push(solve(residual, weight_ref), weight_ref, None, out_ref)


def chain_middle(residual_ref, received_ref, weight_ref, next_ref, out_ref):
    residual = residual_ref[...] - received_ref[0]
    next_ref[...] = residual
    push(solve(residual, weight_ref), weight_ref, received_ref, out_ref)


def chain_last(residual_ref, received_ref, weight_ref, out_ref):
    solved = solve(residual_ref[...] - received_ref[0], weight_ref)
    for row_part in range(4):
        start = row_part * 64
        chunk = jnp.concatenate([solved[:, start : start + 64], solved[:, start + 256 : start + 320]], axis=1)
        for z in range(PLANES):
            for x in range(2):
                out_ref[z, row_part, x] = chunk


def turn(parts_ref, out_ref):
    for part in range(PLANES):
        out_ref[part] = parts_ref[part].T


def whole(*shape):
    return pl.BlockSpec(shape, lambda _: (0,) * len(shape))


def call(kernel, name, outs, *args, weights=None):
    specs = [whole(*a.shape) for a in args]
    if weights is not None:
        array, count = weights
        args += (array,)
        specs.append(whole(count, *array.shape[1:]))
    return pl.pallas_call(
        kernel,
        out_shape=[jax.ShapeDtypeStruct(s, F32) for s in outs],
        grid=(1,),
        in_specs=specs,
        out_specs=[whole(*s) for s in outs],
        compiler_params=pltpu.CompilerParams(vmem_limit_bytes=VMEM_LIMIT),
        name=name,
    )(*args)


def local(right_side, lower_prev, solved_prev, lower_window, inverse_diag):
    blocks, local_rows, columns = right_side.shape
    depth = lower_prev.shape[2]
    y, core, z, x = (lax.axis_index(a) for a in ("y", "core", "z", "x"))
    tile = next(t for t in (2304, 2016, 1792, 1152, 1024, 768, 512, 256, 128) if depth % t == 0)

    swap = functools.partial(lax.ppermute, perm=SWAP)
    own_inverse = lax.dynamic_slice_in_dim(inverse_diag, 2 * z + x, 1, 0)
    twice = jnp.concatenate([lower_window, lower_window], axis=0)
    message = jnp.concatenate([own_inverse, lax.dynamic_slice_in_dim(twice, 2 * z + 1, 7, 0)], axis=0)

    from_x = swap(message, "x")
    from_y = swap(message, "y")
    from_core = swap(message, "core")

    factor = lower_prev.reshape(blocks * local_rows, depth)
    right = right_side.reshape(blocks * local_rows, columns)
    first = (2 * z + x).astype(jnp.int32).reshape(1)
    total, finish = earlier_sums(first, factor, solved_prev, right, tile, (depth // tile + 1) // 2)

    total, from_x, from_y = lax.optimization_barrier((total, from_x, from_y))
    corner_low = swap(from_x[:4], "y")
    corner_high = swap(from_y[4:], "x")
    core_x, core_y = swap(from_x, "core"), swap(from_y, "core")
    parts = finish(total)

    parts, corner_low, corner_high = lax.optimization_barrier((parts, corner_low, corner_high))
    core_low, core_high = swap(corner_low, "core"), swap(corner_high, "core")
    parts = lax.all_to_all(parts.reshape(32, RHS_PART, 128), EVERY, 0, 0, tiled=True)

    pieces = (message, from_core, from_x, core_x, from_y, core_y, corner_low, core_low, corner_high, core_high)
    place = jnp.stack([y, core, x]).astype(jnp.int32)
    weights = pl.pallas_call(
        arrange,
        out_shape=jax.ShapeDtypeStruct((4, 2, SUPER, SUPER), BF16),
        grid=(1,),
        in_specs=[pl.BlockSpec(memory_space=pltpu.SMEM)] + [whole(*p.shape) for p in pieces],
        out_specs=whole(4, 2, SUPER, SUPER),
        compiler_params=pltpu.CompilerParams(vmem_limit_bytes=VMEM_LIMIT),
        name="arrange",
    )(place, *pieces)

    vector = (RHS_PART, SUPER)
    residual, sent = call(
        chain_first, "chain_first", [vector, (3, *vector)], parts.reshape(4, 4, 2, RHS_PART, 128), weights=(weights, 4)
    )
    for step in (1, 2):
        received = lax.ppermute(sent, "z", [(step - 1, step)])
        residual, sent = call(
            chain_middle, "chain_middle", [vector, (3 - step, *vector)], residual, received, weights=(weights, 4 - step)
        )
    received = lax.ppermute(sent, "z", [(2, 3)])
    (chunks,) = call(
        chain_last, "chain_last", [(4, 4, 2, RHS_PART, 128)], residual, received, weights=(weights, 1)
    )
    solved = lax.all_to_all(chunks.reshape(32, RHS_PART, 128), EVERY, 0, 0, tiled=True)
    (result,) = call(turn, "turn", [(PLANES, 128, columns)], solved.reshape(PLANES, columns, 128))
    return result.reshape(blocks, local_rows, columns)


def local_any(right_side, lower_prev, solved_prev, lower_window, inverse_diag):
    highest = lax.Precision.HIGHEST
    blocks, local_rows, columns = right_side.shape
    block_rows = inverse_diag.shape[2]
    row_start = lax.axis_index("prow") * local_rows
    solved = jnp.zeros((blocks * block_rows, columns), F32)
    pieces = []
    full_inverse = lax.all_gather(inverse_diag, "prow", axis=1, tiled=True)
    full_window = lax.all_gather(lower_window, "pcol", axis=2, tiled=True)
    dot = functools.partial(jnp.dot, precision=highest, preferred_element_type=F32)
    for row_block in range(blocks):
        window_term = dot(full_window[row_block], solved)
        earlier_here = lax.psum(dot(lower_prev[row_block], solved_prev), "pcol")
        local_residual = right_side[row_block] - (earlier_here + window_term)
        residual = lax.all_gather(local_residual, "prow", axis=0, tiled=True)
        whole_rows = dot(full_inverse[row_block], residual)
        pieces.append(lax.dynamic_slice_in_dim(whole_rows, row_start, local_rows, 0))
        solved = lax.dynamic_update_slice_in_dim(solved, whole_rows, row_block * block_rows, 0)
    return jnp.stack(pieces)


def run(mesh, body, row, column):
    in_specs = (P(None, row, None), P(None, row, column), P(column, None), P(None, row, column), P(None, row, None))
    return jax.shard_map(body, mesh=mesh, in_specs=in_specs, out_specs=P(None, row, None), check_vma=False)


def solution(mesh):
    if (mesh.shape["prow"], mesh.shape["pcol"]) == (4, 8):
        fine = Mesh(mesh.devices.reshape(2, 2, 4, 2), ("y", "core", "z", "x"))
        return run(fine, local, ("y", "core"), ("z", "x"))
    return run(mesh, local_any, "prow", "pcol")
```

time: 253 us -> 95.1 us (0.38); the launches traced: 249 us -> 94.6 us
  waiting for transfers between devices: 104 us -> 8.53 us
  matrix products: 84.1 us -> 0 us
  Pallas kernels: 0 us -> 40.2 us
  blocking collectives: 43.7 us -> 22.4 us
  starting transfers between devices: 0.08 us -> 15.7 us
  between operations: 13.5 us -> 0.16 us
  local copies, waits for them, and re-layouts: 1.71 us -> 5.87 us
    dot_general x23 -> x0, matrix products: 84.1 us -> none  [the longest x8 67.3 us: local(): jnp.dot(lower_prev[row_block], solved_prev, precision=highest, preferred_...]
    psum x1 -> x0, waiting for transfers between devices: 73.8 us -> none  [local(): earlier_here = lax.psum(earlier_part, 'pcol')]
    all_gather x8 -> x0, blocking collectives: 43.7 us -> none  [local(): residual = lax.all_gather(local_residual, 'prow', axis=0, tiled=True)]
    pallas_call x0 -> x8, Pallas kernels: none -> 40.2 us  [the longest x5 15.5 us: call(): pl.pallas_call(kernel, out_shape=[jax.ShapeDtypeStruct(s, F32) for s in o...]
    all_gather x2 -> x0, waiting for transfers between devices: 29.1 us -> none  [the longest x1 17.4 us: local(): full_inverse = lax.all_gather(inverse_diag, 'prow', axis=1, tiled=True)]
    all_to_all x0 -> x1, blocking collectives: none -> 22.4 us  [local(): lax.all_to_all(chunks.reshape(32, RHS_PART, 128), EVERY, 0, 0, tiled=True)]
    ppermute x0 -> x12, starting transfers between devices: none -> 10.7 us  [the longest x1 3.03 us: local(): from_y = swap(message, 'y')]
    ppermute x0 -> x12, waiting for transfers between devices: none -> 5.55 us  [the longest x2 3.44 us: local(): received = lax.ppermute(sent, 'z', [(step - 1, step)])]
  transfers between devices with their start and end apart: 3 -> 13, of which waited for: 3 -> 5; matrix products, arithmetic and copies ran while one was open for 28% -> 1% of each run, Pallas kernels for 0% -> 26%
where the time goes in v1:
time: 95.1 us; the launch traced here: 94.6 us
  Pallas kernels  40.2 us (42%)
  blocking collectives  22.4 us (24%)
  starting transfers between devices  15.7 us (17%)
  waiting for transfers between devices  8.53 us (9%)
  local copies, waits for them, and re-layouts  5.87 us (6%)
  other arithmetic  1.73 us (2%)
    all_to_all x1, blocking collectives, local(): lax.all_to_all(chunks.reshape(32, RHS_PART, 128), EVERY, 0, 0, tiled=True)  22.4 us
    pallas_call x5, Pallas kernels, call(): pl.pallas_call(kernel, out_shape=[jax.ShapeDtypeStruct(s, F32) for s in o...  15.5 us
    pallas_call x1, Pallas kernels, earlier_sums(): pl.pallas_call(earlier_first, out_shape=jax.ShapeDtypeStruct((rows, 2 * c...  10.9 us
    pallas_call x1, Pallas kernels, finish(): pl.pallas_call(earlier_last, out_shape=jax.ShapeDtypeStruct((PLANES, colu...  9.24 us
    unnamed x24, local copies, waits for them, and re-layouts  5.83 us
    all_to_all x1, starting transfers between devices, local(): lax.all_to_all(parts.reshape(32, RHS_PART, 128), EVERY, 0, 0, tiled=True)  4.94 us
    pallas_call x1, Pallas kernels, local(): pl.pallas_call(arrange, out_shape=jax.ShapeDtypeStruct((4, 2, SUPER, SUPE...  4.59 us
    ppermute x2, waiting for transfers between devices, local(): received = lax.ppermute(sent, 'z', [(step - 1, step)])  3.44 us
  transfers between devices with their start and end apart: 13, of which 5 were waited for; matrix products, arithmetic and copies ran while one was open for 1% of the time, Pallas kernels for 26%

profile of v1, /device:TPU:0, one launch (start us, length us, event | category | flops | bytes accessed | tf_op | source)
XLA Modules:
  0.0 94.6 jit_solution(16608205372760140132)
XLA Ops:
  0.0 0.0 copy-start
  0.0 1.0 %copy-done = f32[8,64,256]{2,1,0:T(8,128)S(1)} copy-done((f32[8,64,256]{2,1,0:T(8,128)S(1)}, f32[8,64,256]{2,1,0:T(8,128)}, u32[]{:S(2)}) %copy-start) | copy-done | bytes 524312
  1.0 1.1 %fusion = f32[7,64,256]{2,1,0:T(8,128)S(1)} fusion(s32[]{:T(128)S(6)} %select_n.7, f32[8,64,256]{2,1,0:T(8,128)} %param.8), kind=kLoop, calls=%fused_computation.3 | loop fusion | flops 114688 | bytes 983044 | tf_op jit(solution)/shard_map/concatenate | solution.py:222
  2.2 0.0 copy-start.1
  2.2 3.0 %collective-permute-start.1 = (f32[8,64,256]{2,1,0:T(8,128)S(1)}, f32[8,64,256]{2,1,0:T(8,128)S(1)}, u32[]{:S(2)}, u32[]{:S(2)}) collective-permute-start(f32[8,64,256]{2,1,0:T(8,128)S(1)} %pad_maximum_fusion.refs_0_), channel_id=1, source_target_pairs={{0,16},{16,0},{1,17},{17,1},{2,18},{18,2},{3,19},{19,3},{4,20},{20... | collective-permute-start | bytes 1572872 | tf_op jit(solution)/shard_map/ppermute | solution.py:226
  5.2 1.5 %collective-permute-start = (f32[8,64,256]{2,1,0:T(8,128)S(1)}, f32[8,64,256]{2,1,0:T(8,128)S(1)}, u32[]{:S(2)}, u32[]{:S(2)}) collective-permute-start(f32[8,64,256]{2,1,0:T(8,128)S(1)} %pad_maximum_fusion.refs_0_), channel_id=1, source_target_pairs={{0,1},{1,0},{2,3},{3,2},{4,5},{5,4},{6,7},{7,6},{8,9},{9,8},{10,11... | collective-permute-start | bytes 1572872 | tf_op jit(solution)/shard_map/ppermute | solution.py:225
  6.7 0.0 collective-permute-start.4
  6.7 10.9 %earlier_first.1.total_in = f32[512,256]{1,0:T(8,128)} custom-call(f32[512,16128]{1,0:T(8,128)} %bitcast.11, f32[16128,128]{1,0:T(8,128)} %solved_ref.3), custom_call_target="tpu_custom_call" | custom-call | flops 4831838208 | bytes 23592960 | tf_op jit(solution)/shard_map/earlier_first/pallas_call | solution.py:80
  17.6 0.0 copy-done.1
  17.6 0.0 collective-permute-done.1.refs_4_
  17.6 0.0 copy-start.2
  17.6 1.0 %collective-permute-done.refs_2_ = f32[8,64,256]{2,1,0:T(8,128)S(1)} collective-permute-done((f32[8,64,256]{2,1,0:T(8,128)S(1)}, f32[8,64,256]{2,1,0:T(8,128)S(1)}, u32[]{:S(2)}, u32[]{:S(2)}) %collective-permute-start) | collective-permute-done | bytes 524320 | tf_op jit(solution)/shard_map/ppermute | solution.py:225
  18.6 0.0 copy-start.3
  18.6 0.1 collective-permute-start.5
  18.7 0.6 collective-permute-start.6
  19.3 1.5 %collective-permute-start.3 = (f32[4,64,256]{2,1,0:T(8,128)S(1)}, f32[4,64,256]{2,1,0:T(8,128)S(1)}, u32[]{:S(2)}, u32[]{:S(2)}) collective-permute-start(f32[4,64,256]{2,1,0:T(8,128)S(1)} %slice.7), channel_id=1, source_target_pairs={{0,1},{1,0},{2,3},{3,2},{4,5},{5,4},{6,7},{7,6},{8,9},{9,8},{10,11... | collective-permute-start | bytes 786440 | tf_op jit(solution)/shard_map/ppermute | solution.py:236
  20.8 0.5 collective-permute-start.2
  21.3 9.2 %earlier_last.1 = f32[4,128,128]{2,1,0:T(8,128)} custom-call(s32[1]{0:T(128)} %bitcast.first_ref, f32[512,16128]{1,0:T(8,128)} %bitcast.12, f32[16128,128]{1,0:T(8,128)} %solved_ref.3, f32[512,256]{1,0:T(8,128)} %earlier_first.1.total_in, f32[512,128]{1,0:T(8,128)} %bitcast.17), custom_call_target="tpu_custom_call" | custom-call | flops 3623878656 | bytes 17694720 | tf_op jit(solution)/shard_map/earlier_last/pallas_call | solution.py:95
  30.5 0.0 copy-done.2
  30.5 0.0 copy-done.3
  30.5 0.0 collective-permute-done.3.refs_8_
  30.6 0.0 copy-start.7
  30.6 0.7 copy-done.7
  31.3 0.0 collective-permute-done.2.refs_6_
  31.3 0.0 copy-start.8
  31.3 0.7 copy-done.8
  32.0 4.9 %all-to-all-start = ((f32[32,16,128]{2,1,0:T(8,128)}), f32[32,16,128]{2,1,0:T(8,128)S(1)}, u32[]{:S(2)}, u32[]{:S(2)}) async-start(f32[32,16,128]{2,1,0:T(8,128)} %bitcast.13), calls=%async_computation | async-start | bytes 524288 | tf_op jit(solution)/shard_map/all_to_all | solution.py:242
  36.9 0.3 collective-permute-start.7
  37.2 0.3 collective-permute-start.8
  37.5 0.6 pad_add_fusion.place_ref
  38.1 0.0 collective-permute-done.4.refs_1_
  38.1 0.0 copy-start.5
  38.1 0.7 collective-permute-done.7.refs_7_
  38.9 0.4 collective-permute-done.8.refs_9_
  39.2 0.0 collective-permute-done.5.refs_3_
  39.3 0.0 copy-start.6
  39.3 0.0 collective-permute-done.6.refs_5_
  39.3 0.0 copy-done.5
  39.3 0.8 copy-done.6
  40.1 4.6 %arrange.1.weight_ref = bf16[4,2,512,512]{3,2,1,0:T(8,128)(2,1)} custom-call(s32[3]{0:T(128)} %pad_add_fusion.place_ref, f32[8,64,256]{2,1,0:T(8,128)} %copy-done.1, f32[8,64,256]{2,1,0:T(8,128)} %copy-done.5, f32[8,64,256]{2,1,0:T(8,128)} %copy-done.3, f32[8,64,256]{2,1,0:T(8,128)} %copy-done.6, f32[8,64,256]{2,1,0:T(8,128)} %copy-done.2, ...), custom_call_target="tpu_custom_call" | custom-call | tf_op jit(solution)/shard_map/arrange/pallas_call | solution.py:246
  44.6 3.0 %all-to-all-done = f32[32,16,128]{2,1,0:T(8,128)S(1)} async-done(((f32[32,16,128]{2,1,0:T(8,128)}), f32[32,16,128]{2,1,0:T(8,128)S(1)}, u32[]{:S(2)}, u32[]{:S(2)}) %all-to-all-start) | async-done | bytes 262176 | tf_op jit(solution)/shard_map/all_to_all | solution.py:242
  47.6 0.0 copy-start.4
  47.6 0.7 copy-done.4
  48.3 4.3 %chain_first.1 = (f32[16,512]{1,0:T(8,128)}, f32[3,16,512]{2,1,0:T(8,128)}) custom-call(f32[4,4,2,16,128]{4,3,2,1,0:T(8,128)} %bitcast.14, bf16[4,2,512,512]{3,2,1,0:T(8,128)(2,1)} %arrange.1.weight_ref), custom_call_target="tpu_custom_call" | custom-call | tf_op jit(solution)/shard_map/chain_first/pallas_call | solution.py:203
  52.6 1.7 %collective-permute-start.9 = (f32[3,16,512]{2,1,0:T(8,128)}, f32[3,16,512]{2,1,0:T(8,128)S(1)}, u32[]{:S(2)}, u32[]{:S(2)}) collective-permute-start(f32[3,16,512]{2,1,0:T(8,128)} %get-tuple-element.24), channel_id=1, source_target_pairs={{0,2},{1,3},{8,10},{9,11},{16,18},{17,19},{24,26},{25,27}} | collective-permute-start | bytes 294920 | tf_op jit(solution)/shard_map/ppermute | solution.py:261
  54.4 3.4 %collective-permute-done.9.received_ref = f32[3,16,512]{2,1,0:T(8,128)S(1)} collective-permute-done((f32[3,16,512]{2,1,0:T(8,128)}, f32[3,16,512]{2,1,0:T(8,128)S(1)}, u32[]{:S(2)}, u32[]{:S(2)}) %collective-permute-start.9) | collective-permute-done | bytes 98336 | tf_op jit(solution)/shard_map/ppermute | solution.py:261
  57.8 0.0 copy-start.9
  57.8 0.6 copy-done.9
  58.4 3.7 %chain_middle.2 = (f32[16,512]{1,0:T(8,128)}, f32[2,16,512]{2,1,0:T(8,128)}) custom-call(f32[16,512]{1,0:T(8,128)} %get-tuple-element.23.residual_ref, f32[3,16,512]{2,1,0:T(8,128)} %copy-done.9, bf16[4,2,512,512]{3,2,1,0:T(8,128)(2,1)} %arrange.1.weight_ref), custom_call_target="tpu_custom_call" | custom-call | tf_op jit(solution)/shard_map/chain_middle/pallas_call | solution.py:203
  62.1 0.7 collective-permute-start.10
  62.8 0.0 collective-permute-done.10.received_ref
  62.8 0.0 copy-start.10
  62.8 0.6 copy-done.10
  63.4 3.1 %chain_middle.3 = (f32[16,512]{1,0:T(8,128)}, f32[1,16,512]{2,1,0:T(8,128)}) custom-call(f32[16,512]{1,0:T(8,128)} %get-tuple-element.25.residual_ref, f32[2,16,512]{2,1,0:T(8,128)} %copy-done.10, bf16[4,2,512,512]{3,2,1,0:T(8,128)(2,1)} %arrange.1.weight_ref), custom_call_target="tpu_custom_call" | custom-call | tf_op jit(solution)/shard_map/chain_middle/pallas_call | solution.py:203
  66.5 0.7 collective-permute-start.11
  67.2 0.0 collective-permute-done.11.received_ref
  67.2 0.0 copy-start.11
  67.2 0.6 copy-done.11
  67.8 2.6 %chain_last.1 = f32[4,4,2,16,128]{4,3,2,1,0:T(8,128)} custom-call(f32[16,512]{1,0:T(8,128)} %get-tuple-element.27.residual_ref, f32[1,16,512]{2,1,0:T(8,128)} %copy-done.11, bf16[4,2,512,512]{3,2,1,0:T(8,128)(2,1)} %arrange.1.weight_ref), custom_call_target="tpu_custom_call" | custom-call | tf_op jit(solution)/shard_map/chain_last/pallas_call | solution.py:203
  70.4 22.4 %all_to_all.10 = f32[32,16,128]{2,1,0:T(8,128)} all-to-all(f32[32,16,128]{2,1,0:T(8,128)} %bitcast.15), channel_id=1, replica_groups=mesh['y'=2,'core'=2,'z'=4,'x'=2] {'z','y','core','x'}, dimensions={0} | all-to-all | bytes 524288 | tf_op jit(solution)/shard_map/all_to_all | solution.py:269
  92.8 1.8 %turn.1 = f32[4,128,128]{2,1,0:T(8,128)} custom-call(f32[4,128,128]{2,1,0:T(8,128)} %bitcast.16), custom_call_target="tpu_custom_call" | custom-call | tf_op jit(solution)/shard_map/turn/pallas_call | solution.py:203
  (4 shorter events, 0.1 us)
Async XLA Ops:
  0.0 1.0 %copy-start = (f32[8,64,256]{2,1,0:T(8,128)S(1)}, f32[8,64,256]{2,1,0:T(8,128)}, u32[]{:S(2)}) copy-start(f32[8,64,256]{2,1,0:T(8,128)} %param.9) | copy-start | bytes 1572868
  2.2 15.4 %copy-start.1 = (f32[8,64,256]{2,1,0:T(8,128)}, f32[8,64,256]{2,1,0:T(8,128)S(1)}, u32[]{:S(2)}) copy-start(f32[8,64,256]{2,1,0:T(8,128)S(1)} %pad_maximum_fusion.refs_0_) | copy-start | bytes 1572868
  2.2 15.4 %collective-permute-start.1 = (f32[8,64,256]{2,1,0:T(8,128)S(1)}, f32[8,64,256]{2,1,0:T(8,128)S(1)}, u32[]{:S(2)}, u32[]{:S(2)}) collective-permute-start(f32[8,64,256]{2,1,0:T(8,128)S(1)} %pad_maximum_fusion.refs_0_), channel_id=1, source_target_pairs={{0,16},{16,0},{1,17},{17,1},{2,18},{18,2},{3,19},{19,3},{4,20},{20... | collective-permute-start | bytes 1572872 | tf_op jit(solution)/shard_map/ppermute | solution.py:226
  5.2 13.4 %collective-permute-start = (f32[8,64,256]{2,1,0:T(8,128)S(1)}, f32[8,64,256]{2,1,0:T(8,128)S(1)}, u32[]{:S(2)}, u32[]{:S(2)}) collective-permute-start(f32[8,64,256]{2,1,0:T(8,128)S(1)} %pad_maximum_fusion.refs_0_), channel_id=1, source_target_pairs={{0,1},{1,0},{2,3},{3,2},{4,5},{5,4},{6,7},{7,6},{8,9},{9,8},{10,11... | collective-permute-start | bytes 1572872 | tf_op jit(solution)/shard_map/ppermute | solution.py:225
  6.7 31.4 %collective-permute-start.4 = (f32[8,64,256]{2,1,0:T(8,128)S(1)}, f32[8,64,256]{2,1,0:T(8,128)S(1)}, u32[]{:S(2)}, u32[]{:S(2)}) collective-permute-start(f32[8,64,256]{2,1,0:T(8,128)S(1)} %pad_maximum_fusion.refs_0_), channel_id=1, source_target_pairs={{0,8},{8,0},{1,9},{9,1},{2,10},{10,2},{3,11},{11,3},{4,12},{12,4},... | collective-permute-start | bytes 1572872 | tf_op jit(solution)/shard_map/ppermute | solution.py:227
  17.6 12.9 %copy-start.2 = (f32[8,64,256]{2,1,0:T(8,128)}, f32[8,64,256]{2,1,0:T(8,128)S(1)}, u32[]{:S(2)}) copy-start(f32[8,64,256]{2,1,0:T(8,128)S(1)} %collective-permute-done.1.refs_4_) | copy-start | bytes 1572868
  18.6 11.9 %copy-start.3 = (f32[8,64,256]{2,1,0:T(8,128)}, f32[8,64,256]{2,1,0:T(8,128)S(1)}, u32[]{:S(2)}) copy-start(f32[8,64,256]{2,1,0:T(8,128)S(1)} %collective-permute-done.refs_2_) | copy-start | bytes 1572868
  18.6 20.6 %collective-permute-start.5 = (f32[8,64,256]{2,1,0:T(8,128)S(1)}, f32[8,64,256]{2,1,0:T(8,128)S(1)}, u32[]{:S(2)}, u32[]{:S(2)}) collective-permute-start(f32[8,64,256]{2,1,0:T(8,128)S(1)} %collective-permute-done.refs_2_), channel_id=1, source_target_pairs={{0,8},{8,0},{1,9},{9,1},{2,10},{10,2},{3,11},{11,3},{4,12},{12,4},... | collective-permute-start | bytes 1572872 | tf_op jit(solution)/shard_map/ppermute | solution.py:237
  18.7 20.5 %collective-permute-start.6 = (f32[8,64,256]{2,1,0:T(8,128)S(1)}, f32[8,64,256]{2,1,0:T(8,128)}, u32[]{:S(2)}, u32[]{:S(2)}) collective-permute-start(f32[8,64,256]{2,1,0:T(8,128)S(1)} %collective-permute-done.1.refs_4_), channel_id=1, source_target_pairs={{0,8},{8,0},{1,9},{9,1},{2,10},{10,2},{3,11},{11,3},{4,12},{12,4},... | collective-permute-start | bytes 1572872 | tf_op jit(solution)/shard_map/ppermute | solution.py:237
  19.3 11.3 %collective-permute-start.3 = (f32[4,64,256]{2,1,0:T(8,128)S(1)}, f32[4,64,256]{2,1,0:T(8,128)S(1)}, u32[]{:S(2)}, u32[]{:S(2)}) collective-permute-start(f32[4,64,256]{2,1,0:T(8,128)S(1)} %slice.7), channel_id=1, source_target_pairs={{0,1},{1,0},{2,3},{3,2},{4,5},{5,4},{6,7},{7,6},{8,9},{9,8},{10,11... | collective-permute-start | bytes 786440 | tf_op jit(solution)/shard_map/ppermute | solution.py:236
  20.8 10.5 %collective-permute-start.2 = (f32[4,64,256]{2,1,0:T(8,128)S(1)}, f32[4,64,256]{2,1,0:T(8,128)S(1)}, u32[]{:S(2)}, u32[]{:S(2)}) collective-permute-start(f32[4,64,256]{2,1,0:T(8,128)S(1)} %slice.6), channel_id=1, source_target_pairs={{0,16},{16,0},{1,17},{17,1},{2,18},{18,2},{3,19},{19,3},{4,20},{20... | collective-permute-start | bytes 786440 | tf_op jit(solution)/shard_map/ppermute | solution.py:235
  30.6 0.7 copy-start.7
  31.3 0.7 copy-start.8
  32.0 15.6 %all-to-all-start = ((f32[32,16,128]{2,1,0:T(8,128)}), f32[32,16,128]{2,1,0:T(8,128)S(1)}, u32[]{:S(2)}, u32[]{:S(2)}) async-start(f32[32,16,128]{2,1,0:T(8,128)} %bitcast.13), calls=%async_computation | async-start | bytes 524288 | tf_op jit(solution)/shard_map/all_to_all | solution.py:242
  36.9 1.9 %collective-permute-start.7 = (f32[4,64,256]{2,1,0:T(8,128)}, f32[4,64,256]{2,1,0:T(8,128)}, u32[]{:S(2)}, u32[]{:S(2)}) collective-permute-start(f32[4,64,256]{2,1,0:T(8,128)} %copy-done.8), channel_id=1, source_target_pairs={{0,8},{8,0},{1,9},{9,1},{2,10},{10,2},{3,11},{11,3},{4,12},{12,4},... | collective-permute-start | bytes 786440 | tf_op jit(solution)/shard_map/ppermute | solution.py:241
  37.2 2.0 %collective-permute-start.8 = (f32[4,64,256]{2,1,0:T(8,128)}, f32[4,64,256]{2,1,0:T(8,128)}, u32[]{:S(2)}, u32[]{:S(2)}) collective-permute-start(f32[4,64,256]{2,1,0:T(8,128)} %copy-done.7), channel_id=1, source_target_pairs={{0,8},{8,0},{1,9},{9,1},{2,10},{10,2},{3,11},{11,3},{4,12},{12,4},... | collective-permute-start | bytes 786440 | tf_op jit(solution)/shard_map/ppermute | solution.py:241
  38.1 1.1 %copy-start.5 = (f32[8,64,256]{2,1,0:T(8,128)}, f32[8,64,256]{2,1,0:T(8,128)S(1)}, u32[]{:S(2)}) copy-start(f32[8,64,256]{2,1,0:T(8,128)S(1)} %collective-permute-done.4.refs_1_) | copy-start | bytes 1572868
  39.3 0.8 copy-start.6
  47.6 0.7 copy-start.4
  52.6 5.1 %collective-permute-start.9 = (f32[3,16,512]{2,1,0:T(8,128)}, f32[3,16,512]{2,1,0:T(8,128)S(1)}, u32[]{:S(2)}, u32[]{:S(2)}) collective-permute-start(f32[3,16,512]{2,1,0:T(8,128)} %get-tuple-element.24), channel_id=1, source_target_pairs={{0,2},{1,3},{8,10},{9,11},{16,18},{17,19},{24,26},{25,27}} | collective-permute-start | bytes 294920 | tf_op jit(solution)/shard_map/ppermute | solution.py:261
  57.8 0.6 copy-start.9
  62.1 0.7 collective-permute-start.10
  62.8 0.6 copy-start.10
  66.5 0.7 collective-permute-start.11
  67.2 0.6 copy-start.11

commit v2 on v0

v2 whole, which is shorter than its diff:
```python
import functools

import jax
import jax.numpy as jnp
from jax import lax
from jax.experimental import pallas as pl
from jax.experimental.pallas import tpu as pltpu
from jax.sharding import Mesh, PartitionSpec as P

F32 = jnp.float32
BF16 = jnp.bfloat16
EVERY = ("z", "y", "core", "x")
SWAP = [(0, 1), (1, 0)]
PLANES = 4
RHS_PART = 16
SUPER = 512


def halves(value):
    high = value.astype(BF16)
    low = (value - high.astype(F32)).astype(BF16)
    return high, low


def dot_f32(a, b):
    return jnp.dot(a, b, preferred_element_type=F32)


def dot_rows(a, b):
    return lax.dot_general(a, b, (((1,), (1,)), ((), ())), preferred_element_type=F32)


def earlier_sums(first_ref, factor_ref, solved_ref, right_ref, out_ref, total):
    step = pl.program_id(0)

    @pl.when(step == 0)
    def _():
        total[...] = jnp.zeros_like(total)

    factor_high, factor_low = halves(factor_ref[...])
    solved_both = jnp.concatenate(halves(solved_ref[...]), axis=1)
    total[...] += dot_f32(factor_high, solved_both) + dot_f32(factor_low, solved_both)

    @pl.when(step == pl.num_programs(0) - 1)
    def _():
        keep = first_ref[0] == 0
        width = right_ref.shape[1]
        for part in range(PLANES):
            rows = slice(part * 128, part * 128 + 128)
            earlier = total[rows, :width] + total[rows, width:]
            right = jnp.where(keep, right_ref[rows, :], 0.0)
            out_ref[part] = (right - earlier).T


def earlier_residual(first, factor, solved, right):
    rows, depth = factor.shape
    columns = solved.shape[1]
    tile = next(t for t in (2304, 2016, 1792, 1152, 1024, 768, 512, 256, 128) if depth % t == 0)
    return pl.pallas_call(
        earlier_sums,
        out_shape=jax.ShapeDtypeStruct((PLANES, columns, 128), F32),
        grid=(depth // tile,),
        in_specs=[
            pl.BlockSpec(memory_space=pltpu.SMEM),
            pl.BlockSpec((rows, tile), lambda k: (0, k)),
            pl.BlockSpec((tile, columns), lambda k: (k, 0)),
            pl.BlockSpec((rows, columns), lambda k: (0, 0)),
        ],
        out_specs=pl.BlockSpec((PLANES, columns, 128), lambda k: (0, 0, 0)),
        scratch_shapes=[pltpu.VMEM((rows, 2 * columns), F32)],
        compiler_params=pltpu.CompilerParams(vmem_limit_bytes=24 << 20),
        cost_estimate=pl.CostEstimate(
            flops=8 * rows * columns * depth, bytes_accessed=4 * (rows + columns) * depth, transcendentals=0
        ),
        name="earlier",
    )(first, factor, solved, right)


def pack(window_ref, inverse_ref, out_ref, held, sems):
    z, x = lax.axis_index("z"), lax.axis_index("x")
    copies = []
    for j in range(8):
        source = inverse_ref.at[2 * z + x] if j == 0 else window_ref.at[lax.rem(2 * z + j, 8)]
        first = pltpu.make_async_copy(source, held.at[j], sems.at[0, j])
        copies.append((first, pltpu.make_async_copy(held.at[j], out_ref.at[j], sems.at[1, j])))
        first.start()
    for first, second in copies:
        first.wait()
        second.start()
    for first, second in copies:
        second.wait()


def place_piece(piece, y, core, x, other, dy, dx, start, outs):
    row_part = 2 * (y + dy - 2 * y * dy) + (core + other - 2 * core * other)
    column = x + dx - 2 * x * dx
    for j in range(piece.shape[0]):
        apart, b = (start + j) // 2, (start + j) % 2
        if apart == 0:
            b = column if b == 0 else 1 - column
        row = pl.multiple_of(b * 256 + row_part * 64, 64)
        where = (pl.ds(row, 64), pl.ds(pl.multiple_of(column * 256, 256), 256))
        for part, value in enumerate(halves(piece[j])):
            outs[apart][(part,) + where] = value


def arrange(spots, kept, *refs):
    count = len(spots)
    pieces, (held, sems) = refs[:count], refs[-2:]
    outs = refs[count + kept : -2]
    y, core, x = (lax.axis_index(a) for a in ("y", "core", "x"))
    copies = [pltpu.make_async_copy(pieces[i], held.at[i], sems.at[i]) for i in range(count)]
    for copy in copies:
        copy.start()
    for i, copy in enumerate(copies):
        copy.wait()
        other, dy, dx, start = spots[i]
        place_piece(held.at[i], y, core, x, other, dy, dx, start, outs)


def arranged(name, spots, pieces, weights=()):
    in_vmem = pl.BlockSpec(memory_space=pltpu.VMEM)
    count = len(pieces)
    return pl.pallas_call(
        functools.partial(arrange, spots, len(weights)),
        out_shape=[jax.ShapeDtypeStruct((2, SUPER, SUPER), BF16)] * 4,
        in_specs=[pl.BlockSpec(memory_space=pl.ANY)] * count + [in_vmem] * len(weights),
        out_specs=[in_vmem] * 4,
        scratch_shapes=[pltpu.VMEM((count, *pieces[0].shape), F32), pltpu.SemaphoreType.DMA((count,))],
        input_output_aliases={count + i: i for i in range(len(weights))},
        compiler_params=pltpu.CompilerParams(vmem_limit_bytes=8 << 20),
        name=name,
    )(*pieces, *weights)


def apply(value, weight_ref, rows, columns):
    high, low = halves(value)
    both = jnp.concatenate([high, low], axis=0)
    first = dot_rows(both, weight_ref[0, rows, columns])
    count = value.shape[0]
    return first[:count] + first[count:] + dot_rows(high, weight_ref[1, rows, columns])


def solve(residual, weight_ref):
    top, bottom = slice(0, 256), slice(256, 512)
    solved_top = apply(residual[:, :256], weight_ref, top, top)
    rest = residual[:, 256:] - apply(solved_top, weight_ref, bottom, top)
    return jnp.concatenate([solved_top, apply(rest, weight_ref, bottom, bottom)], axis=1)


def push(solved, weight_refs, received_ref, out_ref):
    for apart, weight_ref in enumerate(weight_refs, 1):
        term = apply(solved, weight_ref, slice(0, SUPER), slice(0, SUPER))
        out_ref[apart - 1] = term if received_ref is None else received_ref[apart] + term


def chain_first(parts_ref, *refs):
    weight_refs, (residual_ref, out_ref) = refs[:-2], refs[-2:]
    by_rows = []
    for row_part in range(4):
        terms = [parts_ref[z, row_part, x] for z in range(PLANES) for x in range(2)]
        while len(terms) > 1:
            terms = [terms[i] + terms[i + 1] for i in range(0, len(terms), 2)]
        by_rows.append(terms[0])
    residual = jnp.concatenate([t[:, :64] for t in by_rows] + [t[:, 64:] for t in by_rows], axis=1)
    residual_ref[...] = residual
    push(solve(residual, weight_refs[0]), weight_refs[1:], None, out_ref)


def chain_middle(residual_ref, received_ref, *refs):
    weight_refs, (next_ref, out_ref) = refs[:-2], refs[-2:]
    residual = residual_ref[...] - received_ref[0]
    next_ref[...] = residual
    push(solve(residual, weight_refs[0]), weight_refs[1:], received_ref, out_ref)


def chain_last(residual_ref, received_ref, weight_ref, out_ref):
    solved = solve(residual_ref[...] - received_ref[0], weight_ref)
    for row_part in range(4):
        start = row_part * 64
        chunk = jnp.concatenate([solved[:, start : start + 64], solved[:, start + 256 : start + 320]], axis=1)
        for z in range(PLANES):
            for x in range(2):
                out_ref[z, row_part, x] = chunk


def turn(parts_ref, out_ref):
    for part in range(PLANES):
        out_ref[part] = parts_ref[part].T


def call(kernel, name, outs, *args, limit=8 << 20):
    in_vmem = pl.BlockSpec(memory_space=pltpu.VMEM)
    return pl.pallas_call(
        kernel,
        out_shape=[jax.ShapeDtypeStruct(*o) for o in outs],
        in_specs=[in_vmem] * len(args),
        out_specs=[in_vmem] * len(outs),
        compiler_params=pltpu.CompilerParams(vmem_limit_bytes=limit),
        name=name,
    )(*args)


def local(right_side, lower_prev, solved_prev, lower_window, inverse_diag):
    blocks, local_rows, columns = right_side.shape
    depth = lower_prev.shape[2]
    swap = functools.partial(lax.ppermute, perm=SWAP)
    message = pl.pallas_call(
        pack,
        out_shape=jax.ShapeDtypeStruct(lower_window.shape, F32),
        in_specs=[pl.BlockSpec(memory_space=pl.ANY)] * 2,
        out_specs=pl.BlockSpec(memory_space=pl.ANY),
        scratch_shapes=[pltpu.VMEM(lower_window.shape, F32), pltpu.SemaphoreType.DMA((2, 8))],
        compiler_params=pltpu.CompilerParams(vmem_limit_bytes=60 << 20),
        cost_estimate=pl.CostEstimate(flops=0, bytes_accessed=16 << 20, transcendentals=0),
        name="pack",
    )(lower_window, inverse_diag)

    from_x = swap(message, "x")
    from_y = swap(message, "y")
    from_core = swap(message, "core")

    factor = lower_prev.reshape(blocks * local_rows, depth)
    right = right_side.reshape(blocks * local_rows, columns)
    first = (2 * lax.axis_index("z") + lax.axis_index("x")).astype(jnp.int32).reshape(1)
    parts = earlier_residual(first, factor, solved_prev, right)

    parts, from_x, from_y = lax.optimization_barrier((parts, from_x, from_y))
    corner_low = swap(from_x[:4], "y")
    corner_high = swap(from_y[4:], "x")
    core_x, core_y = swap(from_x, "core"), swap(from_y, "core")
    parts = lax.all_to_all(parts.reshape(32, RHS_PART, 128), EVERY, 0, 0, tiled=True)
    core_low, core_high = swap(corner_low, "core"), swap(corner_high, "core")
    pieces = (message, from_x, from_y, from_core, core_x, core_y)
    spots = ((0, 0, 0, 0), (0, 0, 1, 0), (0, 1, 0, 0), (1, 0, 0, 0), (1, 0, 1, 0), (1, 1, 0, 0))
    weights = arranged("arrange", spots, pieces)
    pieces = (corner_low, corner_high, core_low, core_high)
    weights = arranged("arrange_corner", ((0, 1, 1, 0), (0, 1, 1, 4), (1, 1, 1, 0), (1, 1, 1, 4)), pieces, weights)

    def vectors(*counts):
        return ((*counts, RHS_PART, SUPER), F32)

    residual, sent = call(chain_first, "chain_first", [vectors(), vectors(3)], parts.reshape(4, 4, 2, RHS_PART, 128), *weights)
    for step in (1, 2):
        received = lax.ppermute(sent, "z", [(step - 1, step)])
        outs = [vectors(), vectors(3 - step)]
        residual, sent = call(chain_middle, "chain_middle", outs, residual, received, *weights[: 4 - step])
    received = lax.ppermute(sent, "z", [(2, 3)])
    chunk = ((4, 4, 2, RHS_PART, 128), F32)
    (chunks,) = call(chain_last, "chain_last", [chunk], residual, received, weights[0])
    solved = lax.all_to_all(chunks.reshape(32, RHS_PART, 128), EVERY, 0, 0, tiled=True)
    (result,) = call(turn, "turn", [((PLANES, 128, columns), F32)], solved.reshape(PLANES, columns, 128))
    return result.reshape(blocks, local_rows, columns)


def local_any(right_side, lower_prev, solved_prev, lower_window, inverse_diag):
    highest = lax.Precision.HIGHEST
    blocks, local_rows, columns = right_side.shape
    block_rows = inverse_diag.shape[2]
    row_start = lax.axis_index("prow") * local_rows
    solved = jnp.zeros((blocks * block_rows, columns), F32)
    pieces = []
    full_inverse = lax.all_gather(inverse_diag, "prow", axis=1, tiled=True)
    full_window = lax.all_gather(lower_window, "pcol", axis=2, tiled=True)
    dot = functools.partial(jnp.dot, precision=highest, preferred_element_type=F32)
    for row_block in range(blocks):
        window_term = dot(full_window[row_block], solved)
        earlier_here = lax.psum(dot(lower_prev[row_block], solved_prev), "pcol")
        local_residual = right_side[row_block] - (earlier_here + window_term)
        residual = lax.all_gather(local_residual, "prow", axis=0, tiled=True)
        whole_rows = dot(full_inverse[row_block], residual)
        pieces.append(lax.dynamic_slice_in_dim(whole_rows, row_start, local_rows, 0))
        solved = lax.dynamic_update_slice_in_dim(solved, whole_rows, row_block * block_rows, 0)
    return jnp.stack(pieces)


def run(mesh, body, row, column):
    in_specs = (P(None, row, None), P(None, row, column), P(column, None), P(None, row, column), P(None, row, None))
    return jax.shard_map(body, mesh=mesh, in_specs=in_specs, out_specs=P(None, row, None), check_vma=False)


def solution(mesh):
    if (mesh.shape["prow"], mesh.shape["pcol"]) == (4, 8):
        fine = Mesh(mesh.devices.reshape(2, 2, 4, 2), ("y", "core", "z", "x"))
        return run(fine, local, ("y", "core"), ("z", "x"))
    return run(mesh, local_any, "prow", "pcol")
```

time: 253 us -> 84.5 us (0.33); the launches traced: 249 us -> 83.6 us
  waiting for transfers between devices: 104 us -> 4.31 us
  matrix products: 84.1 us -> 0 us
  Pallas kernels: 0 us -> 24.3 us
  blocking collectives: 43.7 us -> 22.5 us
  starting transfers between devices: 0.08 us -> 17.2 us
  local copies, waits for them, and re-layouts: 1.71 us -> 15.2 us
  between operations: 13.5 us -> 0.17 us
    dot_general x23 -> x0, matrix products: 84.1 us -> none  [the longest x8 67.3 us: local(): jnp.dot(lower_prev[row_block], solved_prev, precision=highest, preferred_...]
    psum x1 -> x0, waiting for transfers between devices: 73.8 us -> none  [local(): earlier_here = lax.psum(earlier_part, 'pcol')]
    all_gather x8 -> x0, blocking collectives: 43.7 us -> none  [local(): residual = lax.all_gather(local_residual, 'prow', axis=0, tiled=True)]
    all_gather x2 -> x0, waiting for transfers between devices: 29.1 us -> none  [the longest x1 17.4 us: local(): full_inverse = lax.all_gather(inverse_diag, 'prow', axis=1, tiled=True)]
    pallas_call x0 -> x9, Pallas kernels: none -> 24.3 us  [the longest x1 16 us: earlier_residual(): pl.pallas_call(earlier_sums, out_shape=jax.ShapeDtypeStruct((PLANES, colu...]
    all_to_all x0 -> x1, blocking collectives: none -> 22.5 us  [local(): lax.all_to_all(chunks.reshape(32, RHS_PART, 128), EVERY, 0, 0, tiled=True)]
    unnamed x25 -> x30, local copies, waits for them, and re-layouts: 0.64 us -> 15.1 us
    ppermute x0 -> x12, starting transfers between devices: none -> 10.9 us  [the longest x2 4.18 us: local(): received = lax.ppermute(sent, 'z', [(step - 1, step)])]
  transfers between devices with their start and end apart: 3 -> 13, of which waited for: 3 -> 3; matrix products, arithmetic and copies ran while one was open for 28% -> 0% of each run, Pallas kernels for 0% -> 21%
where the time goes in v2:
time: 84.5 us; the launch traced here: 83.6 us
  Pallas kernels  24.3 us (29%)
  blocking collectives  22.5 us (27%)
  starting transfers between devices  17.2 us (20%)
  local copies, waits for them, and re-layouts  15.2 us (18%)
  waiting for transfers between devices  4.31 us (5%)
    all_to_all x1, blocking collectives, local(): lax.all_to_all(chunks.reshape(32, RHS_PART, 128), EVERY, 0, 0, tiled=True)  22.5 us
    pallas_call x1, Pallas kernels, earlier_residual(): pl.pallas_call(earlier_sums, out_shape=jax.ShapeDtypeStruct((PLANES, colu...  16 us
    unnamed x30, local copies, waits for them, and re-layouts  15.1 us
    all_to_all x1, starting transfers between devices, local(): lax.all_to_all(parts.reshape(32, RHS_PART, 128), EVERY, 0, 0, tiled=True)  6.27 us
    pallas_call x5, Pallas kernels, call(): pl.pallas_call(kernel, out_shape=[jax.ShapeDtypeStruct(*o) for o in outs]...  4.71 us
    ppermute x2, starting transfers between devices, local(): received = lax.ppermute(sent, 'z', [(step - 1, step)])  4.18 us
    ppermute x1, starting transfers between devices, local(): from_y = swap(message, 'y')  2.59 us
    ppermute x2, waiting for transfers between devices, local(): received = lax.ppermute(sent, 'z', [(step - 1, step)])  2.54 us
  transfers between devices with their start and end apart: 13, of which 3 were waited for; matrix products, arithmetic and copies ran while one was open for 0% of the time, Pallas kernels for 21%

profile of v2, /device:TPU:0, one launch (start us, length us, event | category | flops | bytes accessed | tf_op | source)
XLA Modules:
  0.0 83.6 jit_solution(6407785846554446892)
XLA Ops:
  0.0 1.8 %pack.1.refs_0_ = f32[8,64,256]{2,1,0:T(8,128)} custom-call(f32[8,64,256]{2,1,0:T(8,128)} %window_ref.1, f32[8,64,256]{2,1,0:T(8,128)} %inverse_ref.1), custom_call_target="tpu_custom_call" | custom-call | bytes 16777216 | tf_op jit(solution)/shard_map/pack/pallas_call | solution.py:208
  1.8 0.5 collective-permute-start.6
  2.3 2.6 %collective-permute-start.1 = (f32[8,64,256]{2,1,0:T(8,128)}, f32[8,64,256]{2,1,0:T(8,128)S(1)}, u32[]{:S(2)}, u32[]{:S(2)}) collective-permute-start(f32[8,64,256]{2,1,0:T(8,128)} %pack.1.refs_0_), channel_id=1, source_target_pairs={{0,16},{16,0},{1,17},{17,1},{2,18},{18,2},{3,19},{19,3},{4,20},{20... | collective-permute-start | bytes 1572872 | tf_op jit(solution)/shard_map/ppermute | solution.py:220
  4.9 1.5 %collective-permute-start = (f32[8,64,256]{2,1,0:T(8,128)}, f32[8,64,256]{2,1,0:T(8,128)S(1)}, u32[]{:S(2)}, u32[]{:S(2)}) collective-permute-start(f32[8,64,256]{2,1,0:T(8,128)} %pack.1.refs_0_), channel_id=1, source_target_pairs={{0,1},{1,0},{2,3},{3,2},{4,5},{5,4},{6,7},{7,6},{8,9},{9,8},{10,11... | collective-permute-start | bytes 1572872 | tf_op jit(solution)/shard_map/ppermute | solution.py:219
  6.4 0.0 copy-start
  6.4 3.3 %copy-done = f32[16128,128]{1,0:T(8,128)S(1)} copy-done((f32[16128,128]{1,0:T(8,128)S(1)}, f32[16128,128]{1,0:T(8,128)}, u32[]{:S(2)}) %copy-start) | copy-done | bytes 8257560
  9.8 0.0 copy-start.14
  9.8 0.9 %copy-done.14 = f32[8,64,128]{2,1,0:T(8,128)S(1)} copy-done((f32[8,64,128]{2,1,0:T(8,128)S(1)}, f32[8,64,128]{2,1,0:T(8,128)}, u32[]{:S(2)}) %copy-start.14) | copy-done | bytes 262168
  10.7 16.0 %earlier.1 = f32[4,128,128]{2,1,0:T(8,128)} custom-call(s32[1]{0:T(128)} %bitcast.first_ref, f32[512,16128]{1,0:T(8,128)} %bitcast.12, f32[16128,128]{1,0:T(8,128)S(1)} %copy-done, f32[512,128]{1,0:T(8,128)S(1)} %bitcast.11), custom_call_target="tpu_custom_call" | custom-call | flops 8455716864 | bytes 41287680 | tf_op jit(solution)/shard_map/earlier/pallas_call | solution.py:59
  26.7 0.0 collective-permute-done.1.refs_2_
  26.7 0.0 copy-start.4
  26.7 0.0 collective-permute-done.refs_1_
  26.7 0.0 copy-start.6
  26.8 0.1 collective-permute-start.8
  26.8 0.5 collective-permute-start.7
  27.3 0.5 collective-permute-start.3
  27.9 0.2 collective-permute-start.2
  28.0 6.3 %all-to-all-start = ((f32[32,16,128]{2,1,0:T(8,128)}), f32[32,16,128]{2,1,0:T(8,128)S(1)}, u32[]{:S(2)}, u32[]{:S(2)}) async-start(f32[32,16,128]{2,1,0:T(8,128)} %bitcast.3), calls=%async_computation | async-start | bytes 524288 | tf_op jit(solution)/shard_map/all_to_all | solution.py:232
  34.3 1.4 %collective-permute-done.3.refs_1_ = f32[4,64,256]{2,1,0:T(8,128)} collective-permute-done((f32[4,64,256]{2,1,0:T(8,128)S(1)}, f32[4,64,256]{2,1,0:T(8,128)}, u32[]{:S(2)}, u32[]{:S(2)}) %collective-permute-start.3) | collective-permute-done | bytes 262176 | tf_op jit(solution)/shard_map/ppermute | solution.py:230
  35.7 0.0 collective-permute-start.5
  35.7 0.3 collective-permute-done.2.refs_0_
  36.1 0.2 collective-permute-start.4
  36.2 0.0 collective-permute-done.6.refs_3_
  36.2 0.0 copy-start.8
  36.2 0.8 copy-done.8
  37.0 0.0 collective-permute-done.7.refs_4_
  37.1 0.0 copy-done.4
  37.1 0.0 copy-done.6
  37.1 0.0 copy-start.12
  37.1 0.8 copy-done.12
  37.9 0.0 collective-permute-done.8.refs_5_
  37.9 0.0 copy-start.10
  37.9 0.8 copy-done.10
  38.6 0.0 copy-start.3
  38.6 1.0 %copy-done.3 = f32[8,64,256]{2,1,0:T(8,128)S(1)} copy-done((f32[8,64,256]{2,1,0:T(8,128)S(1)}, f32[8,64,256]{2,1,0:T(8,128)}, u32[]{:S(2)}) %copy-start.3) | copy-done | bytes 524312
  39.7 0.0 copy-start.5
  39.7 1.0 %copy-done.5 = f32[8,64,256]{2,1,0:T(8,128)S(1)} copy-done((f32[8,64,256]{2,1,0:T(8,128)S(1)}, f32[8,64,256]{2,1,0:T(8,128)}, u32[]{:S(2)}) %copy-start.5) | copy-done | bytes 524312
  40.7 0.0 copy-start.7
  40.7 1.0 %copy-done.7 = f32[8,64,256]{2,1,0:T(8,128)S(1)} copy-done((f32[8,64,256]{2,1,0:T(8,128)S(1)}, f32[8,64,256]{2,1,0:T(8,128)}, u32[]{:S(2)}) %copy-start.7) | copy-done | bytes 524312
  41.8 0.0 copy-start.9
  41.8 1.0 %copy-done.9 = f32[8,64,256]{2,1,0:T(8,128)S(1)} copy-done((f32[8,64,256]{2,1,0:T(8,128)S(1)}, f32[8,64,256]{2,1,0:T(8,128)}, u32[]{:S(2)}) %copy-start.9) | copy-done | bytes 524312
  42.8 0.0 copy-start.11
  42.8 1.0 %copy-done.11 = f32[8,64,256]{2,1,0:T(8,128)S(1)} copy-done((f32[8,64,256]{2,1,0:T(8,128)S(1)}, f32[8,64,256]{2,1,0:T(8,128)}, u32[]{:S(2)}) %copy-start.11) | copy-done | bytes 524312
  43.9 1.0 %copy-done.13 = f32[8,64,256]{2,1,0:T(8,128)S(1)} copy-done((f32[8,64,256]{2,1,0:T(8,128)S(1)}, f32[8,64,256]{2,1,0:T(8,128)}, u32[]{:S(2)}) %copy-start.13) | copy-done | bytes 524312
  44.9 0.6 arrange.1
  45.6 0.0 collective-permute-done.5.refs_3_
  45.6 0.0 collective-permute-done.4.refs_2_
  45.6 1.2 %arrange_corner.1 = (bf16[2,512,512]{2,1,0:T(8,128)(2,1)S(1)}, bf16[2,512,512]{2,1,0:T(8,128)(2,1)S(1)}, bf16[2,512,512]{2,1,0:T(8,128)(2,1)S(1)}, bf16[2,512,512]{2,1,0:T(8,128)(2,1)S(1)}) custom-call(f32[4,64,256]{2,1,0:T(8,128)} %collective-permute-done.2.refs_0_, ...), custom_call_target="tpu_custom_call", output_to_operand_aliasing={{0}: (4, {}), {1}: (5, {}), {2}: (6, {}), {3}: (7, {})} | custom-call | tf_op jit(solution)/shard_map/arrange_corner/pallas_call | solution.py:124
  46.8 0.0 copy-start.1
  46.8 1.0 %copy-done.1 = bf16[2,512,512]{2,1,0:T(8,128)(2,1)} copy-done((bf16[2,512,512]{2,1,0:T(8,128)(2,1)}, bf16[2,512,512]{2,1,0:T(8,128)(2,1)S(1)}, u32[]{:S(2)}) %copy-start.1) | copy-done | bytes 1048600
  47.7 0.0 all-to-all-done
  47.7 1.2 %copy-done.2 = bf16[2,512,512]{2,1,0:T(8,128)(2,1)S(1)} copy-done((bf16[2,512,512]{2,1,0:T(8,128)(2,1)S(1)}, bf16[2,512,512]{2,1,0:T(8,128)(2,1)}, u32[]{:S(2)}) %copy-start.2) | copy-done | bytes 1048600
  49.0 1.4 %chain_first.1 = (f32[16,512]{1,0:T(8,128)S(1)}, f32[3,16,512]{2,1,0:T(8,128)S(1)}) custom-call(f32[4,4,2,16,128]{4,3,2,1,0:T(8,128)S(1)} %bitcast.8, bf16[2,512,512]{2,1,0:T(8,128)(2,1)S(1)} %get-tuple-element.29.refs_0_.weight_ref, bf16[2,512,512]{2,1,0:T(8,128)(2,1)S(1)} %get-tuple-element.30.refs_1_, bf16[2,512,512]{2,1,0:T(8,128)(2,1)S(1)} %get-tuple-element.31.refs_2_, ...), custom_call_target="tpu_custom_call" | custom-call | tf_op jit(solution)/shard_map/chain_first/pallas_call | solution.py:194
  50.3 3.5 %collective-permute-start.9 = (f32[3,16,512]{2,1,0:T(8,128)S(1)}, f32[3,16,512]{2,1,0:T(8,128)S(1)}, u32[]{:S(2)}, u32[]{:S(2)}) collective-permute-start(f32[3,16,512]{2,1,0:T(8,128)S(1)} %get-tuple-element.34), channel_id=1, source_target_pairs={{0,2},{1,3},{8,10},{9,11},{16,18},{17,19},{24,26},{25,27}} | collective-permute-start | bytes 294920 | tf_op jit(solution)/shard_map/ppermute | solution.py:245
  53.8 2.5 %collective-permute-done.9.received_ref = f32[3,16,512]{2,1,0:T(8,128)S(1)} collective-permute-done((f32[3,16,512]{2,1,0:T(8,128)S(1)}, f32[3,16,512]{2,1,0:T(8,128)S(1)}, u32[]{:S(2)}, u32[]{:S(2)}) %collective-permute-start.9) | collective-permute-done | bytes 98336 | tf_op jit(solution)/shard_map/ppermute | solution.py:245
  56.4 1.1 %chain_middle.2 = (f32[16,512]{1,0:T(8,128)S(1)}, f32[2,16,512]{2,1,0:T(8,128)S(1)}) custom-call(f32[16,512]{1,0:T(8,128)S(1)} %get-tuple-element.33.residual_ref, f32[3,16,512]{2,1,0:T(8,128)S(1)} %collective-permute-done.9.received_ref, bf16[2,512,512]{2,1,0:T(8,128)(2,1)S(1)} %get-tuple-element.29.refs_0_.weight_ref, ...), custom_call_target="tpu_custom_call" | custom-call | tf_op jit(solution)/shard_map/chain_middle/pallas_call | solution.py:194
  57.4 0.7 collective-permute-start.10
  58.1 0.0 collective-permute-done.10.received_ref
  58.1 0.8 chain_middle.3
  58.9 0.7 collective-permute-start.11
  59.6 0.0 collective-permute-done.11.received_ref
  59.6 0.6 chain_last.1
  60.3 22.5 %all_to_all.10 = f32[32,16,128]{2,1,0:T(8,128)S(1)} all-to-all(f32[32,16,128]{2,1,0:T(8,128)S(1)} %bitcast.10), channel_id=1, replica_groups=mesh['y'=2,'core'=2,'z'=4,'x'=2] {'z','y','core','x'}, dimensions={0} | all-to-all | bytes 524288 | tf_op jit(solution)/shard_map/all_to_all | solution.py:251
  82.8 0.8 turn.1
  (4 shorter events, 0.0 us)
Async XLA Ops:
  1.8 34.4 %collective-permute-start.6 = (f32[8,64,256]{2,1,0:T(8,128)}, f32[8,64,256]{2,1,0:T(8,128)S(1)}, u32[]{:S(2)}, u32[]{:S(2)}) collective-permute-start(f32[8,64,256]{2,1,0:T(8,128)} %pack.1.refs_0_), channel_id=1, source_target_pairs={{0,8},{8,0},{1,9},{9,1},{2,10},{10,2},{3,11},{11,3},{4,12},{12,4},... | collective-permute-start | bytes 1572872 | tf_op jit(solution)/shard_map/ppermute | solution.py:221
  2.3 24.4 %collective-permute-start.1 = (f32[8,64,256]{2,1,0:T(8,128)}, f32[8,64,256]{2,1,0:T(8,128)S(1)}, u32[]{:S(2)}, u32[]{:S(2)}) collective-permute-start(f32[8,64,256]{2,1,0:T(8,128)} %pack.1.refs_0_), channel_id=1, source_target_pairs={{0,16},{16,0},{1,17},{17,1},{2,18},{18,2},{3,19},{19,3},{4,20},{20... | collective-permute-start | bytes 1572872 | tf_op jit(solution)/shard_map/ppermute | solution.py:220
  4.9 21.8 %collective-permute-start = (f32[8,64,256]{2,1,0:T(8,128)}, f32[8,64,256]{2,1,0:T(8,128)S(1)}, u32[]{:S(2)}, u32[]{:S(2)}) collective-permute-start(f32[8,64,256]{2,1,0:T(8,128)} %pack.1.refs_0_), channel_id=1, source_target_pairs={{0,1},{1,0},{2,3},{3,2},{4,5},{5,4},{6,7},{7,6},{8,9},{9,8},{10,11... | collective-permute-start | bytes 1572872 | tf_op jit(solution)/shard_map/ppermute | solution.py:219
  6.4 3.3 %copy-start = (f32[16128,128]{1,0:T(8,128)S(1)}, f32[16128,128]{1,0:T(8,128)}, u32[]{:S(2)}) copy-start(f32[16128,128]{1,0:T(8,128)} %solved_ref.1) | copy-start | bytes 24772612
  9.8 0.9 %copy-start.14 = (f32[8,64,128]{2,1,0:T(8,128)S(1)}, f32[8,64,128]{2,1,0:T(8,128)}, u32[]{:S(2)}) copy-start(f32[8,64,128]{2,1,0:T(8,128)} %param.5) | copy-start | bytes 786436
  26.7 10.3 %copy-start.4 = (f32[8,64,256]{2,1,0:T(8,128)}, f32[8,64,256]{2,1,0:T(8,128)S(1)}, u32[]{:S(2)}) copy-start(f32[8,64,256]{2,1,0:T(8,128)S(1)} %collective-permute-done.1.refs_2_) | copy-start | bytes 1572868
  26.7 10.3 %copy-start.6 = (f32[8,64,256]{2,1,0:T(8,128)}, f32[8,64,256]{2,1,0:T(8,128)S(1)}, u32[]{:S(2)}) copy-start(f32[8,64,256]{2,1,0:T(8,128)S(1)} %collective-permute-done.refs_1_) | copy-start | bytes 1572868
  26.8 11.1 %collective-permute-start.8 = (f32[8,64,256]{2,1,0:T(8,128)S(1)}, f32[8,64,256]{2,1,0:T(8,128)S(1)}, u32[]{:S(2)}, u32[]{:S(2)}) collective-permute-start(f32[8,64,256]{2,1,0:T(8,128)S(1)} %collective-permute-done.1.refs_2_), channel_id=1, source_target_pairs={{0,8},{8,0},{1,9},{9,1},{2,10},{10,2},{3,11},{11,3},{4,12},{12,4},... | collective-permute-start | bytes 1572872 | tf_op jit(solution)/shard_map/ppermute | solution.py:231
  26.8 10.2 %collective-permute-start.7 = (f32[8,64,256]{2,1,0:T(8,128)S(1)}, f32[8,64,256]{2,1,0:T(8,128)S(1)}, u32[]{:S(2)}, u32[]{:S(2)}) collective-permute-start(f32[8,64,256]{2,1,0:T(8,128)S(1)} %collective-permute-done.refs_1_), channel_id=1, source_target_pairs={{0,8},{8,0},{1,9},{9,1},{2,10},{10,2},{3,11},{11,3},{4,12},{12,4},... | collective-permute-start | bytes 1572872 | tf_op jit(solution)/shard_map/ppermute | solution.py:231
  27.3 8.4 %collective-permute-start.3 = (f32[4,64,256]{2,1,0:T(8,128)S(1)}, f32[4,64,256]{2,1,0:T(8,128)}, u32[]{:S(2)}, u32[]{:S(2)}) collective-permute-start(f32[4,64,256]{2,1,0:T(8,128)S(1)} %slice.7), channel_id=1, source_target_pairs={{0,1},{1,0},{2,3},{3,2},{4,5},{5,4},{6,7},{7,6},{8,9},{9,8},{10,11... | collective-permute-start | bytes 786440 | tf_op jit(solution)/shard_map/ppermute | solution.py:230
  27.9 8.2 %collective-permute-start.2 = (f32[4,64,256]{2,1,0:T(8,128)S(1)}, f32[4,64,256]{2,1,0:T(8,128)}, u32[]{:S(2)}, u32[]{:S(2)}) collective-permute-start(f32[4,64,256]{2,1,0:T(8,128)S(1)} %slice.6), channel_id=1, source_target_pairs={{0,16},{16,0},{1,17},{17,1},{2,18},{18,2},{3,19},{19,3},{4,20},{20... | collective-permute-start | bytes 786440 | tf_op jit(solution)/shard_map/ppermute | solution.py:229
  28.0 19.7 %all-to-all-start = ((f32[32,16,128]{2,1,0:T(8,128)}), f32[32,16,128]{2,1,0:T(8,128)S(1)}, u32[]{:S(2)}, u32[]{:S(2)}) async-start(f32[32,16,128]{2,1,0:T(8,128)} %bitcast.3), calls=%async_computation | async-start | bytes 524288 | tf_op jit(solution)/shard_map/all_to_all | solution.py:232
  35.7 9.8 %collective-permute-start.5 = (f32[4,64,256]{2,1,0:T(8,128)}, f32[4,64,256]{2,1,0:T(8,128)S(1)}, u32[]{:S(2)}, u32[]{:S(2)}) collective-permute-start(f32[4,64,256]{2,1,0:T(8,128)} %collective-permute-done.3.refs_1_), channel_id=1, source_target_pairs={{0,8},{8,0},{1,9},{9,1},{2,10},{10,2},{3,11},{11,3},{4,12},{12,4},... | collective-permute-start | bytes 786440 | tf_op jit(solution)/shard_map/ppermute | solution.py:233
  36.1 9.5 %collective-permute-start.4 = (f32[4,64,256]{2,1,0:T(8,128)}, f32[4,64,256]{2,1,0:T(8,128)S(1)}, u32[]{:S(2)}, u32[]{:S(2)}) collective-permute-start(f32[4,64,256]{2,1,0:T(8,128)} %collective-permute-done.2.refs_0_), channel_id=1, source_target_pairs={{0,8},{8,0},{1,9},{9,1},{2,10},{10,2},{3,11},{11,3},{4,12},{12,4},... | collective-permute-start | bytes 786440 | tf_op jit(solution)/shard_map/ppermute | solution.py:233
  36.2 0.8 copy-start.8
  37.1 0.8 copy-start.12
  37.9 0.8 copy-start.10
  38.6 1.0 %copy-start.3 = (f32[8,64,256]{2,1,0:T(8,128)S(1)}, f32[8,64,256]{2,1,0:T(8,128)}, u32[]{:S(2)}) copy-start(f32[8,64,256]{2,1,0:T(8,128)} %pack.1.refs_0_) | copy-start | bytes 1572868
  39.7 1.0 %copy-start.5 = (f32[8,64,256]{2,1,0:T(8,128)S(1)}, f32[8,64,256]{2,1,0:T(8,128)}, u32[]{:S(2)}) copy-start(f32[8,64,256]{2,1,0:T(8,128)} %copy-done.4) | copy-start | bytes 1572868
  40.7 1.0 %copy-start.7 = (f32[8,64,256]{2,1,0:T(8,128)S(1)}, f32[8,64,256]{2,1,0:T(8,128)}, u32[]{:S(2)}) copy-start(f32[8,64,256]{2,1,0:T(8,128)} %copy-done.6) | copy-start | bytes 1572868
  41.8 1.0 %copy-start.9 = (f32[8,64,256]{2,1,0:T(8,128)S(1)}, f32[8,64,256]{2,1,0:T(8,128)}, u32[]{:S(2)}) copy-start(f32[8,64,256]{2,1,0:T(8,128)} %copy-done.8) | copy-start | bytes 1572868
  42.8 1.0 %copy-start.11 = (f32[8,64,256]{2,1,0:T(8,128)S(1)}, f32[8,64,256]{2,1,0:T(8,128)}, u32[]{:S(2)}) copy-start(f32[8,64,256]{2,1,0:T(8,128)} %copy-done.10) | copy-start | bytes 1572868
  43.9 1.0 %copy-start.13 = (f32[8,64,256]{2,1,0:T(8,128)S(1)}, f32[8,64,256]{2,1,0:T(8,128)}, u32[]{:S(2)}) copy-start(f32[8,64,256]{2,1,0:T(8,128)} %copy-done.12) | copy-start | bytes 1572868
  46.8 1.0 %copy-start.1 = (bf16[2,512,512]{2,1,0:T(8,128)(2,1)}, bf16[2,512,512]{2,1,0:T(8,128)(2,1)S(1)}, u32[]{:S(2)}) copy-start(bf16[2,512,512]{2,1,0:T(8,128)(2,1)S(1)} %get-tuple-element.32.refs_3_) | copy-start | bytes 3145732
  47.7 1.2 %copy-start.2 = (bf16[2,512,512]{2,1,0:T(8,128)(2,1)S(1)}, bf16[2,512,512]{2,1,0:T(8,128)(2,1)}, u32[]{:S(2)}) copy-start(bf16[2,512,512]{2,1,0:T(8,128)(2,1)} %copy-done.1) | copy-start | bytes 3145732
  50.3 6.0 %collective-permute-start.9 = (f32[3,16,512]{2,1,0:T(8,128)S(1)}, f32[3,16,512]{2,1,0:T(8,128)S(1)}, u32[]{:S(2)}, u32[]{:S(2)}) collective-permute-start(f32[3,16,512]{2,1,0:T(8,128)S(1)} %get-tuple-element.34), channel_id=1, source_target_pairs={{0,2},{1,3},{8,10},{9,11},{16,18},{17,19},{24,26},{25,27}} | collective-permute-start | bytes 294920 | tf_op jit(solution)/shard_map/ppermute | solution.py:245
  57.4 0.7 collective-permute-start.10
  58.9 0.7 collective-permute-start.11

commit v3 on v2

--- a/solution.py
+++ b/solution.py
@@ -30,65 +30,89 @@
     return lax.dot_general(a, b, (((1,), (1,)), ((), ())), preferred_element_type=F32)
 
 
-def earlier_sums(first_ref, factor_ref, solved_ref, right_ref, out_ref, total):
-    step = pl.program_id(0)
-
-    @pl.when(step == 0)
-    def _():
-        total[...] = jnp.zeros_like(total)
-
-    factor_high, factor_low = halves(factor_ref[...])
-    solved_both = jnp.concatenate(halves(solved_ref[...]), axis=1)
-    total[...] += dot_f32(factor_high, solved_both) + dot_f32(factor_low, solved_both)
-
-    @pl.when(step == pl.num_programs(0) - 1)
-    def _():
-        keep = first_ref[0] == 0
-        width = right_ref.shape[1]
-        for part in range(PLANES):
-            rows = slice(part * 128, part * 128 + 128)
-            earlier = total[rows, :width] + total[rows, width:]
-            right = jnp.where(keep, right_ref[rows, :], 0.0)
-            out_ref[part] = (right - earlier).T
+def earlier_sums(tile, first_ref, factor_ref, solved_ref, right_ref, out_ref, factors, solves, right, total, sems):
+    steps = factor_ref.shape[1] // tile
+    slots = factors.shape[0]
+
+    def copies(step, slot):
+        where = pl.ds(pl.multiple_of(step * tile, 128), tile)
+        return (
+            pltpu.make_async_copy(factor_ref.at[:, where], factors.at[slot], sems.at[0, slot]),
+            pltpu.make_async_copy(solved_ref.at[where, :], solves.at[slot], sems.at[1, slot]),
+        )
+
+    for step in range(min(slots - 1, steps)):
+        for copy in copies(step, step):
+            copy.start()
+    fetch_right = pltpu.make_async_copy(right_ref, right, sems.at[2, 0])
+    fetch_right.start()
+    total[...] = jnp.zeros_like(total)
+
+    def body(step, carry):
+        ahead = step + slots - 1
+
+        @pl.when(ahead < steps)
+        def _():
+            for copy in copies(ahead, lax.rem(ahead, slots)):
+                copy.start()
+
+        slot = lax.rem(step, slots)
+        for copy in copies(step, slot):
+            copy.wait()
+        factor_high, factor_low = halves(factors[slot])
+        solved_both = jnp.concatenate(halves(solves[slot]), axis=1)
+        total[...] += dot_f32(factor_high, solved_both) + dot_f32(factor_low, solved_both)
+        return carry
+
+    lax.fori_loop(0, steps, body, 0)
+    fetch_right.wait()
+    keep = first_ref[0] == 0
+    width = right.shape[1]
+    for part in range(PLANES):
+        rows = slice(part * 128, part * 128 + 128)
+        earlier = total[rows, :width] + total[rows, width:]
+        out_ref[part] = (jnp.where(keep, right[rows, :], 0.0) - earlier).T
+
+
+def in_hbm(*arrays):
+    return tuple(pltpu.with_memory_space_constraint(a, pltpu.HBM) for a in arrays)
 
 
 def earlier_residual(first, factor, solved, right):
     rows, depth = factor.shape
     columns = solved.shape[1]
-    tile = next(t for t in (2304, 2016, 1792, 1152, 1024, 768, 512, 256, 128) if depth % t == 0)
+    tile = next(t for t in (1152, 1024, 768, 512, 256, 128) if depth % t == 0)
+    slots = 4
+    anywhere = pl.BlockSpec(memory_space=pl.ANY)
     return pl.pallas_call(
-        earlier_sums,
+        functools.partial(earlier_sums, tile),
         out_shape=jax.ShapeDtypeStruct((PLANES, columns, 128), F32),
-        grid=(depth // tile,),
-        in_specs=[
-            pl.BlockSpec(memory_space=pltpu.SMEM),
-            pl.BlockSpec((rows, tile), lambda k: (0, k)),
-            pl.BlockSpec((tile, columns), lambda k: (k, 0)),
-            pl.BlockSpec((rows, columns), lambda k: (0, 0)),
+        in_specs=[pl.BlockSpec(memory_space=pltpu.SMEM)] + [anywhere] * 3,
+        out_specs=pl.BlockSpec(memory_space=pltpu.VMEM),
+        scratch_shapes=[
+            pltpu.VMEM((slots, rows, tile), F32),
+            pltpu.VMEM((slots, tile, columns), F32),
+            pltpu.VMEM((rows, columns), F32),
+            pltpu.VMEM((rows, 2 * columns), F32),
+            pltpu.SemaphoreType.DMA((3, slots)),
         ],
-        out_specs=pl.BlockSpec((PLANES, columns, 128), lambda k: (0, 0, 0)),
-        scratch_shapes=[pltpu.VMEM((rows, 2 * columns), F32)],
-        compiler_params=pltpu.CompilerParams(vmem_limit_bytes=24 << 20),
+        compiler_params=pltpu.CompilerParams(vmem_limit_bytes=32 << 20),
         cost_estimate=pl.CostEstimate(
             flops=8 * rows * columns * depth, bytes_accessed=4 * (rows + columns) * depth, transcendentals=0
         ),
         name="earlier",
-    )(first, factor, solved, right)
-
-
-def pack(window_ref, inverse_ref, out_ref, held, sems):
+    )(first, *in_hbm(factor, solved, right))
+
+
+def pack(window_ref, inverse_ref, out_ref, sems):
     z, x = lax.axis_index("z"), lax.axis_index("x")
-    copies = []
-    for j in range(8):
-        source = inverse_ref.at[2 * z + x] if j == 0 else window_ref.at[lax.rem(2 * z + j, 8)]
-        first = pltpu.make_async_copy(source, held.at[j], sems.at[0, j])
-        copies.append((first, pltpu.make_async_copy(held.at[j], out_ref.at[j], sems.at[1, j])))
-        first.start()
-    for first, second in copies:
-        first.wait()
-        second.start()
-    for first, second in copies:
-        second.wait()
+    copies = [pltpu.make_async_copy(inverse_ref.at[2 * z + x], out_ref.at[0], sems.at[0])]
+    for j in range(1, 8):
+        copies.append(pltpu.make_async_copy(window_ref.at[lax.rem(2 * z + j, 8)], out_ref.at[j], sems.at[j]))
+    for copy in copies:
+        copy.start()
+    for copy in copies:
+        copy.wait()
 
 
 def place_piece(piece, y, core, x, other, dy, dx, start, outs):
@@ -130,7 +154,7 @@
         input_output_aliases={count + i: i for i in range(len(weights))},
         compiler_params=pltpu.CompilerParams(vmem_limit_bytes=8 << 20),
         name=name,
-    )(*pieces, *weights)
+    )(*in_hbm(*pieces), *weights)
 
 
 def apply(value, weight_ref, rows, columns):
@@ -209,12 +233,11 @@
         pack,
         out_shape=jax.ShapeDtypeStruct(lower_window.shape, F32),
         in_specs=[pl.BlockSpec(memory_space=pl.ANY)] * 2,
-        out_specs=pl.BlockSpec(memory_space=pl.ANY),
-        scratch_shapes=[pltpu.VMEM(lower_window.shape, F32), pltpu.SemaphoreType.DMA((2, 8))],
-        compiler_params=pltpu.CompilerParams(vmem_limit_bytes=60 << 20),
-        cost_estimate=pl.CostEstimate(flops=0, bytes_accessed=16 << 20, transcendentals=0),
+        out_specs=pl.BlockSpec(memory_space=pltpu.VMEM),
+        scratch_shapes=[pltpu.SemaphoreType.DMA((8,))],
+        compiler_params=pltpu.CompilerParams(vmem_limit_bytes=4 << 20),
         name="pack",
-    )(lower_window, inverse_diag)
+    )(*in_hbm(lower_window, inverse_diag))
 
     from_x = swap(message, "x")
     from_y = swap(message, "y")

time: 84.5 us -> 73.3 us (0.87)
  local copies, waits for them, and re-layouts: 15.2 us -> 4.62 us
  waiting for transfers between devices: 4.31 us -> 7.01 us
  starting transfers between devices: 17.2 us -> 15.4 us
    unnamed x30 -> x18, local copies, waits for them, and re-layouts: 15.1 us -> 4.58 us
    all_to_all x1, waiting for transfers between devices: 0.01 us -> 2.12 us  [local(): lax.all_to_all(parts.reshape(32, RHS_PART, 128), EVERY, 0, 0, tiled=True)]
    ppermute x2, starting transfers between devices: 4.18 us -> 2.41 us  [local(): received = lax.ppermute(sent, 'z', [(step - 1, step)])]
    pallas_call x2, Pallas kernels: 1.82 us -> 3.2 us  [arranged(): pl.pallas_call(functools.partial(arrange, spots, len(weights)), out_shape...]
    pallas_call x1, Pallas kernels: 16 us -> 14.9 us  [earlier_residual(): pl.pallas_call(functools.partial(earlier_sums, tile), out_shape=jax.Shape...]
  transfers between devices with their start and end apart: 13 -> 13, of which waited for: 3 -> 4; matrix products, arithmetic and copies ran while one was open for 0% -> 0% of each run, Pallas kernels for 21% -> 25%
where the time goes in v3:
time: 73.3 us; the launch traced here: 73 us
  Pallas kernels  24 us (33%)
  blocking collectives  21.8 us (30%)
  starting transfers between devices  15.4 us (21%)
  waiting for transfers between devices  7.01 us (10%)
  local copies, waits for them, and re-layouts  4.62 us (6%)
    all_to_all x1, blocking collectives, local(): lax.all_to_all(chunks.reshape(32, RHS_PART, 128), EVERY, 0, 0, tiled=True)  21.8 us
    pallas_call x1, Pallas kernels, earlier_residual(): pl.pallas_call(functools.partial(earlier_sums, tile), out_shape=jax.Shape...  14.9 us
    all_to_all x1, starting transfers between devices, local(): lax.all_to_all(parts.reshape(32, RHS_PART, 128), EVERY, 0, 0, tiled=True)  6.28 us
    pallas_call x5, Pallas kernels, call(): pl.pallas_call(kernel, out_shape=[jax.ShapeDtypeStruct(*o) for o in outs]...  4.71 us
    unnamed x18, local copies, waits for them, and re-layouts  4.58 us
    pallas_call x2, Pallas kernels, arranged(): pl.pallas_call(functools.partial(arrange, spots, len(weights)), out_shape...  3.2 us
    ppermute x2, waiting for transfers between devices, local(): received = lax.ppermute(sent, 'z', [(step - 1, step)])  3.12 us
    ppermute x1, starting transfers between devices, local(): from_y = swap(message, 'y')  2.59 us
  transfers between devices with their start and end apart: 13, of which 4 were waited for; matrix products, arithmetic and copies ran while one was open for 0% of the time, Pallas kernels for 25%

profile of v3, /device:TPU:0, one launch (start us, length us, event | category | flops | bytes accessed | tf_op | source)
XLA Modules:
  0.0 73.0 jit_solution(7798094708011091786)
XLA Ops:
  0.0 1.1 %pack.1.refs_0_ = f32[8,64,256]{2,1,0:T(8,128)S(1)} custom-call(f32[8,64,256]{2,1,0:T(8,128)} %window_ref.1, f32[8,64,256]{2,1,0:T(8,128)} %inverse_ref.1), custom_call_target="tpu_custom_call" | custom-call | tf_op jit(solution)/shard_map/pack/pallas_call | solution.py:232
  1.1 0.0 copy-start.2
  1.1 0.5 collective-permute-start.6
  1.7 2.6 %collective-permute-start.1 = (f32[8,64,256]{2,1,0:T(8,128)S(1)}, f32[8,64,256]{2,1,0:T(8,128)S(1)}, u32[]{:S(2)}, u32[]{:S(2)}) collective-permute-start(f32[8,64,256]{2,1,0:T(8,128)S(1)} %pack.1.refs_0_), channel_id=1, source_target_pairs={{0,16},{16,0},{1,17},{17,1},{2,18},{18,2},{3,19},{19,3},{4,20},{20... | collective-permute-start | bytes 1572872 | tf_op jit(solution)/shard_map/ppermute | solution.py:243
  4.3 1.5 %collective-permute-start = (f32[8,64,256]{2,1,0:T(8,128)S(1)}, f32[8,64,256]{2,1,0:T(8,128)S(1)}, u32[]{:S(2)}, u32[]{:S(2)}) collective-permute-start(f32[8,64,256]{2,1,0:T(8,128)S(1)} %pack.1.refs_0_), channel_id=1, source_target_pairs={{0,1},{1,0},{2,3},{3,2},{4,5},{5,4},{6,7},{7,6},{8,9},{9,8},{10,11... | collective-permute-start | bytes 1572872 | tf_op jit(solution)/shard_map/ppermute | solution.py:242
  5.7 14.9 %earlier.1 = f32[4,128,128]{2,1,0:T(8,128)} custom-call(s32[1]{0:T(128)} %bitcast.first_ref, f32[512,16128]{1,0:T(8,128)} %bitcast.11, f32[16128,128]{1,0:T(8,128)} %solved_ref.1, f32[512,128]{1,0:T(8,128)} %bitcast.12), custom_call_target="tpu_custom_call" | custom-call | flops 8455716864 | bytes 41287680 | tf_op jit(solution)/shard_map/earlier/pallas_call | solution.py:87
  20.7 0.0 collective-permute-done.1.refs_2_
  20.7 0.0 copy-start.3
  20.7 0.0 collective-permute-done.refs_1_
  20.7 0.0 copy-start.4
  20.7 0.1 collective-permute-start.8
  20.8 0.5 collective-permute-start.7
  21.3 0.5 collective-permute-start.3
  21.9 0.1 collective-permute-start.2
  22.0 6.3 %all-to-all-start = ((f32[32,16,128]{2,1,0:T(8,128)}), f32[32,16,128]{2,1,0:T(8,128)S(1)}, u32[]{:S(2)}, u32[]{:S(2)}) async-start(f32[32,16,128]{2,1,0:T(8,128)} %bitcast.3), calls=%async_computation | async-start | bytes 524288 | tf_op jit(solution)/shard_map/all_to_all | solution.py:255
  28.3 1.4 %collective-permute-done.3.refs_1_ = f32[4,64,256]{2,1,0:T(8,128)} collective-permute-done((f32[4,64,256]{2,1,0:T(8,128)S(1)}, f32[4,64,256]{2,1,0:T(8,128)}, u32[]{:S(2)}, u32[]{:S(2)}) %collective-permute-start.3) | collective-permute-done | bytes 262176 | tf_op jit(solution)/shard_map/ppermute | solution.py:253
  29.7 0.0 collective-permute-start.5
  29.7 0.3 collective-permute-done.2.refs_0_
  30.1 0.2 collective-permute-start.4
  30.2 0.0 collective-permute-done.6.refs_3_
  30.2 0.0 copy-start.5
  30.2 0.0 collective-permute-done.7.refs_4_
  30.2 0.0 copy-done.2
  30.2 0.0 copy-done.3
  30.3 0.0 copy-done.4
  30.3 0.8 %copy-done.5 = f32[8,64,256]{2,1,0:T(8,128)} copy-done((f32[8,64,256]{2,1,0:T(8,128)}, f32[8,64,256]{2,1,0:T(8,128)S(1)}, u32[]{:S(2)}) %copy-start.5) | copy-done | bytes 524312
  31.0 0.0 copy-start.6
  31.0 0.8 %copy-done.6 = f32[8,64,256]{2,1,0:T(8,128)} copy-done((f32[8,64,256]{2,1,0:T(8,128)}, f32[8,64,256]{2,1,0:T(8,128)S(1)}, u32[]{:S(2)}) %copy-start.6) | copy-done | bytes 524312
  31.8 0.0 collective-permute-done.8.refs_5_
  31.8 1.9 %arrange.1 = (bf16[2,512,512]{2,1,0:T(8,128)(2,1)S(1)}, bf16[2,512,512]{2,1,0:T(8,128)(2,1)S(1)}, bf16[2,512,512]{2,1,0:T(8,128)(2,1)S(1)}, bf16[2,512,512]{2,1,0:T(8,128)(2,1)S(1)}) custom-call(f32[8,64,256]{2,1,0:T(8,128)} %copy-done.2, f32[8,64,256]{2,1,0:T(8,128)} %copy-done.4, f32[8,64,256]{2,1,0:T(8,128)} %copy-done.3, f32[8,64,256]{2,1,0:T(8,128)} %copy-done.5, ...), custom_call_target="tpu_custom_call" | custom-call | tf_op jit(solution)/shard_map/arrange/pallas_call | solution.py:148
  33.8 0.0 collective-permute-done.5.refs_3_
  33.8 0.0 copy-start.7
  33.8 0.0 collective-permute-done.4.refs_2_
  33.8 0.0 copy-start.8
  33.8 0.7 copy-done.7
  34.5 0.1 copy-done.8
  34.6 1.3 %arrange_corner.1 = (bf16[2,512,512]{2,1,0:T(8,128)(2,1)S(1)}, bf16[2,512,512]{2,1,0:T(8,128)(2,1)S(1)}, bf16[2,512,512]{2,1,0:T(8,128)(2,1)S(1)}, bf16[2,512,512]{2,1,0:T(8,128)(2,1)S(1)}) custom-call(f32[4,64,256]{2,1,0:T(8,128)} %collective-permute-done.2.refs_0_, ...), custom_call_target="tpu_custom_call", output_to_operand_aliasing={{0}: (4, {}), {1}: (5, {}), {2}: (6, {}), {3}: (7, {})} | custom-call | tf_op jit(solution)/shard_map/arrange_corner/pallas_call | solution.py:148
  35.9 0.0 copy-start
  35.9 1.0 %copy-done = bf16[2,512,512]{2,1,0:T(8,128)(2,1)} copy-done((bf16[2,512,512]{2,1,0:T(8,128)(2,1)}, bf16[2,512,512]{2,1,0:T(8,128)(2,1)S(1)}, u32[]{:S(2)}) %copy-start) | copy-done | bytes 1048600
  36.9 2.1 %all-to-all-done = f32[32,16,128]{2,1,0:T(8,128)S(1)} async-done(((f32[32,16,128]{2,1,0:T(8,128)}), f32[32,16,128]{2,1,0:T(8,128)S(1)}, u32[]{:S(2)}, u32[]{:S(2)}) %all-to-all-start) | async-done | bytes 262176 | tf_op jit(solution)/shard_map/all_to_all | solution.py:255
  39.0 0.0 copy-start.1
  39.0 1.2 %copy-done.1 = bf16[2,512,512]{2,1,0:T(8,128)(2,1)S(1)} copy-done((bf16[2,512,512]{2,1,0:T(8,128)(2,1)S(1)}, bf16[2,512,512]{2,1,0:T(8,128)(2,1)}, u32[]{:S(2)}) %copy-start.1) | copy-done | bytes 1048600
  40.2 1.4 %chain_first.1 = (f32[16,512]{1,0:T(8,128)S(1)}, f32[3,16,512]{2,1,0:T(8,128)S(1)}) custom-call(f32[4,4,2,16,128]{4,3,2,1,0:T(8,128)S(1)} %bitcast.8, bf16[2,512,512]{2,1,0:T(8,128)(2,1)S(1)} %get-tuple-element.29.refs_0_.weight_ref, bf16[2,512,512]{2,1,0:T(8,128)(2,1)S(1)} %get-tuple-element.30.refs_1_, bf16[2,512,512]{2,1,0:T(8,128)(2,1)S(1)} %get-tuple-element.31.refs_2_, ...), custom_call_target="tpu_custom_call" | custom-call | tf_op jit(solution)/shard_map/chain_first/pallas_call | solution.py:218
  41.6 1.7 %collective-permute-start.9 = (f32[3,16,512]{2,1,0:T(8,128)S(1)}, f32[3,16,512]{2,1,0:T(8,128)S(1)}, u32[]{:S(2)}, u32[]{:S(2)}) collective-permute-start(f32[3,16,512]{2,1,0:T(8,128)S(1)} %get-tuple-element.34), channel_id=1, source_target_pairs={{0,2},{1,3},{8,10},{9,11},{16,18},{17,19},{24,26},{25,27}} | collective-permute-start | bytes 294920 | tf_op jit(solution)/shard_map/ppermute | solution.py:268
  43.3 3.1 %collective-permute-done.9.received_ref = f32[3,16,512]{2,1,0:T(8,128)S(1)} collective-permute-done((f32[3,16,512]{2,1,0:T(8,128)S(1)}, f32[3,16,512]{2,1,0:T(8,128)S(1)}, u32[]{:S(2)}, u32[]{:S(2)}) %collective-permute-start.9) | collective-permute-done | bytes 98336 | tf_op jit(solution)/shard_map/ppermute | solution.py:268
  46.4 1.1 %chain_middle.2 = (f32[16,512]{1,0:T(8,128)S(1)}, f32[2,16,512]{2,1,0:T(8,128)S(1)}) custom-call(f32[16,512]{1,0:T(8,128)S(1)} %get-tuple-element.33.residual_ref, f32[3,16,512]{2,1,0:T(8,128)S(1)} %collective-permute-done.9.received_ref, bf16[2,512,512]{2,1,0:T(8,128)(2,1)S(1)} %get-tuple-element.29.refs_0_.weight_ref, ...), custom_call_target="tpu_custom_call" | custom-call | tf_op jit(solution)/shard_map/chain_middle/pallas_call | solution.py:218
  47.5 0.7 collective-permute-start.10
  48.2 0.0 collective-permute-done.10.received_ref
  48.2 0.8 %chain_middle.3 = (f32[16,512]{1,0:T(8,128)S(1)}, f32[1,16,512]{2,1,0:T(8,128)S(1)}) custom-call(f32[16,512]{1,0:T(8,128)S(1)} %get-tuple-element.35.residual_ref, f32[2,16,512]{2,1,0:T(8,128)S(1)} %collective-permute-done.10.received_ref, bf16[2,512,512]{2,1,0:T(8,128)(2,1)S(1)} %get-tuple-element.29.refs_0_.weight_ref, ...), custom_call_target="tpu_custom_call" | custom-call | tf_op jit(solution)/shard_map/chain_middle/pallas_call | solution.py:218
  49.0 0.7 collective-permute-start.11
  49.7 0.0 collective-permute-done.11.received_ref
  49.7 0.6 chain_last.1
  50.4 21.8 %all_to_all.10 = f32[32,16,128]{2,1,0:T(8,128)S(1)} all-to-all(f32[32,16,128]{2,1,0:T(8,128)S(1)} %bitcast.10), channel_id=1, replica_groups=mesh['y'=2,'core'=2,'z'=4,'x'=2] {'z','y','core','x'}, dimensions={0} | all-to-all | bytes 524288 | tf_op jit(solution)/shard_map/all_to_all | solution.py:274
  72.1 0.8 %turn.1 = f32[4,128,128]{2,1,0:T(8,128)} custom-call(f32[4,128,128]{2,1,0:T(8,128)S(1)} %bitcast.9), custom_call_target="tpu_custom_call" | custom-call | tf_op jit(solution)/shard_map/turn/pallas_call | solution.py:218
  (2 shorter events, 0.0 us)
Async XLA Ops:
  1.1 29.1 %copy-start.2 = (f32[8,64,256]{2,1,0:T(8,128)}, f32[8,64,256]{2,1,0:T(8,128)S(1)}, u32[]{:S(2)}) copy-start(f32[8,64,256]{2,1,0:T(8,128)S(1)} %pack.1.refs_0_) | copy-start | bytes 1572868
  1.1 29.1 %collective-permute-start.6 = (f32[8,64,256]{2,1,0:T(8,128)S(1)}, f32[8,64,256]{2,1,0:T(8,128)S(1)}, u32[]{:S(2)}, u32[]{:S(2)}) collective-permute-start(f32[8,64,256]{2,1,0:T(8,128)S(1)} %pack.1.refs_0_), channel_id=1, source_target_pairs={{0,8},{8,0},{1,9},{9,1},{2,10},{10,2},{3,11},{11,3},{4,12},{12,4},... | collective-permute-start | bytes 1572872 | tf_op jit(solution)/shard_map/ppermute | solution.py:244
  1.7 19.0 %collective-permute-start.1 = (f32[8,64,256]{2,1,0:T(8,128)S(1)}, f32[8,64,256]{2,1,0:T(8,128)S(1)}, u32[]{:S(2)}, u32[]{:S(2)}) collective-permute-start(f32[8,64,256]{2,1,0:T(8,128)S(1)} %pack.1.refs_0_), channel_id=1, source_target_pairs={{0,16},{16,0},{1,17},{17,1},{2,18},{18,2},{3,19},{19,3},{4,20},{20... | collective-permute-start | bytes 1572872 | tf_op jit(solution)/shard_map/ppermute | solution.py:243
  4.3 16.4 %collective-permute-start = (f32[8,64,256]{2,1,0:T(8,128)S(1)}, f32[8,64,256]{2,1,0:T(8,128)S(1)}, u32[]{:S(2)}, u32[]{:S(2)}) collective-permute-start(f32[8,64,256]{2,1,0:T(8,128)S(1)} %pack.1.refs_0_), channel_id=1, source_target_pairs={{0,1},{1,0},{2,3},{3,2},{4,5},{5,4},{6,7},{7,6},{8,9},{9,8},{10,11... | collective-permute-start | bytes 1572872 | tf_op jit(solution)/shard_map/ppermute | solution.py:242
  20.7 9.6 %copy-start.3 = (f32[8,64,256]{2,1,0:T(8,128)}, f32[8,64,256]{2,1,0:T(8,128)S(1)}, u32[]{:S(2)}) copy-start(f32[8,64,256]{2,1,0:T(8,128)S(1)} %collective-permute-done.1.refs_2_) | copy-start | bytes 1572868
  20.7 9.6 %copy-start.4 = (f32[8,64,256]{2,1,0:T(8,128)}, f32[8,64,256]{2,1,0:T(8,128)S(1)}, u32[]{:S(2)}) copy-start(f32[8,64,256]{2,1,0:T(8,128)S(1)} %collective-permute-done.refs_1_) | copy-start | bytes 1572868
  20.7 11.1 %collective-permute-start.8 = (f32[8,64,256]{2,1,0:T(8,128)S(1)}, f32[8,64,256]{2,1,0:T(8,128)}, u32[]{:S(2)}, u32[]{:S(2)}) collective-permute-start(f32[8,64,256]{2,1,0:T(8,128)S(1)} %collective-permute-done.1.refs_2_), channel_id=1, source_target_pairs={{0,8},{8,0},{1,9},{9,1},{2,10},{10,2},{3,11},{11,3},{4,12},{12,4},... | collective-permute-start | bytes 1572872 | tf_op jit(solution)/shard_map/ppermute | solution.py:254
  20.8 9.4 %collective-permute-start.7 = (f32[8,64,256]{2,1,0:T(8,128)S(1)}, f32[8,64,256]{2,1,0:T(8,128)S(1)}, u32[]{:S(2)}, u32[]{:S(2)}) collective-permute-start(f32[8,64,256]{2,1,0:T(8,128)S(1)} %collective-permute-done.refs_1_), channel_id=1, source_target_pairs={{0,8},{8,0},{1,9},{9,1},{2,10},{10,2},{3,11},{11,3},{4,12},{12,4},... | collective-permute-start | bytes 1572872 | tf_op jit(solution)/shard_map/ppermute | solution.py:254
  21.3 8.4 %collective-permute-start.3 = (f32[4,64,256]{2,1,0:T(8,128)S(1)}, f32[4,64,256]{2,1,0:T(8,128)}, u32[]{:S(2)}, u32[]{:S(2)}) collective-permute-start(f32[4,64,256]{2,1,0:T(8,128)S(1)} %slice.7), channel_id=1, source_target_pairs={{0,1},{1,0},{2,3},{3,2},{4,5},{5,4},{6,7},{7,6},{8,9},{9,8},{10,11... | collective-permute-start | bytes 786440 | tf_op jit(solution)/shard_map/ppermute | solution.py:253
  21.9 8.2 %collective-permute-start.2 = (f32[4,64,256]{2,1,0:T(8,128)S(1)}, f32[4,64,256]{2,1,0:T(8,128)}, u32[]{:S(2)}, u32[]{:S(2)}) collective-permute-start(f32[4,64,256]{2,1,0:T(8,128)S(1)} %slice.6), channel_id=1, source_target_pairs={{0,16},{16,0},{1,17},{17,1},{2,18},{18,2},{3,19},{19,3},{4,20},{20... | collective-permute-start | bytes 786440 | tf_op jit(solution)/shard_map/ppermute | solution.py:252
  22.0 17.0 %all-to-all-start = ((f32[32,16,128]{2,1,0:T(8,128)}), f32[32,16,128]{2,1,0:T(8,128)S(1)}, u32[]{:S(2)}, u32[]{:S(2)}) async-start(f32[32,16,128]{2,1,0:T(8,128)} %bitcast.3), calls=%async_computation | async-start | bytes 524288 | tf_op jit(solution)/shard_map/all_to_all | solution.py:255
  29.7 4.1 %collective-permute-start.5 = (f32[4,64,256]{2,1,0:T(8,128)}, f32[4,64,256]{2,1,0:T(8,128)S(1)}, u32[]{:S(2)}, u32[]{:S(2)}) collective-permute-start(f32[4,64,256]{2,1,0:T(8,128)} %collective-permute-done.3.refs_1_), channel_id=1, source_target_pairs={{0,8},{8,0},{1,9},{9,1},{2,10},{10,2},{3,11},{11,3},{4,12},{12,4},... | collective-permute-start | bytes 786440 | tf_op jit(solution)/shard_map/ppermute | solution.py:256
  30.1 3.7 %collective-permute-start.4 = (f32[4,64,256]{2,1,0:T(8,128)}, f32[4,64,256]{2,1,0:T(8,128)S(1)}, u32[]{:S(2)}, u32[]{:S(2)}) collective-permute-start(f32[4,64,256]{2,1,0:T(8,128)} %collective-permute-done.2.refs_0_), channel_id=1, source_target_pairs={{0,8},{8,0},{1,9},{9,1},{2,10},{10,2},{3,11},{11,3},{4,12},{12,4},... | collective-permute-start | bytes 786440 | tf_op jit(solution)/shard_map/ppermute | solution.py:256
  30.2 0.8 %copy-start.5 = (f32[8,64,256]{2,1,0:T(8,128)}, f32[8,64,256]{2,1,0:T(8,128)S(1)}, u32[]{:S(2)}) copy-start(f32[8,64,256]{2,1,0:T(8,128)S(1)} %collective-permute-done.6.refs_3_) | copy-start | bytes 1572868
  31.0 0.8 %copy-start.6 = (f32[8,64,256]{2,1,0:T(8,128)}, f32[8,64,256]{2,1,0:T(8,128)S(1)}, u32[]{:S(2)}) copy-start(f32[8,64,256]{2,1,0:T(8,128)S(1)} %collective-permute-done.7.refs_4_) | copy-start | bytes 1572868
  33.8 0.7 copy-start.7
  33.8 0.8 %copy-start.8 = (f32[4,64,256]{2,1,0:T(8,128)}, f32[4,64,256]{2,1,0:T(8,128)S(1)}, u32[]{:S(2)}) copy-start(f32[4,64,256]{2,1,0:T(8,128)S(1)} %collective-permute-done.4.refs_2_) | copy-start | bytes 786436
  35.9 1.0 %copy-start = (bf16[2,512,512]{2,1,0:T(8,128)(2,1)}, bf16[2,512,512]{2,1,0:T(8,128)(2,1)S(1)}, u32[]{:S(2)}) copy-start(bf16[2,512,512]{2,1,0:T(8,128)(2,1)S(1)} %get-tuple-element.32.refs_3_) | copy-start | bytes 3145732
  39.0 1.2 %copy-start.1 = (bf16[2,512,512]{2,1,0:T(8,128)(2,1)S(1)}, bf16[2,512,512]{2,1,0:T(8,128)(2,1)}, u32[]{:S(2)}) copy-start(bf16[2,512,512]{2,1,0:T(8,128)(2,1)} %copy-done) | copy-start | bytes 3145732
  41.6 4.9 %collective-permute-start.9 = (f32[3,16,512]{2,1,0:T(8,128)S(1)}, f32[3,16,512]{2,1,0:T(8,128)S(1)}, u32[]{:S(2)}, u32[]{:S(2)}) collective-permute-start(f32[3,16,512]{2,1,0:T(8,128)S(1)} %get-tuple-element.34), channel_id=1, source_target_pairs={{0,2},{1,3},{8,10},{9,11},{16,18},{17,19},{24,26},{25,27}} | collective-permute-start | bytes 294920 | tf_op jit(solution)/shard_map/ppermute | solution.py:268
  47.5 0.7 collective-permute-start.10
  49.0 0.7 collective-permute-start.11

commit v4 on v3

--- a/solution.py
+++ b/solution.py
@@ -142,7 +142,7 @@
         place_piece(held.at[i], y, core, x, other, dy, dx, start, outs)
 
 
-def arranged(name, spots, pieces, weights=()):
+def arranged(name, spots, pieces, *weights):
     in_vmem = pl.BlockSpec(memory_space=pltpu.VMEM)
     count = len(pieces)
     return pl.pallas_call(
@@ -154,7 +154,7 @@
         input_output_aliases={count + i: i for i in range(len(weights))},
         compiler_params=pltpu.CompilerParams(vmem_limit_bytes=8 << 20),
         name=name,
-    )(*in_hbm(*pieces), *weights)
+    )(*pieces, *weights)
 
 
 def apply(value, weight_ref, rows, columns):
@@ -178,8 +178,9 @@
         out_ref[apart - 1] = term if received_ref is None else received_ref[apart] + term
 
 
-def chain_first(parts_ref, *refs):
-    weight_refs, (residual_ref, out_ref) = refs[:-2], refs[-2:]
+def chain_first(parts_ref, here_ref, near_ref, far_ref, farthest_ref, residual_ref, out_ref, held, sem):
+    fetch = pltpu.make_async_copy(farthest_ref, held, sem)
+    fetch.start()
     by_rows = []
     for row_part in range(4):
         terms = [parts_ref[z, row_part, x] for z in range(PLANES) for x in range(2)]
@@ -188,7 +189,10 @@
         by_rows.append(terms[0])
     residual = jnp.concatenate([t[:, :64] for t in by_rows] + [t[:, 64:] for t in by_rows], axis=1)
     residual_ref[...] = residual
-    push(solve(residual, weight_refs[0]), weight_refs[1:], None, out_ref)
+    solved = solve(residual, here_ref)
+    push(solved, (near_ref, far_ref), None, out_ref)
+    fetch.wait()
+    push(solved, (held,), None, out_ref.at[pl.ds(2, 1)])
 
 
 def chain_middle(residual_ref, received_ref, *refs):
@@ -213,16 +217,17 @@
         out_ref[part] = parts_ref[part].T
 
 
-def call(kernel, name, outs, *args, limit=8 << 20):
+def call(kernel, name, outs, *args, large=(), scratch=()):
     in_vmem = pl.BlockSpec(memory_space=pltpu.VMEM)
     return pl.pallas_call(
         kernel,
         out_shape=[jax.ShapeDtypeStruct(*o) for o in outs],
-        in_specs=[in_vmem] * len(args),
+        in_specs=[in_vmem] * len(args) + [pl.BlockSpec(memory_space=pl.ANY)] * len(large),
         out_specs=[in_vmem] * len(outs),
-        compiler_params=pltpu.CompilerParams(vmem_limit_bytes=limit),
+        scratch_shapes=scratch,
+        compiler_params=pltpu.CompilerParams(vmem_limit_bytes=8 << 20),
         name=name,
-    )(*args)
+    )(*args, *in_hbm(*large))
 
 
 def local(right_side, lower_prev, solved_prev, lower_window, inverse_diag):
@@ -256,14 +261,18 @@
     core_low, core_high = swap(corner_low, "core"), swap(corner_high, "core")
     pieces = (message, from_x, from_y, from_core, core_x, core_y)
     spots = ((0, 0, 0, 0), (0, 0, 1, 0), (0, 1, 0, 0), (1, 0, 0, 0), (1, 0, 1, 0), (1, 1, 0, 0))
-    weights = arranged("arrange", spots, pieces)
+    weights = arranged("arrange", spots, in_hbm(*pieces))
     pieces = (corner_low, corner_high, core_low, core_high)
-    weights = arranged("arrange_corner", ((0, 1, 1, 0), (0, 1, 1, 4), (1, 1, 1, 0), (1, 1, 1, 4)), pieces, weights)
+    weights = arranged("arrange_corner", ((0, 1, 1, 0), (0, 1, 1, 4), (1, 1, 1, 0), (1, 1, 1, 4)), pieces, *weights)
 
     def vectors(*counts):
         return ((*counts, RHS_PART, SUPER), F32)
 
-    residual, sent = call(chain_first, "chain_first", [vectors(), vectors(3)], parts.reshape(4, 4, 2, RHS_PART, 128), *weights)
+    parts = parts.reshape(4, 4, 2, RHS_PART, 128)
+    scratch = [pltpu.VMEM((2, SUPER, SUPER), BF16), pltpu.SemaphoreType.DMA]
+    residual, sent = call(
+        chain_first, "chain_first", [vectors(), vectors(3)], parts, *weights[:3], large=weights[3:], scratch=scratch
+    )
     for step in (1, 2):
         received = lax.ppermute(sent, "z", [(step - 1, step)])
         outs = [vectors(), vectors(3 - step)]

time: 73.3 us -> 72.4 us (0.988)
  local copies, waits for them, and re-layouts: 4.62 us -> 2.59 us
  waiting for transfers between devices: 7.01 us -> 7.91 us
    unnamed x18 -> x12, local copies, waits for them, and re-layouts: 4.58 us -> 2.56 us
    all_to_all x1, waiting for transfers between devices: 2.12 us -> 3.02 us  [local(): lax.all_to_all(parts.reshape(32, RHS_PART, 128), EVERY, 0, 0, tiled=True)]
where the time goes in v4:
time: 72.4 us; the launch traced here: 72 us
  Pallas kernels  24.1 us (33%)
  blocking collectives  21.8 us (30%)
  starting transfers between devices  15.4 us (21%)
  waiting for transfers between devices  7.91 us (11%)
  local copies, waits for them, and re-layouts  2.59 us (4%)
    all_to_all x1, blocking collectives, local(): lax.all_to_all(chunks.reshape(32, RHS_PART, 128), EVERY, 0, 0, tiled=True)  21.8 us
    pallas_call x1, Pallas kernels, earlier_residual(): pl.pallas_call(functools.partial(earlier_sums, tile), out_shape=jax.Shape...  14.9 us
    all_to_all x1, starting transfers between devices, local(): lax.all_to_all(parts.reshape(32, RHS_PART, 128), EVERY, 0, 0, tiled=True)  6.28 us
    pallas_call x5, Pallas kernels, call(): pl.pallas_call(kernel, out_shape=[jax.ShapeDtypeStruct(*o) for o in outs]...  4.99 us
    ppermute x2, waiting for transfers between devices, local(): received = lax.ppermute(sent, 'z', [(step - 1, step)])  3.12 us
    pallas_call x2, Pallas kernels, arranged(): pl.pallas_call(functools.partial(arrange, spots, len(weights)), out_shape...  3.11 us
    all_to_all x1, waiting for transfers between devices, local(): lax.all_to_all(parts.reshape(32, RHS_PART, 128), EVERY, 0, 0, tiled=True)  3.02 us
    ppermute x1, starting transfers between devices, local(): from_y = swap(message, 'y')  2.59 us
  transfers between devices with their start and end apart: 13, of which 4 were waited for; matrix products, arithmetic and copies ran while one was open for 0% of the time, Pallas kernels for 25%

profile of v4, /device:TPU:0, one launch (start us, length us, event | category | flops | bytes accessed | tf_op | source)
XLA Modules:
  0.0 72.0 jit_solution(15780025857573130409)
XLA Ops:
  0.0 1.1 %pack.1.refs_0_ = f32[8,64,256]{2,1,0:T(8,128)S(1)} custom-call(f32[8,64,256]{2,1,0:T(8,128)} %window_ref.1, f32[8,64,256]{2,1,0:T(8,128)} %inverse_ref.1), custom_call_target="tpu_custom_call" | custom-call | tf_op jit(solution)/shard_map/pack/pallas_call | solution.py:237
  1.1 0.0 copy-start.1
  1.1 0.5 collective-permute-start.6
  1.7 2.6 %collective-permute-start.1 = (f32[8,64,256]{2,1,0:T(8,128)S(1)}, f32[8,64,256]{2,1,0:T(8,128)S(1)}, u32[]{:S(2)}, u32[]{:S(2)}) collective-permute-start(f32[8,64,256]{2,1,0:T(8,128)S(1)} %pack.1.refs_0_), channel_id=1, source_target_pairs={{0,16},{16,0},{1,17},{17,1},{2,18},{18,2},{3,19},{19,3},{4,20},{20... | collective-permute-start | bytes 1572872 | tf_op jit(solution)/shard_map/ppermute | solution.py:248
  4.3 1.5 %collective-permute-start = (f32[8,64,256]{2,1,0:T(8,128)S(1)}, f32[8,64,256]{2,1,0:T(8,128)S(1)}, u32[]{:S(2)}, u32[]{:S(2)}) collective-permute-start(f32[8,64,256]{2,1,0:T(8,128)S(1)} %pack.1.refs_0_), channel_id=1, source_target_pairs={{0,1},{1,0},{2,3},{3,2},{4,5},{5,4},{6,7},{7,6},{8,9},{9,8},{10,11... | collective-permute-start | bytes 1572872 | tf_op jit(solution)/shard_map/ppermute | solution.py:247
  5.7 14.9 %earlier.1 = f32[4,128,128]{2,1,0:T(8,128)} custom-call(s32[1]{0:T(128)} %bitcast.first_ref, f32[512,16128]{1,0:T(8,128)} %bitcast.11, f32[16128,128]{1,0:T(8,128)} %solved_ref.1, f32[512,128]{1,0:T(8,128)} %bitcast.12), custom_call_target="tpu_custom_call" | custom-call | flops 8455716864 | bytes 41287680 | tf_op jit(solution)/shard_map/earlier/pallas_call | solution.py:87
  20.7 0.0 collective-permute-done.1.refs_2_
  20.7 0.0 copy-start.2
  20.7 0.0 collective-permute-done.refs_1_
  20.7 0.0 copy-start.3
  20.7 0.1 collective-permute-start.8
  20.8 0.5 collective-permute-start.7
  21.3 0.5 collective-permute-start.3
  21.9 0.1 collective-permute-start.2
  22.0 6.3 %all-to-all-start = ((f32[32,16,128]{2,1,0:T(8,128)}), f32[32,16,128]{2,1,0:T(8,128)S(1)}, u32[]{:S(2)}, u32[]{:S(2)}) async-start(f32[32,16,128]{2,1,0:T(8,128)} %bitcast.3), calls=%async_computation | async-start | bytes 524288 | tf_op jit(solution)/shard_map/all_to_all | solution.py:260
  28.3 1.4 %collective-permute-done.3.refs_1_ = f32[4,64,256]{2,1,0:T(8,128)} collective-permute-done((f32[4,64,256]{2,1,0:T(8,128)S(1)}, f32[4,64,256]{2,1,0:T(8,128)}, u32[]{:S(2)}, u32[]{:S(2)}) %collective-permute-start.3) | collective-permute-done | bytes 262176 | tf_op jit(solution)/shard_map/ppermute | solution.py:258
  29.7 0.0 collective-permute-start.5
  29.7 0.3 collective-permute-done.2.refs_0_
  30.1 0.2 collective-permute-start.4
  30.2 0.0 collective-permute-done.6.refs_3_
  30.2 0.0 copy-start.4
  30.2 0.0 collective-permute-done.7.refs_4_
  30.2 0.0 copy-done.1
  30.2 0.0 copy-done.2
  30.3 0.0 copy-done.3
  30.3 0.8 %copy-done.4 = f32[8,64,256]{2,1,0:T(8,128)} copy-done((f32[8,64,256]{2,1,0:T(8,128)}, f32[8,64,256]{2,1,0:T(8,128)S(1)}, u32[]{:S(2)}) %copy-start.4) | copy-done | bytes 524312
  31.0 0.0 copy-start.5
  31.0 0.8 %copy-done.5 = f32[8,64,256]{2,1,0:T(8,128)} copy-done((f32[8,64,256]{2,1,0:T(8,128)}, f32[8,64,256]{2,1,0:T(8,128)S(1)}, u32[]{:S(2)}) %copy-start.5) | copy-done | bytes 524312
  31.8 0.0 collective-permute-done.8.refs_5_
  31.8 1.9 %arrange.1 = (bf16[2,512,512]{2,1,0:T(8,128)(2,1)S(1)}, bf16[2,512,512]{2,1,0:T(8,128)(2,1)S(1)}, bf16[2,512,512]{2,1,0:T(8,128)(2,1)S(1)}, bf16[2,512,512]{2,1,0:T(8,128)(2,1)S(1)}) custom-call(f32[8,64,256]{2,1,0:T(8,128)} %copy-done.1, f32[8,64,256]{2,1,0:T(8,128)} %copy-done.3, f32[8,64,256]{2,1,0:T(8,128)} %copy-done.2, f32[8,64,256]{2,1,0:T(8,128)} %copy-done.4, ...), custom_call_target="tpu_custom_call" | custom-call | tf_op jit(solution)/shard_map/arrange/pallas_call | solution.py:148
  33.8 0.0 collective-permute-done.5.refs_3_
  33.8 0.0 collective-permute-done.4.refs_2_
  33.8 1.2 %arrange_corner.1 = (bf16[2,512,512]{2,1,0:T(8,128)(2,1)S(1)}, bf16[2,512,512]{2,1,0:T(8,128)(2,1)S(1)}, bf16[2,512,512]{2,1,0:T(8,128)(2,1)S(1)}, bf16[2,512,512]{2,1,0:T(8,128)(2,1)S(1)}) custom-call(f32[4,64,256]{2,1,0:T(8,128)} %collective-permute-done.2.refs_0_, ...), custom_call_target="tpu_custom_call", output_to_operand_aliasing={{0}: (4, {}), {1}: (5, {}), {2}: (6, {}), {3}: (7, {})} | custom-call | tf_op jit(solution)/shard_map/arrange_corner/pallas_call | solution.py:148
  35.0 0.0 copy-start
  35.0 1.0 %copy-done = bf16[2,512,512]{2,1,0:T(8,128)(2,1)} copy-done((bf16[2,512,512]{2,1,0:T(8,128)(2,1)}, bf16[2,512,512]{2,1,0:T(8,128)(2,1)S(1)}, u32[]{:S(2)}) %copy-start) | copy-done | bytes 1048600
  36.0 3.0 %all-to-all-done = f32[32,16,128]{2,1,0:T(8,128)S(1)} async-done(((f32[32,16,128]{2,1,0:T(8,128)}), f32[32,16,128]{2,1,0:T(8,128)S(1)}, u32[]{:S(2)}, u32[]{:S(2)}) %all-to-all-start) | async-done | bytes 262176 | tf_op jit(solution)/shard_map/all_to_all | solution.py:260
  39.0 1.6 %chain_first.1 = (f32[16,512]{1,0:T(8,128)S(1)}, f32[3,16,512]{2,1,0:T(8,128)S(1)}) custom-call(f32[4,4,2,16,128]{4,3,2,1,0:T(8,128)S(1)} %bitcast.8, bf16[2,512,512]{2,1,0:T(8,128)(2,1)S(1)} %get-tuple-element.29.here_ref.refs_0_.weight_ref, bf16[2,512,512]{2,1,0:T(8,128)(2,1)S(1)} %get-tuple-element.30.near_ref.refs_1_, ...), custom_call_target="tpu_custom_call" | custom-call | tf_op jit(solution)/shard_map/chain_first/pallas_call | solution.py:222
  40.6 1.7 %collective-permute-start.9 = (f32[3,16,512]{2,1,0:T(8,128)S(1)}, f32[3,16,512]{2,1,0:T(8,128)S(1)}, u32[]{:S(2)}, u32[]{:S(2)}) collective-permute-start(f32[3,16,512]{2,1,0:T(8,128)S(1)} %get-tuple-element.34), channel_id=1, source_target_pairs={{0,2},{1,3},{8,10},{9,11},{16,18},{17,19},{24,26},{25,27}} | collective-permute-start | bytes 294920 | tf_op jit(solution)/shard_map/ppermute | solution.py:277
  42.4 3.1 %collective-permute-done.9.received_ref = f32[3,16,512]{2,1,0:T(8,128)S(1)} collective-permute-done((f32[3,16,512]{2,1,0:T(8,128)S(1)}, f32[3,16,512]{2,1,0:T(8,128)S(1)}, u32[]{:S(2)}, u32[]{:S(2)}) %collective-permute-start.9) | collective-permute-done | bytes 98336 | tf_op jit(solution)/shard_map/ppermute | solution.py:277
  45.5 1.1 %chain_middle.2 = (f32[16,512]{1,0:T(8,128)S(1)}, f32[2,16,512]{2,1,0:T(8,128)S(1)}) custom-call(f32[16,512]{1,0:T(8,128)S(1)} %get-tuple-element.33.residual_ref, f32[3,16,512]{2,1,0:T(8,128)S(1)} %collective-permute-done.9.received_ref, bf16[2,512,512]{2,1,0:T(8,128)(2,1)S(1)} %get-tuple-element.29.here_ref.refs_0_.weight_ref, ...), custom_call_target="tpu_custom_call" | custom-call | tf_op jit(solution)/shard_map/chain_middle/pallas_call | solution.py:222
  46.6 0.7 collective-permute-start.10
  47.2 0.0 collective-permute-done.10.received_ref
  47.3 0.8 %chain_middle.3 = (f32[16,512]{1,0:T(8,128)S(1)}, f32[1,16,512]{2,1,0:T(8,128)S(1)}) custom-call(f32[16,512]{1,0:T(8,128)S(1)} %get-tuple-element.35.residual_ref, f32[2,16,512]{2,1,0:T(8,128)S(1)} %collective-permute-done.10.received_ref, bf16[2,512,512]{2,1,0:T(8,128)(2,1)S(1)} %get-tuple-element.29.here_ref.refs_0_.weight_ref, ...), custom_call_target="tpu_custom_call" | custom-call | tf_op jit(solution)/shard_map/chain_middle/pallas_call | solution.py:222
  48.1 0.7 collective-permute-start.11
  48.8 0.0 collective-permute-done.11.received_ref
  48.8 0.6 chain_last.1
  49.4 21.8 %all_to_all.10 = f32[32,16,128]{2,1,0:T(8,128)S(1)} all-to-all(f32[32,16,128]{2,1,0:T(8,128)S(1)} %bitcast.10), channel_id=1, replica_groups=mesh['y'=2,'core'=2,'z'=4,'x'=2] {'z','y','core','x'}, dimensions={0} | all-to-all | bytes 524288 | tf_op jit(solution)/shard_map/all_to_all | solution.py:283
  71.2 0.8 %turn.1 = f32[4,128,128]{2,1,0:T(8,128)} custom-call(f32[4,128,128]{2,1,0:T(8,128)S(1)} %bitcast.9), custom_call_target="tpu_custom_call" | custom-call | tf_op jit(solution)/shard_map/turn/pallas_call | solution.py:222
  (2 shorter events, 0.0 us)
Async XLA Ops:
  1.1 29.1 %copy-start.1 = (f32[8,64,256]{2,1,0:T(8,128)}, f32[8,64,256]{2,1,0:T(8,128)S(1)}, u32[]{:S(2)}) copy-start(f32[8,64,256]{2,1,0:T(8,128)S(1)} %pack.1.refs_0_) | copy-start | bytes 1572868
  1.1 29.1 %collective-permute-start.6 = (f32[8,64,256]{2,1,0:T(8,128)S(1)}, f32[8,64,256]{2,1,0:T(8,128)S(1)}, u32[]{:S(2)}, u32[]{:S(2)}) collective-permute-start(f32[8,64,256]{2,1,0:T(8,128)S(1)} %pack.1.refs_0_), channel_id=1, source_target_pairs={{0,8},{8,0},{1,9},{9,1},{2,10},{10,2},{3,11},{11,3},{4,12},{12,4},... | collective-permute-start | bytes 1572872 | tf_op jit(solution)/shard_map/ppermute | solution.py:249
  1.7 19.0 %collective-permute-start.1 = (f32[8,64,256]{2,1,0:T(8,128)S(1)}, f32[8,64,256]{2,1,0:T(8,128)S(1)}, u32[]{:S(2)}, u32[]{:S(2)}) collective-permute-start(f32[8,64,256]{2,1,0:T(8,128)S(1)} %pack.1.refs_0_), channel_id=1, source_target_pairs={{0,16},{16,0},{1,17},{17,1},{2,18},{18,2},{3,19},{19,3},{4,20},{20... | collective-permute-start | bytes 1572872 | tf_op jit(solution)/shard_map/ppermute | solution.py:248
  4.3 16.4 %collective-permute-start = (f32[8,64,256]{2,1,0:T(8,128)S(1)}, f32[8,64,256]{2,1,0:T(8,128)S(1)}, u32[]{:S(2)}, u32[]{:S(2)}) collective-permute-start(f32[8,64,256]{2,1,0:T(8,128)S(1)} %pack.1.refs_0_), channel_id=1, source_target_pairs={{0,1},{1,0},{2,3},{3,2},{4,5},{5,4},{6,7},{7,6},{8,9},{9,8},{10,11... | collective-permute-start | bytes 1572872 | tf_op jit(solution)/shard_map/ppermute | solution.py:247
  20.7 9.6 %copy-start.2 = (f32[8,64,256]{2,1,0:T(8,128)}, f32[8,64,256]{2,1,0:T(8,128)S(1)}, u32[]{:S(2)}) copy-start(f32[8,64,256]{2,1,0:T(8,128)S(1)} %collective-permute-done.1.refs_2_) | copy-start | bytes 1572868
  20.7 9.6 %copy-start.3 = (f32[8,64,256]{2,1,0:T(8,128)}, f32[8,64,256]{2,1,0:T(8,128)S(1)}, u32[]{:S(2)}) copy-start(f32[8,64,256]{2,1,0:T(8,128)S(1)} %collective-permute-done.refs_1_) | copy-start | bytes 1572868
  20.7 11.1 %collective-permute-start.8 = (f32[8,64,256]{2,1,0:T(8,128)S(1)}, f32[8,64,256]{2,1,0:T(8,128)}, u32[]{:S(2)}, u32[]{:S(2)}) collective-permute-start(f32[8,64,256]{2,1,0:T(8,128)S(1)} %collective-permute-done.1.refs_2_), channel_id=1, source_target_pairs={{0,8},{8,0},{1,9},{9,1},{2,10},{10,2},{3,11},{11,3},{4,12},{12,4},... | collective-permute-start | bytes 1572872 | tf_op jit(solution)/shard_map/ppermute | solution.py:259
  20.8 9.4 %collective-permute-start.7 = (f32[8,64,256]{2,1,0:T(8,128)S(1)}, f32[8,64,256]{2,1,0:T(8,128)S(1)}, u32[]{:S(2)}, u32[]{:S(2)}) collective-permute-start(f32[8,64,256]{2,1,0:T(8,128)S(1)} %collective-permute-done.refs_1_), channel_id=1, source_target_pairs={{0,8},{8,0},{1,9},{9,1},{2,10},{10,2},{3,11},{11,3},{4,12},{12,4},... | collective-permute-start | bytes 1572872 | tf_op jit(solution)/shard_map/ppermute | solution.py:259
  21.3 8.4 %collective-permute-start.3 = (f32[4,64,256]{2,1,0:T(8,128)S(1)}, f32[4,64,256]{2,1,0:T(8,128)}, u32[]{:S(2)}, u32[]{:S(2)}) collective-permute-start(f32[4,64,256]{2,1,0:T(8,128)S(1)} %slice.7), channel_id=1, source_target_pairs={{0,1},{1,0},{2,3},{3,2},{4,5},{5,4},{6,7},{7,6},{8,9},{9,8},{10,11... | collective-permute-start | bytes 786440 | tf_op jit(solution)/shard_map/ppermute | solution.py:258
  21.9 8.2 %collective-permute-start.2 = (f32[4,64,256]{2,1,0:T(8,128)S(1)}, f32[4,64,256]{2,1,0:T(8,128)}, u32[]{:S(2)}, u32[]{:S(2)}) collective-permute-start(f32[4,64,256]{2,1,0:T(8,128)S(1)} %slice.6), channel_id=1, source_target_pairs={{0,16},{16,0},{1,17},{17,1},{2,18},{18,2},{3,19},{19,3},{4,20},{20... | collective-permute-start | bytes 786440 | tf_op jit(solution)/shard_map/ppermute | solution.py:257
  22.0 17.0 %all-to-all-start = ((f32[32,16,128]{2,1,0:T(8,128)}), f32[32,16,128]{2,1,0:T(8,128)S(1)}, u32[]{:S(2)}, u32[]{:S(2)}) async-start(f32[32,16,128]{2,1,0:T(8,128)} %bitcast.3), calls=%async_computation | async-start | bytes 524288 | tf_op jit(solution)/shard_map/all_to_all | solution.py:260
  29.7 4.1 %collective-permute-start.5 = (f32[4,64,256]{2,1,0:T(8,128)}, f32[4,64,256]{2,1,0:T(8,128)S(1)}, u32[]{:S(2)}, u32[]{:S(2)}) collective-permute-start(f32[4,64,256]{2,1,0:T(8,128)} %collective-permute-done.3.refs_1_), channel_id=1, source_target_pairs={{0,8},{8,0},{1,9},{9,1},{2,10},{10,2},{3,11},{11,3},{4,12},{12,4},... | collective-permute-start | bytes 786440 | tf_op jit(solution)/shard_map/ppermute | solution.py:261
  30.1 3.7 %collective-permute-start.4 = (f32[4,64,256]{2,1,0:T(8,128)}, f32[4,64,256]{2,1,0:T(8,128)S(1)}, u32[]{:S(2)}, u32[]{:S(2)}) collective-permute-start(f32[4,64,256]{2,1,0:T(8,128)} %collective-permute-done.2.refs_0_), channel_id=1, source_target_pairs={{0,8},{8,0},{1,9},{9,1},{2,10},{10,2},{3,11},{11,3},{4,12},{12,4},... | collective-permute-start | bytes 786440 | tf_op jit(solution)/shard_map/ppermute | solution.py:261
  30.2 0.8 %copy-start.4 = (f32[8,64,256]{2,1,0:T(8,128)}, f32[8,64,256]{2,1,0:T(8,128)S(1)}, u32[]{:S(2)}) copy-start(f32[8,64,256]{2,1,0:T(8,128)S(1)} %collective-permute-done.6.refs_3_) | copy-start | bytes 1572868
  31.0 0.8 %copy-start.5 = (f32[8,64,256]{2,1,0:T(8,128)}, f32[8,64,256]{2,1,0:T(8,128)S(1)}, u32[]{:S(2)}) copy-start(f32[8,64,256]{2,1,0:T(8,128)S(1)} %collective-permute-done.7.refs_4_) | copy-start | bytes 1572868
  35.0 1.0 %copy-start = (bf16[2,512,512]{2,1,0:T(8,128)(2,1)}, bf16[2,512,512]{2,1,0:T(8,128)(2,1)S(1)}, u32[]{:S(2)}) copy-start(bf16[2,512,512]{2,1,0:T(8,128)(2,1)S(1)} %get-tuple-element.32.farthest_ref) | copy-start | bytes 3145732
  40.6 4.8 %collective-permute-start.9 = (f32[3,16,512]{2,1,0:T(8,128)S(1)}, f32[3,16,512]{2,1,0:T(8,128)S(1)}, u32[]{:S(2)}, u32[]{:S(2)}) collective-permute-start(f32[3,16,512]{2,1,0:T(8,128)S(1)} %get-tuple-element.34), channel_id=1, source_target_pairs={{0,2},{1,3},{8,10},{9,11},{16,18},{17,19},{24,26},{25,27}} | collective-permute-start | bytes 294920 | tf_op jit(solution)/shard_map/ppermute | solution.py:277
  46.6 0.7 collective-permute-start.10
  48.1 0.7 collective-permute-start.11

commit v5 on v4

--- a/solution.py
+++ b/solution.py
@@ -157,28 +157,40 @@
     )(*pieces, *weights)
 
 
-def apply(value, weight_ref, rows, columns):
+def product(left, right):
+    return dot_f32(left[0], right[0]) + (dot_f32(left[1], right[0]) + dot_f32(left[0], right[1]))
+
+
+def both_parts(weight_ref, rows=slice(0, SUPER), columns=slice(0, SUPER)):
+    return weight_ref[0, rows, columns], weight_ref[1, rows, columns]
+
+
+def invert(here_ref, out_ref):
+    top, bottom = slice(0, 256), slice(256, 512)
+    first, second = both_parts(here_ref, top, top), both_parts(here_ref, bottom, bottom)
+    below = halves(product(both_parts(here_ref, bottom, top), first))
+    corner = halves(-product(second, below))
+    for part in range(2):
+        out_ref[part, top, top] = first[part]
+        out_ref[part, top, bottom] = jnp.zeros((256, 256), BF16)
+        out_ref[part, bottom, top] = corner[part]
+        out_ref[part, bottom, bottom] = second[part]
+
+
+def combine(inverse_ref, near_ref, far_ref, *out_refs):
+    inverse = both_parts(inverse_ref)
+    for weight_ref, out_ref in zip((near_ref, far_ref), out_refs):
+        out_ref[0], out_ref[1] = halves(product(both_parts(weight_ref), inverse))
+
+
+def apply(value, weight_ref):
     high, low = halves(value)
-    both = jnp.concatenate([high, low], axis=0)
-    first = dot_rows(both, weight_ref[0, rows, columns])
     count = value.shape[0]
-    return first[:count] + first[count:] + dot_rows(high, weight_ref[1, rows, columns])
-
-
-def solve(residual, weight_ref):
-    top, bottom = slice(0, 256), slice(256, 512)
-    solved_top = apply(residual[:, :256], weight_ref, top, top)
-    rest = residual[:, 256:] - apply(solved_top, weight_ref, bottom, top)
-    return jnp.concatenate([solved_top, apply(rest, weight_ref, bottom, bottom)], axis=1)
-
-
-def push(solved, weight_refs, received_ref, out_ref):
-    for apart, weight_ref in enumerate(weight_refs, 1):
-        term = apply(solved, weight_ref, slice(0, SUPER), slice(0, SUPER))
-        out_ref[apart - 1] = term if received_ref is None else received_ref[apart] + term
-
-
-def chain_first(parts_ref, here_ref, near_ref, far_ref, farthest_ref, residual_ref, out_ref, held, sem):
+    first = dot_rows(jnp.concatenate([high, low], axis=0), weight_ref[0])
+    return first[:count] + first[count:] + dot_rows(high, weight_ref[1])
+
+
+def chain_first(parts_ref, inverse_ref, near_ref, far_ref, farthest_ref, residual_ref, out_ref, held, sem):
     fetch = pltpu.make_async_copy(farthest_ref, held, sem)
     fetch.start()
     by_rows = []
@@ -189,21 +201,23 @@
         by_rows.append(terms[0])
     residual = jnp.concatenate([t[:, :64] for t in by_rows] + [t[:, 64:] for t in by_rows], axis=1)
     residual_ref[...] = residual
-    solved = solve(residual, here_ref)
-    push(solved, (near_ref, far_ref), None, out_ref)
+    solved = apply(residual, inverse_ref)
+    out_ref[0] = apply(solved, near_ref)
+    out_ref[1] = apply(solved, far_ref)
     fetch.wait()
-    push(solved, (held,), None, out_ref.at[pl.ds(2, 1)])
+    out_ref[2] = apply(solved, held)
 
 
 def chain_middle(residual_ref, received_ref, *refs):
-    weight_refs, (next_ref, out_ref) = refs[:-2], refs[-2:]
+    combined_refs, (next_ref, out_ref) = refs[:-2], refs[-2:]
     residual = residual_ref[...] - received_ref[0]
     next_ref[...] = residual
-    push(solve(residual, weight_refs[0]), weight_refs[1:], received_ref, out_ref)
-
-
-def chain_last(residual_ref, received_ref, weight_ref, out_ref):
-    solved = solve(residual_ref[...] - received_ref[0], weight_ref)
+    for apart, combined_ref in enumerate(combined_refs):
+        out_ref[apart] = received_ref[apart + 1] + apply(residual, combined_ref)
+
+
+def chain_last(residual_ref, received_ref, inverse_ref, out_ref):
+    solved = apply(residual_ref[...] - received_ref[0], inverse_ref)
     for row_part in range(4):
         start = row_part * 64
         chunk = jnp.concatenate([solved[:, start : start + 64], solved[:, start + 256 : start + 320]], axis=1)
@@ -212,12 +226,17 @@
                 out_ref[z, row_part, x] = chunk
 
 
+def split(first_ref, second_ref, low_ref, high_ref):
+    low_ref[...] = first_ref[:4]
+    high_ref[...] = second_ref[4:]
+
+
 def turn(parts_ref, out_ref):
     for part in range(PLANES):
         out_ref[part] = parts_ref[part].T
 
 
-def call(kernel, name, outs, *args, large=(), scratch=()):
+def call(kernel, name, outs, *args, large=(), scratch=(), flops=None):
     in_vmem = pl.BlockSpec(memory_space=pltpu.VMEM)
     return pl.pallas_call(
         kernel,
@@ -226,6 +245,7 @@
         out_specs=[in_vmem] * len(outs),
         scratch_shapes=scratch,
         compiler_params=pltpu.CompilerParams(vmem_limit_bytes=8 << 20),
+        cost_estimate=flops and pl.CostEstimate(flops=flops, bytes_accessed=1 << 21, transcendentals=0),
         name=name,
     )(*args, *in_hbm(*large))
 
@@ -254,8 +274,9 @@
     parts = earlier_residual(first, factor, solved_prev, right)
 
     parts, from_x, from_y = lax.optimization_barrier((parts, from_x, from_y))
-    corner_low = swap(from_x[:4], "y")
-    corner_high = swap(from_y[4:], "x")
+    half = ((4, *lower_window.shape[1:]), F32)
+    low, high = call(split, "split", [half] * 2, from_x, from_y)
+    corner_low, corner_high = swap(low, "y"), swap(high, "x")
     core_x, core_y = swap(from_x, "core"), swap(from_y, "core")
     parts = lax.all_to_all(parts.reshape(32, RHS_PART, 128), EVERY, 0, 0, tiled=True)
     core_low, core_high = swap(corner_low, "core"), swap(corner_high, "core")
@@ -265,21 +286,31 @@
     pieces = (corner_low, corner_high, core_low, core_high)
     weights = arranged("arrange_corner", ((0, 1, 1, 0), (0, 1, 1, 4), (1, 1, 1, 0), (1, 1, 1, 4)), pieces, *weights)
 
+    here, near, far, farthest = weights
+    weight = ((2, SUPER, SUPER), BF16)
+    (inverse,) = call(invert, "invert", [weight], here, flops=6 * 256**3 * 2)
+
     def vectors(*counts):
         return ((*counts, RHS_PART, SUPER), F32)
 
     parts = parts.reshape(4, 4, 2, RHS_PART, 128)
     scratch = [pltpu.VMEM((2, SUPER, SUPER), BF16), pltpu.SemaphoreType.DMA]
     residual, sent = call(
-        chain_first, "chain_first", [vectors(), vectors(3)], parts, *weights[:3], large=weights[3:], scratch=scratch
+        chain_first,
+        "chain_first",
+        [vectors(), vectors(3)],
+        *(parts, inverse, near, far),
+        large=[farthest],
+        scratch=scratch,
     )
+    combined = call(combine, "combine", [weight] * 2, inverse, near, far, flops=6 * SUPER**3 * 2)
     for step in (1, 2):
         received = lax.ppermute(sent, "z", [(step - 1, step)])
         outs = [vectors(), vectors(3 - step)]
-        residual, sent = call(chain_middle, "chain_middle", outs, residual, received, *weights[: 4 - step])
+        residual, sent = call(chain_middle, "chain_middle", outs, residual, received, *combined[: 3 - step])
     received = lax.ppermute(sent, "z", [(2, 3)])
     chunk = ((4, 4, 2, RHS_PART, 128), F32)
-    (chunks,) = call(chain_last, "chain_last", [chunk], residual, received, weights[0])
+    (chunks,) = call(chain_last, "chain_last", [chunk], residual, received, inverse)
     solved = lax.all_to_all(chunks.reshape(32, RHS_PART, 128), EVERY, 0, 0, tiled=True)
     (result,) = call(turn, "turn", [((PLANES, 128, columns), F32)], solved.reshape(PLANES, columns, 128))
     return result.reshape(blocks, local_rows, columns)

time: 72.4 us -> 71.4 us (0.986)
  waiting for transfers between devices: 7.91 us -> 5.27 us
  Pallas kernels: 24.1 us -> 25.8 us
    ppermute x2, waiting for transfers between devices: 3.12 us -> 1.32 us  [local(): received = lax.ppermute(sent, 'z', [(step - 1, step)])]
    pallas_call x5 -> x8, Pallas kernels: 4.99 us -> 6.61 us  [call(): pl.pallas_call(kernel, out_shape=[jax.ShapeDtypeStruct(*o) for o in outs]...]
    all_to_all x1, waiting for transfers between devices: 3.02 us -> 2.21 us  [local(): lax.all_to_all(parts.reshape(32, RHS_PART, 128), EVERY, 0, 0, tiled=True)]
  transfers between devices with their start and end apart: 13 -> 13, of which waited for: 4 -> 4; matrix products, arithmetic and copies ran while one was open for 0% -> 0% of each run, Pallas kernels for 25% -> 29%
where the time goes in v5:
time: 71.4 us; the launch traced here: 71.1 us
  Pallas kernels  25.8 us (36%)
  blocking collectives  21.8 us (31%)
  starting transfers between devices  15.5 us (22%)
  waiting for transfers between devices  5.27 us (7%)
  local copies, waits for them, and re-layouts  2.61 us (4%)
    all_to_all x1, blocking collectives, local(): lax.all_to_all(chunks.reshape(32, RHS_PART, 128), EVERY, 0, 0, tiled=True)  21.8 us
    pallas_call x1, Pallas kernels, earlier_residual(): pl.pallas_call(functools.partial(earlier_sums, tile), out_shape=jax.Shape...  14.9 us
    pallas_call x8, Pallas kernels, call(): pl.pallas_call(kernel, out_shape=[jax.ShapeDtypeStruct(*o) for o in outs]...  6.61 us
    all_to_all x1, starting transfers between devices, local(): lax.all_to_all(parts.reshape(32, RHS_PART, 128), EVERY, 0, 0, tiled=True)  6.28 us
    pallas_call x2, Pallas kernels, arranged(): pl.pallas_call(functools.partial(arrange, spots, len(weights)), out_shape...  3.12 us
    unnamed x12, local copies, waits for them, and re-layouts  2.61 us
    ppermute x1, starting transfers between devices, local(): from_y = swap(message, 'y')  2.59 us
    ppermute x2, starting transfers between devices, local(): received = lax.ppermute(sent, 'z', [(step - 1, step)])  2.39 us
  transfers between devices with their start and end apart: 13, of which 4 were waited for; matrix products, arithmetic and copies ran while one was open for 0% of the time, Pallas kernels for 29%

profile of v5, /device:TPU:0, one launch (start us, length us, event | category | flops | bytes accessed | tf_op | source)
XLA Modules:
  0.0 71.1 jit_solution(12490011403606245913)
XLA Ops:
  0.0 1.1 %pack.1.refs_0_ = f32[8,64,256]{2,1,0:T(8,128)S(1)} custom-call(f32[8,64,256]{2,1,0:T(8,128)} %window_ref.1, f32[8,64,256]{2,1,0:T(8,128)} %inverse_ref.1), custom_call_target="tpu_custom_call" | custom-call | tf_op jit(solution)/shard_map/pack/pallas_call | solution.py:257
  1.1 0.0 copy-start.1
  1.1 0.5 collective-permute-start.6
  1.7 2.6 %collective-permute-start.1 = (f32[8,64,256]{2,1,0:T(8,128)S(1)}, f32[8,64,256]{2,1,0:T(8,128)S(1)}, u32[]{:S(2)}, u32[]{:S(2)}) collective-permute-start(f32[8,64,256]{2,1,0:T(8,128)S(1)} %pack.1.refs_0_), channel_id=1, source_target_pairs={{0,16},{16,0},{1,17},{17,1},{2,18},{18,2},{3,19},{19,3},{4,20},{20... | collective-permute-start | bytes 1572872 | tf_op jit(solution)/shard_map/ppermute | solution.py:268
  4.3 1.5 %collective-permute-start = (f32[8,64,256]{2,1,0:T(8,128)S(1)}, f32[8,64,256]{2,1,0:T(8,128)S(1)}, u32[]{:S(2)}, u32[]{:S(2)}) collective-permute-start(f32[8,64,256]{2,1,0:T(8,128)S(1)} %pack.1.refs_0_), channel_id=1, source_target_pairs={{0,1},{1,0},{2,3},{3,2},{4,5},{5,4},{6,7},{7,6},{8,9},{9,8},{10,11... | collective-permute-start | bytes 1572872 | tf_op jit(solution)/shard_map/ppermute | solution.py:267
  5.7 14.9 %earlier.1 = f32[4,128,128]{2,1,0:T(8,128)} custom-call(s32[1]{0:T(128)} %bitcast.first_ref, f32[512,16128]{1,0:T(8,128)} %bitcast.11, f32[16128,128]{1,0:T(8,128)} %solved_ref.1, f32[512,128]{1,0:T(8,128)} %bitcast.12), custom_call_target="tpu_custom_call" | custom-call | flops 8455716864 | bytes 41287680 | tf_op jit(solution)/shard_map/earlier/pallas_call | solution.py:87
  20.7 0.0 collective-permute-done.1.second_ref.refs_2_
  20.7 0.0 copy-start.2
  20.7 0.0 collective-permute-done.first_ref.refs_1_
  20.7 0.0 copy-start.3
  20.7 0.1 collective-permute-start.7
  20.8 0.6 collective-permute-start.8
  21.4 0.5 collective-permute-start.2
  21.9 0.1 collective-permute-start.3
  22.0 6.3 %all-to-all-start = ((f32[32,16,128]{2,1,0:T(8,128)}), f32[32,16,128]{2,1,0:T(8,128)S(1)}, u32[]{:S(2)}, u32[]{:S(2)}) async-start(f32[32,16,128]{2,1,0:T(8,128)} %bitcast.3), calls=%async_computation | async-start | bytes 524288 | tf_op jit(solution)/shard_map/all_to_all | solution.py:281
  28.3 1.5 %collective-permute-done.2.refs_0_ = f32[4,64,256]{2,1,0:T(8,128)} collective-permute-done((f32[4,64,256]{2,1,0:T(8,128)S(1)}, f32[4,64,256]{2,1,0:T(8,128)}, u32[]{:S(2)}, u32[]{:S(2)}) %collective-permute-start.2) | collective-permute-done | bytes 262176 | tf_op jit(solution)/shard_map/ppermute | solution.py:279
  29.8 0.0 collective-permute-start.4
  29.8 0.2 collective-permute-done.3.refs_1_
  30.0 0.3 collective-permute-start.5
  30.3 0.0 collective-permute-done.6.refs_3_
  30.3 0.0 copy-start.4
  30.3 0.0 collective-permute-done.7.refs_4_
  30.3 0.0 copy-done.3
  30.3 0.8 %copy-done.4 = f32[8,64,256]{2,1,0:T(8,128)} copy-done((f32[8,64,256]{2,1,0:T(8,128)}, f32[8,64,256]{2,1,0:T(8,128)S(1)}, u32[]{:S(2)}) %copy-start.4) | copy-done | bytes 524312
  31.1 0.0 copy-start.5
  31.1 0.8 %copy-done.5 = f32[8,64,256]{2,1,0:T(8,128)} copy-done((f32[8,64,256]{2,1,0:T(8,128)}, f32[8,64,256]{2,1,0:T(8,128)S(1)}, u32[]{:S(2)}) %copy-start.5) | copy-done | bytes 524312
  31.9 0.0 collective-permute-done.8.refs_5_
  31.9 0.0 copy-done.1
  31.9 0.0 copy-done.2
  31.9 1.9 %arrange.1 = (bf16[2,512,512]{2,1,0:T(8,128)(2,1)S(1)}, bf16[2,512,512]{2,1,0:T(8,128)(2,1)S(1)}, bf16[2,512,512]{2,1,0:T(8,128)(2,1)S(1)}, bf16[2,512,512]{2,1,0:T(8,128)(2,1)S(1)}) custom-call(f32[8,64,256]{2,1,0:T(8,128)} %copy-done.1, f32[8,64,256]{2,1,0:T(8,128)} %copy-done.3, f32[8,64,256]{2,1,0:T(8,128)} %copy-done.2, f32[8,64,256]{2,1,0:T(8,128)} %copy-done.4, ...), custom_call_target="tpu_custom_call" | custom-call | tf_op jit(solution)/shard_map/arrange/pallas_call | solution.py:148
  33.9 0.0 collective-permute-done.4.refs_2_
  33.9 0.0 collective-permute-done.5.refs_3_
  33.9 1.2 %arrange_corner.1 = (bf16[2,512,512]{2,1,0:T(8,128)(2,1)S(1)}, bf16[2,512,512]{2,1,0:T(8,128)(2,1)S(1)}, bf16[2,512,512]{2,1,0:T(8,128)(2,1)S(1)}, bf16[2,512,512]{2,1,0:T(8,128)(2,1)S(1)}) custom-call(f32[4,64,256]{2,1,0:T(8,128)} %collective-permute-done.2.refs_0_, ...), custom_call_target="tpu_custom_call", output_to_operand_aliasing={{0}: (4, {}), {1}: (5, {}), {2}: (6, {}), {3}: (7, {})} | custom-call | tf_op jit(solution)/shard_map/arrange_corner/pallas_call | solution.py:148
  35.1 0.0 copy-start
  35.1 1.0 %copy-done = bf16[2,512,512]{2,1,0:T(8,128)(2,1)} copy-done((bf16[2,512,512]{2,1,0:T(8,128)(2,1)}, bf16[2,512,512]{2,1,0:T(8,128)(2,1)S(1)}, u32[]{:S(2)}) %copy-start) | copy-done | bytes 1048600
  36.1 0.7 invert.1.inverse_ref
  36.8 2.2 %all-to-all-done = f32[32,16,128]{2,1,0:T(8,128)S(1)} async-done(((f32[32,16,128]{2,1,0:T(8,128)}), f32[32,16,128]{2,1,0:T(8,128)S(1)}, u32[]{:S(2)}, u32[]{:S(2)}) %all-to-all-start) | async-done | bytes 262176 | tf_op jit(solution)/shard_map/all_to_all | solution.py:281
  39.0 1.7 %chain_first.1 = (f32[16,512]{1,0:T(8,128)S(1)}, f32[3,16,512]{2,1,0:T(8,128)S(1)}) custom-call(f32[4,4,2,16,128]{4,3,2,1,0:T(8,128)S(1)} %bitcast.8, bf16[2,512,512]{2,1,0:T(8,128)(2,1)S(1)} %invert.1.inverse_ref, bf16[2,512,512]{2,1,0:T(8,128)(2,1)S(1)} %get-tuple-element.36.near_ref, bf16[2,512,512]{2,1,0:T(8,128)(2,1)S(1)} %get-tuple-element.37.far_ref, ...), custom_call_target="tpu_custom_call" | custom-call | tf_op jit(solution)/shard_map/chain_first/pallas_call | solution.py:241
  40.7 1.7 %collective-permute-start.9 = (f32[3,16,512]{2,1,0:T(8,128)S(1)}, f32[3,16,512]{2,1,0:T(8,128)S(1)}, u32[]{:S(2)}, u32[]{:S(2)}) collective-permute-start(f32[3,16,512]{2,1,0:T(8,128)S(1)} %get-tuple-element.40), channel_id=1, source_target_pairs={{0,2},{1,3},{8,10},{9,11},{16,18},{17,19},{24,26},{25,27}} | collective-permute-start | bytes 294920 | tf_op jit(solution)/shard_map/ppermute | solution.py:308
  42.5 1.8 %combine.1 = (bf16[2,512,512]{2,1,0:T(8,128)(2,1)S(1)}, bf16[2,512,512]{2,1,0:T(8,128)(2,1)S(1)}) custom-call(bf16[2,512,512]{2,1,0:T(8,128)(2,1)S(1)} %invert.1.inverse_ref, bf16[2,512,512]{2,1,0:T(8,128)(2,1)S(1)} %get-tuple-element.36.near_ref, bf16[2,512,512]{2,1,0:T(8,128)(2,1)S(1)} %get-tuple-element.37.far_ref), custom_call_target="tpu_custom_call" | custom-call | flops 1610612736 | bytes 2097152 | tf_op jit(solution)/shard_map/combine/pallas_call | solution.py:241
  44.3 1.3 %collective-permute-done.9.received_ref = f32[3,16,512]{2,1,0:T(8,128)S(1)} collective-permute-done((f32[3,16,512]{2,1,0:T(8,128)S(1)}, f32[3,16,512]{2,1,0:T(8,128)S(1)}, u32[]{:S(2)}, u32[]{:S(2)}) %collective-permute-start.9) | collective-permute-done | bytes 98336 | tf_op jit(solution)/shard_map/ppermute | solution.py:308
  45.6 0.7 chain_middle.2
  46.2 0.7 collective-permute-start.10
  46.9 0.0 collective-permute-done.10.received_ref
  46.9 0.4 chain_middle.3
  47.3 0.7 collective-permute-start.11
  48.0 0.0 collective-permute-done.11.received_ref
  48.0 0.5 chain_last.1
  48.5 21.8 %all_to_all.10 = f32[32,16,128]{2,1,0:T(8,128)S(1)} all-to-all(f32[32,16,128]{2,1,0:T(8,128)S(1)} %bitcast.10), channel_id=1, replica_groups=mesh['y'=2,'core'=2,'z'=4,'x'=2] {'z','y','core','x'}, dimensions={0} | all-to-all | bytes 524288 | tf_op jit(solution)/shard_map/all_to_all | solution.py:314
  70.3 0.8 %turn.1 = f32[4,128,128]{2,1,0:T(8,128)} custom-call(f32[4,128,128]{2,1,0:T(8,128)S(1)} %bitcast.9), custom_call_target="tpu_custom_call" | custom-call | tf_op jit(solution)/shard_map/turn/pallas_call | solution.py:241
  (1 shorter events, 0.0 us)
Async XLA Ops:
  1.1 30.8 %copy-start.1 = (f32[8,64,256]{2,1,0:T(8,128)}, f32[8,64,256]{2,1,0:T(8,128)S(1)}, u32[]{:S(2)}) copy-start(f32[8,64,256]{2,1,0:T(8,128)S(1)} %pack.1.refs_0_) | copy-start | bytes 1572868
  1.1 29.2 %collective-permute-start.6 = (f32[8,64,256]{2,1,0:T(8,128)S(1)}, f32[8,64,256]{2,1,0:T(8,128)S(1)}, u32[]{:S(2)}, u32[]{:S(2)}) collective-permute-start(f32[8,64,256]{2,1,0:T(8,128)S(1)} %pack.1.refs_0_), channel_id=1, source_target_pairs={{0,8},{8,0},{1,9},{9,1},{2,10},{10,2},{3,11},{11,3},{4,12},{12,4},... | collective-permute-start | bytes 1572872 | tf_op jit(solution)/shard_map/ppermute | solution.py:269
  1.7 19.0 %collective-permute-start.1 = (f32[8,64,256]{2,1,0:T(8,128)S(1)}, f32[8,64,256]{2,1,0:T(8,128)S(1)}, u32[]{:S(2)}, u32[]{:S(2)}) collective-permute-start(f32[8,64,256]{2,1,0:T(8,128)S(1)} %pack.1.refs_0_), channel_id=1, source_target_pairs={{0,16},{16,0},{1,17},{17,1},{2,18},{18,2},{3,19},{19,3},{4,20},{20... | collective-permute-start | bytes 1572872 | tf_op jit(solution)/shard_map/ppermute | solution.py:268
  4.3 16.4 %collective-permute-start = (f32[8,64,256]{2,1,0:T(8,128)S(1)}, f32[8,64,256]{2,1,0:T(8,128)S(1)}, u32[]{:S(2)}, u32[]{:S(2)}) collective-permute-start(f32[8,64,256]{2,1,0:T(8,128)S(1)} %pack.1.refs_0_), channel_id=1, source_target_pairs={{0,1},{1,0},{2,3},{3,2},{4,5},{5,4},{6,7},{7,6},{8,9},{9,8},{10,11... | collective-permute-start | bytes 1572872 | tf_op jit(solution)/shard_map/ppermute | solution.py:267
  20.7 11.2 %copy-start.2 = (f32[8,64,256]{2,1,0:T(8,128)}, f32[8,64,256]{2,1,0:T(8,128)S(1)}, u32[]{:S(2)}) copy-start(f32[8,64,256]{2,1,0:T(8,128)S(1)} %collective-permute-done.1.second_ref.refs_2_) | copy-start | bytes 1572868
  20.7 9.6 %copy-start.3 = (f32[8,64,256]{2,1,0:T(8,128)}, f32[8,64,256]{2,1,0:T(8,128)S(1)}, u32[]{:S(2)}) copy-start(f32[8,64,256]{2,1,0:T(8,128)S(1)} %collective-permute-done.first_ref.refs_1_) | copy-start | bytes 1572868
  20.7 9.6 %collective-permute-start.7 = (f32[8,64,256]{2,1,0:T(8,128)S(1)}, f32[8,64,256]{2,1,0:T(8,128)S(1)}, u32[]{:S(2)}, u32[]{:S(2)}) collective-permute-start(f32[8,64,256]{2,1,0:T(8,128)S(1)} %collective-permute-done.first_ref.refs_1_), channel_id=1, source_target_pairs={{0,8},{8,0},{1,9},{9,1},{2,10},{10,2},{3,11},{11,3},{4,12},{12,4},... | collective-permute-start | bytes 1572872 | tf_op jit(solution)/shard_map/ppermute | solution.py:280
  20.8 11.1 %collective-permute-start.8 = (f32[8,64,256]{2,1,0:T(8,128)S(1)}, f32[8,64,256]{2,1,0:T(8,128)}, u32[]{:S(2)}, u32[]{:S(2)}) collective-permute-start(f32[8,64,256]{2,1,0:T(8,128)S(1)} %collective-permute-done.1.second_ref.refs_2_), channel_id=1, source_target_pairs={{0,8},{8,0},{1,9},{9,1},{2,10},{10,2},{3,11},{11,3},{4,12},{12,4},... | collective-permute-start | bytes 1572872 | tf_op jit(solution)/shard_map/ppermute | solution.py:280
  21.4 8.4 %collective-permute-start.2 = (f32[4,64,256]{2,1,0:T(8,128)S(1)}, f32[4,64,256]{2,1,0:T(8,128)}, u32[]{:S(2)}, u32[]{:S(2)}) collective-permute-start(f32[4,64,256]{2,1,0:T(8,128)S(1)} %get-tuple-element.29), channel_id=1, source_target_pairs={{0,16},{16,0},{1,17},{17,1},{2,18},{18,2},{3,19},{19,3},{4,20},{20... | collective-permute-start | bytes 786440 | tf_op jit(solution)/shard_map/ppermute | solution.py:279
  21.9 8.1 %collective-permute-start.3 = (f32[4,64,256]{2,1,0:T(8,128)S(1)}, f32[4,64,256]{2,1,0:T(8,128)}, u32[]{:S(2)}, u32[]{:S(2)}) collective-permute-start(f32[4,64,256]{2,1,0:T(8,128)S(1)} %get-tuple-element.30), channel_id=1, source_target_pairs={{0,1},{1,0},{2,3},{3,2},{4,5},{5,4},{6,7},{7,6},{8,9},{9,8},{10,11... | collective-permute-start | bytes 786440 | tf_op jit(solution)/shard_map/ppermute | solution.py:279
  22.0 17.0 %all-to-all-start = ((f32[32,16,128]{2,1,0:T(8,128)}), f32[32,16,128]{2,1,0:T(8,128)S(1)}, u32[]{:S(2)}, u32[]{:S(2)}) async-start(f32[32,16,128]{2,1,0:T(8,128)} %bitcast.3), calls=%async_computation | async-start | bytes 524288 | tf_op jit(solution)/shard_map/all_to_all | solution.py:281
  29.8 4.1 %collective-permute-start.4 = (f32[4,64,256]{2,1,0:T(8,128)}, f32[4,64,256]{2,1,0:T(8,128)S(1)}, u32[]{:S(2)}, u32[]{:S(2)}) collective-permute-start(f32[4,64,256]{2,1,0:T(8,128)} %collective-permute-done.2.refs_0_), channel_id=1, source_target_pairs={{0,8},{8,0},{1,9},{9,1},{2,10},{10,2},{3,11},{11,3},{4,12},{12,4},... | collective-permute-start | bytes 786440 | tf_op jit(solution)/shard_map/ppermute | solution.py:282
  30.0 3.9 %collective-permute-start.5 = (f32[4,64,256]{2,1,0:T(8,128)}, f32[4,64,256]{2,1,0:T(8,128)S(1)}, u32[]{:S(2)}, u32[]{:S(2)}) collective-permute-start(f32[4,64,256]{2,1,0:T(8,128)} %collective-permute-done.3.refs_1_), channel_id=1, source_target_pairs={{0,8},{8,0},{1,9},{9,1},{2,10},{10,2},{3,11},{11,3},{4,12},{12,4},... | collective-permute-start | bytes 786440 | tf_op jit(solution)/shard_map/ppermute | solution.py:282
  30.3 0.8 %copy-start.4 = (f32[8,64,256]{2,1,0:T(8,128)}, f32[8,64,256]{2,1,0:T(8,128)S(1)}, u32[]{:S(2)}) copy-start(f32[8,64,256]{2,1,0:T(8,128)S(1)} %collective-permute-done.6.refs_3_) | copy-start | bytes 1572868
  31.1 0.8 %copy-start.5 = (f32[8,64,256]{2,1,0:T(8,128)}, f32[8,64,256]{2,1,0:T(8,128)S(1)}, u32[]{:S(2)}) copy-start(f32[8,64,256]{2,1,0:T(8,128)S(1)} %collective-permute-done.7.refs_4_) | copy-start | bytes 1572868
  35.1 1.0 %copy-start = (bf16[2,512,512]{2,1,0:T(8,128)(2,1)}, bf16[2,512,512]{2,1,0:T(8,128)(2,1)S(1)}, u32[]{:S(2)}) copy-start(bf16[2,512,512]{2,1,0:T(8,128)(2,1)S(1)} %get-tuple-element.38.farthest_ref) | copy-start | bytes 3145732
  40.7 4.8 %collective-permute-start.9 = (f32[3,16,512]{2,1,0:T(8,128)S(1)}, f32[3,16,512]{2,1,0:T(8,128)S(1)}, u32[]{:S(2)}, u32[]{:S(2)}) collective-permute-start(f32[3,16,512]{2,1,0:T(8,128)S(1)} %get-tuple-element.40), channel_id=1, source_target_pairs={{0,2},{1,3},{8,10},{9,11},{16,18},{17,19},{24,26},{25,27}} | collective-permute-start | bytes 294920 | tf_op jit(solution)/shard_map/ppermute | solution.py:308
  46.2 0.7 collective-permute-start.10
  47.3 0.7 collective-permute-start.11

commit v6 on v5

--- a/solution.py
+++ b/solution.py
@@ -190,9 +190,7 @@
     return first[:count] + first[count:] + dot_rows(high, weight_ref[1])
 
 
-def chain_first(parts_ref, inverse_ref, near_ref, far_ref, farthest_ref, residual_ref, out_ref, held, sem):
-    fetch = pltpu.make_async_copy(farthest_ref, held, sem)
-    fetch.start()
+def chain_first(parts_ref, inverse_ref, near_ref, far_ref, residual_ref, solved_ref, out_ref):
     by_rows = []
     for row_part in range(4):
         terms = [parts_ref[z, row_part, x] for z in range(PLANES) for x in range(2)]
@@ -202,10 +200,16 @@
     residual = jnp.concatenate([t[:, :64] for t in by_rows] + [t[:, 64:] for t in by_rows], axis=1)
     residual_ref[...] = residual
     solved = apply(residual, inverse_ref)
+    solved_ref[...] = solved
     out_ref[0] = apply(solved, near_ref)
     out_ref[1] = apply(solved, far_ref)
+
+
+def chain_direct(solved_ref, farthest_ref, out_ref, held, sem):
+    fetch = pltpu.make_async_copy(farthest_ref, held, sem)
+    fetch.start()
     fetch.wait()
-    out_ref[2] = apply(solved, held)
+    out_ref[...] = apply(solved_ref[...], held)
 
 
 def chain_middle(residual_ref, received_ref, *refs):
@@ -213,11 +217,12 @@
     residual = residual_ref[...] - received_ref[0]
     next_ref[...] = residual
     for apart, combined_ref in enumerate(combined_refs):
-        out_ref[apart] = received_ref[apart + 1] + apply(residual, combined_ref)
-
-
-def chain_last(residual_ref, received_ref, inverse_ref, out_ref):
-    solved = apply(residual_ref[...] - received_ref[0], inverse_ref)
+        term = apply(residual, combined_ref)
+        out_ref[apart] = received_ref[1] + term if apart == 0 else term
+
+
+def chain_last(residual_ref, received_ref, direct_ref, inverse_ref, out_ref):
+    solved = apply(residual_ref[...] - (received_ref[0] + direct_ref[...]), inverse_ref)
     for row_part in range(4):
         start = row_part * 64
         chunk = jnp.concatenate([solved[:, start : start + 64], solved[:, start + 256 : start + 320]], axis=1)
@@ -295,14 +300,12 @@
 
     parts = parts.reshape(4, 4, 2, RHS_PART, 128)
     scratch = [pltpu.VMEM((2, SUPER, SUPER), BF16), pltpu.SemaphoreType.DMA]
-    residual, sent = call(
-        chain_first,
-        "chain_first",
-        [vectors(), vectors(3)],
-        *(parts, inverse, near, far),
-        large=[farthest],
-        scratch=scratch,
+    outs = [vectors(), vectors(), vectors(2)]
+    residual, solved, sent = call(chain_first, "chain_first", outs, parts, inverse, near, far)
+    (direct,) = call(
+        chain_direct, "chain_direct", [vectors()], solved, large=[farthest], scratch=scratch, flops=6 * 16 * SUPER**2
     )
+    direct = lax.ppermute(direct, "z", [(0, 3)])
     combined = call(combine, "combine", [weight] * 2, inverse, near, far, flops=6 * SUPER**3 * 2)
     for step in (1, 2):
         received = lax.ppermute(sent, "z", [(step - 1, step)])
@@ -310,7 +313,7 @@
         residual, sent = call(chain_middle, "chain_middle", outs, residual, received, *combined[: 3 - step])
     received = lax.ppermute(sent, "z", [(2, 3)])
     chunk = ((4, 4, 2, RHS_PART, 128), F32)
-    (chunks,) = call(chain_last, "chain_last", [chunk], residual, received, inverse)
+    (chunks,) = call(chain_last, "chain_last", [chunk], residual, received, direct, inverse)
     solved = lax.all_to_all(chunks.reshape(32, RHS_PART, 128), EVERY, 0, 0, tiled=True)
     (result,) = call(turn, "turn", [((PLANES, 128, columns), F32)], solved.reshape(PLANES, columns, 128))
     return result.reshape(blocks, local_rows, columns)

time: 71.4 us -> 70.7 us (level)
  blocking collectives: 21.8 us -> 18.7 us
  starting transfers between devices: 15.5 us -> 17.1 us
  Pallas kernels: 25.8 us -> 26.7 us
    all_to_all x1, blocking collectives: 21.8 us -> 18.7 us  [local(): lax.all_to_all(chunks.reshape(32, RHS_PART, 128), EVERY, 0, 0, tiled=True)]
    ppermute x0 -> x1, starting transfers between devices: none -> 1.64 us  [local(): direct = lax.ppermute(direct, 'z', [(0, 3)])]
    pallas_call x8 -> x9, Pallas kernels: 6.61 us -> 7.51 us  [call(): pl.pallas_call(kernel, out_shape=[jax.ShapeDtypeStruct(*o) for o in outs]...]
  transfers between devices with their start and end apart: 13 -> 14, of which waited for: 4 -> 5; matrix products, arithmetic and copies ran while one was open for 0% -> 0% of each run, Pallas kernels for 29% -> 32%
where the time goes in v6:
time: 70.7 us; the launch traced here: 70.4 us
  Pallas kernels  26.7 us (38%)
  blocking collectives  18.7 us (26%)
  starting transfers between devices  17.1 us (24%)
  waiting for transfers between devices  5.09 us (7%)
  local copies, waits for them, and re-layouts  2.59 us (4%)
    all_to_all x1, blocking collectives, local(): lax.all_to_all(chunks.reshape(32, RHS_PART, 128), EVERY, 0, 0, tiled=True)  18.7 us
    pallas_call x1, Pallas kernels, earlier_residual(): pl.pallas_call(functools.partial(earlier_sums, tile), out_shape=jax.Shape...  14.9 us
    pallas_call x9, Pallas kernels, call(): pl.pallas_call(kernel, out_shape=[jax.ShapeDtypeStruct(*o) for o in outs]...  7.51 us
    all_to_all x1, starting transfers between devices, local(): lax.all_to_all(parts.reshape(32, RHS_PART, 128), EVERY, 0, 0, tiled=True)  6.28 us
    pallas_call x2, Pallas kernels, arranged(): pl.pallas_call(functools.partial(arrange, spots, len(weights)), out_shape...  3.12 us
    unnamed x12, local copies, waits for them, and re-layouts  2.59 us
    ppermute x1, starting transfers between devices, local(): from_y = swap(message, 'y')  2.59 us
    ppermute x2, starting transfers between devices, local(): received = lax.ppermute(sent, 'z', [(step - 1, step)])  2.4 us
  transfers between devices with their start and end apart: 14, of which 5 were waited for; matrix products, arithmetic and copies ran while one was open for 0% of the time, Pallas kernels for 32%

profile of v6, /device:TPU:0, one launch (start us, length us, event | category | flops | bytes accessed | tf_op | source)
XLA Modules:
  0.0 70.4 jit_solution(7002224390915242777)
XLA Ops:
  0.0 1.1 %pack.1.refs_0_ = f32[8,64,256]{2,1,0:T(8,128)S(1)} custom-call(f32[8,64,256]{2,1,0:T(8,128)} %window_ref.1, f32[8,64,256]{2,1,0:T(8,128)} %inverse_ref.1), custom_call_target="tpu_custom_call" | custom-call | tf_op jit(solution)/shard_map/pack/pallas_call | solution.py:262
  1.1 0.0 copy-start.1
  1.1 0.5 collective-permute-start.6
  1.7 2.6 %collective-permute-start.1 = (f32[8,64,256]{2,1,0:T(8,128)S(1)}, f32[8,64,256]{2,1,0:T(8,128)S(1)}, u32[]{:S(2)}, u32[]{:S(2)}) collective-permute-start(f32[8,64,256]{2,1,0:T(8,128)S(1)} %pack.1.refs_0_), channel_id=1, source_target_pairs={{0,16},{16,0},{1,17},{17,1},{2,18},{18,2},{3,19},{19,3},{4,20},{20... | collective-permute-start | bytes 1572872 | tf_op jit(solution)/shard_map/ppermute | solution.py:273
  4.3 1.5 %collective-permute-start = (f32[8,64,256]{2,1,0:T(8,128)S(1)}, f32[8,64,256]{2,1,0:T(8,128)S(1)}, u32[]{:S(2)}, u32[]{:S(2)}) collective-permute-start(f32[8,64,256]{2,1,0:T(8,128)S(1)} %pack.1.refs_0_), channel_id=1, source_target_pairs={{0,1},{1,0},{2,3},{3,2},{4,5},{5,4},{6,7},{7,6},{8,9},{9,8},{10,11... | collective-permute-start | bytes 1572872 | tf_op jit(solution)/shard_map/ppermute | solution.py:272
  5.7 14.9 %earlier.1 = f32[4,128,128]{2,1,0:T(8,128)} custom-call(s32[1]{0:T(128)} %bitcast.first_ref, f32[512,16128]{1,0:T(8,128)} %bitcast.11, f32[16128,128]{1,0:T(8,128)} %solved_ref.1, f32[512,128]{1,0:T(8,128)} %bitcast.12), custom_call_target="tpu_custom_call" | custom-call | flops 8455716864 | bytes 41287680 | tf_op jit(solution)/shard_map/earlier/pallas_call | solution.py:87
  20.7 0.0 collective-permute-done.1.second_ref.refs_2_
  20.7 0.0 copy-start.2
  20.7 0.0 collective-permute-done.first_ref.refs_1_
  20.7 0.0 copy-start.3
  20.7 0.1 collective-permute-start.7
  20.8 0.6 collective-permute-start.8
  21.4 0.5 collective-permute-start.2
  21.9 0.1 collective-permute-start.3
  22.0 6.3 %all-to-all-start = ((f32[32,16,128]{2,1,0:T(8,128)}), f32[32,16,128]{2,1,0:T(8,128)S(1)}, u32[]{:S(2)}, u32[]{:S(2)}) async-start(f32[32,16,128]{2,1,0:T(8,128)} %bitcast.3), calls=%async_computation | async-start | bytes 524288 | tf_op jit(solution)/shard_map/all_to_all | solution.py:286
  28.3 1.5 %collective-permute-done.2.refs_0_ = f32[4,64,256]{2,1,0:T(8,128)} collective-permute-done((f32[4,64,256]{2,1,0:T(8,128)S(1)}, f32[4,64,256]{2,1,0:T(8,128)}, u32[]{:S(2)}, u32[]{:S(2)}) %collective-permute-start.2) | collective-permute-done | bytes 262176 | tf_op jit(solution)/shard_map/ppermute | solution.py:284
  29.8 0.0 collective-permute-start.4
  29.8 0.2 collective-permute-done.3.refs_1_
  30.0 0.3 collective-permute-start.5
  30.3 0.0 collective-permute-done.6.refs_3_
  30.3 0.0 copy-start.4
  30.3 0.0 collective-permute-done.7.refs_4_
  30.3 0.0 copy-done.3
  30.3 0.8 %copy-done.4 = f32[8,64,256]{2,1,0:T(8,128)} copy-done((f32[8,64,256]{2,1,0:T(8,128)}, f32[8,64,256]{2,1,0:T(8,128)S(1)}, u32[]{:S(2)}) %copy-start.4) | copy-done | bytes 524312
  31.1 0.0 copy-start.5
  31.1 0.8 %copy-done.5 = f32[8,64,256]{2,1,0:T(8,128)} copy-done((f32[8,64,256]{2,1,0:T(8,128)}, f32[8,64,256]{2,1,0:T(8,128)S(1)}, u32[]{:S(2)}) %copy-start.5) | copy-done | bytes 524312
  31.9 0.0 collective-permute-done.8.refs_5_
  31.9 0.0 copy-done.1
  31.9 0.0 copy-done.2
  31.9 1.9 %arrange.1 = (bf16[2,512,512]{2,1,0:T(8,128)(2,1)S(1)}, bf16[2,512,512]{2,1,0:T(8,128)(2,1)S(1)}, bf16[2,512,512]{2,1,0:T(8,128)(2,1)S(1)}, bf16[2,512,512]{2,1,0:T(8,128)(2,1)S(1)}) custom-call(f32[8,64,256]{2,1,0:T(8,128)} %copy-done.1, f32[8,64,256]{2,1,0:T(8,128)} %copy-done.3, f32[8,64,256]{2,1,0:T(8,128)} %copy-done.2, f32[8,64,256]{2,1,0:T(8,128)} %copy-done.4, ...), custom_call_target="tpu_custom_call" | custom-call | tf_op jit(solution)/shard_map/arrange/pallas_call | solution.py:148
  33.9 0.0 collective-permute-done.4.refs_2_
  33.9 0.0 collective-permute-done.5.refs_3_
  33.9 1.2 %arrange_corner.1 = (bf16[2,512,512]{2,1,0:T(8,128)(2,1)S(1)}, bf16[2,512,512]{2,1,0:T(8,128)(2,1)S(1)}, bf16[2,512,512]{2,1,0:T(8,128)(2,1)S(1)}, bf16[2,512,512]{2,1,0:T(8,128)(2,1)S(1)}) custom-call(f32[4,64,256]{2,1,0:T(8,128)} %collective-permute-done.2.refs_0_, ...), custom_call_target="tpu_custom_call", output_to_operand_aliasing={{0}: (4, {}), {1}: (5, {}), {2}: (6, {}), {3}: (7, {})} | custom-call | tf_op jit(solution)/shard_map/arrange_corner/pallas_call | solution.py:148
  35.1 0.0 copy-start
  35.1 1.0 %copy-done = bf16[2,512,512]{2,1,0:T(8,128)(2,1)} copy-done((bf16[2,512,512]{2,1,0:T(8,128)(2,1)}, bf16[2,512,512]{2,1,0:T(8,128)(2,1)S(1)}, u32[]{:S(2)}) %copy-start) | copy-done | bytes 1048600
  36.1 0.7 invert.1.inverse_ref
  36.8 2.2 %all-to-all-done = f32[32,16,128]{2,1,0:T(8,128)S(1)} async-done(((f32[32,16,128]{2,1,0:T(8,128)}), f32[32,16,128]{2,1,0:T(8,128)S(1)}, u32[]{:S(2)}, u32[]{:S(2)}) %all-to-all-start) | async-done | bytes 262176 | tf_op jit(solution)/shard_map/all_to_all | solution.py:286
  39.0 1.0 %chain_first.1 = (f32[16,512]{1,0:T(8,128)S(1)}, f32[16,512]{1,0:T(8,128)S(1)}, f32[2,16,512]{2,1,0:T(8,128)S(1)}) custom-call(f32[4,4,2,16,128]{4,3,2,1,0:T(8,128)S(1)} %bitcast.10, bf16[2,512,512]{2,1,0:T(8,128)(2,1)S(1)} %invert.1.inverse_ref, bf16[2,512,512]{2,1,0:T(8,128)(2,1)S(1)} %get-tuple-element.37.near_ref, ...), custom_call_target="tpu_custom_call" | custom-call | tf_op jit(solution)/shard_map/chain_first/pallas_call | solution.py:246
  40.0 1.7 %collective-permute-start.9 = (f32[2,16,512]{2,1,0:T(8,128)S(1)}, f32[2,16,512]{2,1,0:T(8,128)S(1)}, u32[]{:S(2)}, u32[]{:S(2)}) collective-permute-start(f32[2,16,512]{2,1,0:T(8,128)S(1)} %get-tuple-element.40), channel_id=1, source_target_pairs={{0,2},{1,3},{8,10},{9,11},{16,18},{17,19},{24,26},{25,27}} | collective-permute-start | bytes 196616 | tf_op jit(solution)/shard_map/ppermute | solution.py:311
  41.7 1.8 %combine.1 = (bf16[2,512,512]{2,1,0:T(8,128)(2,1)S(1)}, bf16[2,512,512]{2,1,0:T(8,128)(2,1)S(1)}) custom-call(bf16[2,512,512]{2,1,0:T(8,128)(2,1)S(1)} %invert.1.inverse_ref, bf16[2,512,512]{2,1,0:T(8,128)(2,1)S(1)} %get-tuple-element.37.near_ref, bf16[2,512,512]{2,1,0:T(8,128)(2,1)S(1)} %get-tuple-element.38.far_ref), custom_call_target="tpu_custom_call" | custom-call | flops 1610612736 | bytes 2097152 | tf_op jit(solution)/shard_map/combine/pallas_call | solution.py:246
  43.5 0.6 collective-permute-done.9.received_ref
  44.2 0.7 chain_middle.2
  44.8 0.7 collective-permute-start.10
  45.5 1.6 %chain_direct.1 = f32[16,512]{1,0:T(8,128)S(1)} custom-call(f32[16,512]{1,0:T(8,128)S(1)} %get-tuple-element.47.solved_ref, bf16[2,512,512]{2,1,0:T(8,128)(2,1)} %copy-done), custom_call_target="tpu_custom_call" | custom-call | flops 25165824 | bytes 2097152 | tf_op jit(solution)/shard_map/chain_direct/pallas_call | solution.py:246
  47.1 1.6 %collective-permute-start.12 = (f32[16,512]{1,0:T(8,128)S(1)}, f32[16,512]{1,0:T(8,128)S(1)}, u32[]{:S(2)}, u32[]{:S(2)}) collective-permute-start(f32[16,512]{1,0:T(8,128)S(1)} %chain_direct.1), channel_id=1, source_target_pairs={{0,6},{1,7},{8,14},{9,15},{16,22},{17,23},{24,30},{25,31}} | collective-permute-start | bytes 98312 | tf_op jit(solution)/shard_map/ppermute | solution.py:308
  48.8 0.0 collective-permute-done.10.received_ref
  48.8 0.4 chain_middle.3
  49.2 0.7 collective-permute-start.11
  49.9 0.5 collective-permute-done.12.direct_ref
  50.4 0.0 collective-permute-done.11.received_ref
  50.4 0.5 chain_last.1
  50.9 18.7 %all_to_all.10 = f32[32,16,128]{2,1,0:T(8,128)S(1)} all-to-all(f32[32,16,128]{2,1,0:T(8,128)S(1)} %bitcast.9), channel_id=1, replica_groups=mesh['y'=2,'core'=2,'z'=4,'x'=2] {'z','y','core','x'}, dimensions={0} | all-to-all | bytes 524288 | tf_op jit(solution)/shard_map/all_to_all | solution.py:317
  69.5 0.8 %turn.1 = f32[4,128,128]{2,1,0:T(8,128)} custom-call(f32[4,128,128]{2,1,0:T(8,128)S(1)} %bitcast.8), custom_call_target="tpu_custom_call" | custom-call | tf_op jit(solution)/shard_map/turn/pallas_call | solution.py:246
  (1 shorter events, 0.0 us)
Async XLA Ops:
  1.1 30.8 %copy-start.1 = (f32[8,64,256]{2,1,0:T(8,128)}, f32[8,64,256]{2,1,0:T(8,128)S(1)}, u32[]{:S(2)}) copy-start(f32[8,64,256]{2,1,0:T(8,128)S(1)} %pack.1.refs_0_) | copy-start | bytes 1572868
  1.1 29.2 %collective-permute-start.6 = (f32[8,64,256]{2,1,0:T(8,128)S(1)}, f32[8,64,256]{2,1,0:T(8,128)S(1)}, u32[]{:S(2)}, u32[]{:S(2)}) collective-permute-start(f32[8,64,256]{2,1,0:T(8,128)S(1)} %pack.1.refs_0_), channel_id=1, source_target_pairs={{0,8},{8,0},{1,9},{9,1},{2,10},{10,2},{3,11},{11,3},{4,12},{12,4},... | collective-permute-start | bytes 1572872 | tf_op jit(solution)/shard_map/ppermute | solution.py:274
  1.7 19.0 %collective-permute-start.1 = (f32[8,64,256]{2,1,0:T(8,128)S(1)}, f32[8,64,256]{2,1,0:T(8,128)S(1)}, u32[]{:S(2)}, u32[]{:S(2)}) collective-permute-start(f32[8,64,256]{2,1,0:T(8,128)S(1)} %pack.1.refs_0_), channel_id=1, source_target_pairs={{0,16},{16,0},{1,17},{17,1},{2,18},{18,2},{3,19},{19,3},{4,20},{20... | collective-permute-start | bytes 1572872 | tf_op jit(solution)/shard_map/ppermute | solution.py:273
  4.3 16.4 %collective-permute-start = (f32[8,64,256]{2,1,0:T(8,128)S(1)}, f32[8,64,256]{2,1,0:T(8,128)S(1)}, u32[]{:S(2)}, u32[]{:S(2)}) collective-permute-start(f32[8,64,256]{2,1,0:T(8,128)S(1)} %pack.1.refs_0_), channel_id=1, source_target_pairs={{0,1},{1,0},{2,3},{3,2},{4,5},{5,4},{6,7},{7,6},{8,9},{9,8},{10,11... | collective-permute-start | bytes 1572872 | tf_op jit(solution)/shard_map/ppermute | solution.py:272
  20.7 11.2 %copy-start.2 = (f32[8,64,256]{2,1,0:T(8,128)}, f32[8,64,256]{2,1,0:T(8,128)S(1)}, u32[]{:S(2)}) copy-start(f32[8,64,256]{2,1,0:T(8,128)S(1)} %collective-permute-done.1.second_ref.refs_2_) | copy-start | bytes 1572868
  20.7 9.6 %copy-start.3 = (f32[8,64,256]{2,1,0:T(8,128)}, f32[8,64,256]{2,1,0:T(8,128)S(1)}, u32[]{:S(2)}) copy-start(f32[8,64,256]{2,1,0:T(8,128)S(1)} %collective-permute-done.first_ref.refs_1_) | copy-start | bytes 1572868
  20.7 9.6 %collective-permute-start.7 = (f32[8,64,256]{2,1,0:T(8,128)S(1)}, f32[8,64,256]{2,1,0:T(8,128)S(1)}, u32[]{:S(2)}, u32[]{:S(2)}) collective-permute-start(f32[8,64,256]{2,1,0:T(8,128)S(1)} %collective-permute-done.first_ref.refs_1_), channel_id=1, source_target_pairs={{0,8},{8,0},{1,9},{9,1},{2,10},{10,2},{3,11},{11,3},{4,12},{12,4},... | collective-permute-start | bytes 1572872 | tf_op jit(solution)/shard_map/ppermute | solution.py:285
  20.8 11.1 %collective-permute-start.8 = (f32[8,64,256]{2,1,0:T(8,128)S(1)}, f32[8,64,256]{2,1,0:T(8,128)}, u32[]{:S(2)}, u32[]{:S(2)}) collective-permute-start(f32[8,64,256]{2,1,0:T(8,128)S(1)} %collective-permute-done.1.second_ref.refs_2_), channel_id=1, source_target_pairs={{0,8},{8,0},{1,9},{9,1},{2,10},{10,2},{3,11},{11,3},{4,12},{12,4},... | collective-permute-start | bytes 1572872 | tf_op jit(solution)/shard_map/ppermute | solution.py:285
  21.4 8.4 %collective-permute-start.2 = (f32[4,64,256]{2,1,0:T(8,128)S(1)}, f32[4,64,256]{2,1,0:T(8,128)}, u32[]{:S(2)}, u32[]{:S(2)}) collective-permute-start(f32[4,64,256]{2,1,0:T(8,128)S(1)} %get-tuple-element.30), channel_id=1, source_target_pairs={{0,16},{16,0},{1,17},{17,1},{2,18},{18,2},{3,19},{19,3},{4,20},{20... | collective-permute-start | bytes 786440 | tf_op jit(solution)/shard_map/ppermute | solution.py:284
  21.9 8.1 %collective-permute-start.3 = (f32[4,64,256]{2,1,0:T(8,128)S(1)}, f32[4,64,256]{2,1,0:T(8,128)}, u32[]{:S(2)}, u32[]{:S(2)}) collective-permute-start(f32[4,64,256]{2,1,0:T(8,128)S(1)} %get-tuple-element.31), channel_id=1, source_target_pairs={{0,1},{1,0},{2,3},{3,2},{4,5},{5,4},{6,7},{7,6},{8,9},{9,8},{10,11... | collective-permute-start | bytes 786440 | tf_op jit(solution)/shard_map/ppermute | solution.py:284
  22.0 17.0 %all-to-all-start = ((f32[32,16,128]{2,1,0:T(8,128)}), f32[32,16,128]{2,1,0:T(8,128)S(1)}, u32[]{:S(2)}, u32[]{:S(2)}) async-start(f32[32,16,128]{2,1,0:T(8,128)} %bitcast.3), calls=%async_computation | async-start | bytes 524288 | tf_op jit(solution)/shard_map/all_to_all | solution.py:286
  29.8 4.1 %collective-permute-start.4 = (f32[4,64,256]{2,1,0:T(8,128)}, f32[4,64,256]{2,1,0:T(8,128)S(1)}, u32[]{:S(2)}, u32[]{:S(2)}) collective-permute-start(f32[4,64,256]{2,1,0:T(8,128)} %collective-permute-done.2.refs_0_), channel_id=1, source_target_pairs={{0,8},{8,0},{1,9},{9,1},{2,10},{10,2},{3,11},{11,3},{4,12},{12,4},... | collective-permute-start | bytes 786440 | tf_op jit(solution)/shard_map/ppermute | solution.py:287
  30.0 3.9 %collective-permute-start.5 = (f32[4,64,256]{2,1,0:T(8,128)}, f32[4,64,256]{2,1,0:T(8,128)S(1)}, u32[]{:S(2)}, u32[]{:S(2)}) collective-permute-start(f32[4,64,256]{2,1,0:T(8,128)} %collective-permute-done.3.refs_1_), channel_id=1, source_target_pairs={{0,8},{8,0},{1,9},{9,1},{2,10},{10,2},{3,11},{11,3},{4,12},{12,4},... | collective-permute-start | bytes 786440 | tf_op jit(solution)/shard_map/ppermute | solution.py:287
  30.3 0.8 %copy-start.4 = (f32[8,64,256]{2,1,0:T(8,128)}, f32[8,64,256]{2,1,0:T(8,128)S(1)}, u32[]{:S(2)}) copy-start(f32[8,64,256]{2,1,0:T(8,128)S(1)} %collective-permute-done.6.refs_3_) | copy-start | bytes 1572868
  31.1 0.8 %copy-start.5 = (f32[8,64,256]{2,1,0:T(8,128)}, f32[8,64,256]{2,1,0:T(8,128)S(1)}, u32[]{:S(2)}) copy-start(f32[8,64,256]{2,1,0:T(8,128)S(1)} %collective-permute-done.7.refs_4_) | copy-start | bytes 1572868
  35.1 1.0 %copy-start = (bf16[2,512,512]{2,1,0:T(8,128)(2,1)}, bf16[2,512,512]{2,1,0:T(8,128)(2,1)S(1)}, u32[]{:S(2)}) copy-start(bf16[2,512,512]{2,1,0:T(8,128)(2,1)S(1)} %get-tuple-element.48.farthest_ref) | copy-start | bytes 3145732
  40.0 4.2 %collective-permute-start.9 = (f32[2,16,512]{2,1,0:T(8,128)S(1)}, f32[2,16,512]{2,1,0:T(8,128)S(1)}, u32[]{:S(2)}, u32[]{:S(2)}) collective-permute-start(f32[2,16,512]{2,1,0:T(8,128)S(1)} %get-tuple-element.40), channel_id=1, source_target_pairs={{0,2},{1,3},{8,10},{9,11},{16,18},{17,19},{24,26},{25,27}} | collective-permute-start | bytes 196616 | tf_op jit(solution)/shard_map/ppermute | solution.py:311
  44.8 4.0 %collective-permute-start.10 = (f32[2,16,512]{2,1,0:T(8,128)S(1)}, f32[2,16,512]{2,1,0:T(8,128)S(1)}, u32[]{:S(2)}, u32[]{:S(2)}) collective-permute-start(f32[2,16,512]{2,1,0:T(8,128)S(1)} %get-tuple-element.44), channel_id=1, source_target_pairs={{2,4},{3,5},{10,12},{11,13},{18,20},{19,21},{26,28},{27,29}} | collective-permute-start | bytes 196616 | tf_op jit(solution)/shard_map/ppermute | solution.py:311
  47.1 3.2 %collective-permute-start.12 = (f32[16,512]{1,0:T(8,128)S(1)}, f32[16,512]{1,0:T(8,128)S(1)}, u32[]{:S(2)}, u32[]{:S(2)}) collective-permute-start(f32[16,512]{1,0:T(8,128)S(1)} %chain_direct.1), channel_id=1, source_target_pairs={{0,6},{1,7},{8,14},{9,15},{16,22},{17,23},{24,30},{25,31}} | collective-permute-start | bytes 98312 | tf_op jit(solution)/shard_map/ppermute | solution.py:308
  49.2 1.2 %collective-permute-start.11 = (f32[1,16,512]{2,1,0:T(8,128)S(1)}, f32[1,16,512]{2,1,0:T(8,128)S(1)}, u32[]{:S(2)}, u32[]{:S(2)}) collective-permute-start(f32[1,16,512]{2,1,0:T(8,128)S(1)} %get-tuple-element.46), channel_id=1, source_target_pairs={{4,6},{5,7},{12,14},{13,15},{20,22},{21,23},{28,30},{29,31}} | collective-permute-start | bytes 98312 | tf_op jit(solution)/shard_map/ppermute | solution.py:314

commit v7 on v6

--- a/solution.py
+++ b/solution.py
@@ -212,17 +212,19 @@
     out_ref[...] = apply(solved_ref[...], held)
 
 
-def chain_middle(residual_ref, received_ref, *refs):
-    combined_refs, (next_ref, out_ref) = refs[:-2], refs[-2:]
+def chain_middle(residual_ref, received_ref, near_ref, next_ref, out_ref):
     residual = residual_ref[...] - received_ref[0]
     next_ref[...] = residual
-    for apart, combined_ref in enumerate(combined_refs):
-        term = apply(residual, combined_ref)
-        out_ref[apart] = received_ref[1] + term if apart == 0 else term
-
-
-def chain_last(residual_ref, received_ref, direct_ref, inverse_ref, out_ref):
-    solved = apply(residual_ref[...] - (received_ref[0] + direct_ref[...]), inverse_ref)
+    term = apply(residual, near_ref)
+    out_ref[0] = received_ref[1] + term if received_ref.shape[0] > 1 else term
+
+
+def chain_second_direct(residual_ref, far_ref, out_ref):
+    out_ref[...] = apply(residual_ref[...], far_ref)
+
+
+def chain_last(residual_ref, received_ref, direct_ref, second_ref, inverse_ref, out_ref):
+    solved = apply(residual_ref[...] - ((received_ref[0] + second_ref[...]) + direct_ref[...]), inverse_ref)
     for row_part in range(4):
         start = row_part * 64
         chunk = jnp.concatenate([solved[:, start : start + 64], solved[:, start + 256 : start + 320]], axis=1)
@@ -309,11 +311,15 @@
     combined = call(combine, "combine", [weight] * 2, inverse, near, far, flops=6 * SUPER**3 * 2)
     for step in (1, 2):
         received = lax.ppermute(sent, "z", [(step - 1, step)])
-        outs = [vectors(), vectors(3 - step)]
-        residual, sent = call(chain_middle, "chain_middle", outs, residual, received, *combined[: 3 - step])
+        residual, sent = call(chain_middle, "chain_middle", [vectors(), vectors(1)], residual, received, combined[0])
+        if step == 1:
+            (second,) = call(
+                chain_second_direct, "chain_second_direct", [vectors()], residual, combined[1], flops=6 * 16 * SUPER**2
+            )
+            second = lax.ppermute(second, "z", [(1, 3)])
     received = lax.ppermute(sent, "z", [(2, 3)])
     chunk = ((4, 4, 2, RHS_PART, 128), F32)
-    (chunks,) = call(chain_last, "chain_last", [chunk], residual, received, direct, inverse)
+    (chunks,) = call(chain_last, "chain_last", [chunk], residual, received, direct, second, inverse)
     solved = lax.all_to_all(chunks.reshape(32, RHS_PART, 128), EVERY, 0, 0, tiled=True)
     (result,) = call(turn, "turn", [((PLANES, 128, columns), F32)], solved.reshape(PLANES, columns, 128))
     return result.reshape(blocks, local_rows, columns)

time: 70.7 us -> 70 us (0.990)
  blocking collectives: 18.7 us -> 17.6 us
    all_to_all x1, blocking collectives: 18.7 us -> 17.6 us  [local(): lax.all_to_all(chunks.reshape(32, RHS_PART, 128), EVERY, 0, 0, tiled=True)]
    pallas_call x9 -> x10, Pallas kernels: 7.51 us -> 7.61 us  [call(): pl.pallas_call(kernel, out_shape=[jax.ShapeDtypeStruct(*o) for o in outs]...]
  transfers between devices with their start and end apart: 14 -> 15, of which waited for: 5 -> 4; matrix products, arithmetic and copies ran while one was open for 0% -> 0% of each run, Pallas kernels for 32% -> 33%
where the time goes in v7:
time: 70 us; the launch traced here: 69.6 us
  Pallas kernels  26.8 us (38%)
  starting transfers between devices  17.8 us (25%)
  blocking collectives  17.6 us (25%)
  waiting for transfers between devices  4.57 us (7%)
  local copies, waits for them, and re-layouts  2.62 us (4%)
    all_to_all x1, blocking collectives, local(): lax.all_to_all(chunks.reshape(32, RHS_PART, 128), EVERY, 0, 0, tiled=True)  17.6 us
    pallas_call x1, Pallas kernels, earlier_residual(): pl.pallas_call(functools.partial(earlier_sums, tile), out_shape=jax.Shape...  14.9 us
    pallas_call x10, Pallas kernels, call(): pl.pallas_call(kernel, out_shape=[jax.ShapeDtypeStruct(*o) for o in outs]...  7.61 us
    all_to_all x1, starting transfers between devices, local(): lax.all_to_all(parts.reshape(32, RHS_PART, 128), EVERY, 0, 0, tiled=True)  6.28 us
    pallas_call x2, Pallas kernels, arranged(): pl.pallas_call(functools.partial(arrange, spots, len(weights)), out_shape...  3.12 us
    unnamed x12, local copies, waits for them, and re-layouts  2.62 us
    ppermute x1, starting transfers between devices, local(): from_y = swap(message, 'y')  2.59 us
    ppermute x2, starting transfers between devices, local(): received = lax.ppermute(sent, 'z', [(step - 1, step)])  2.4 us
  transfers between devices with their start and end apart: 15, of which 4 were waited for; matrix products, arithmetic and copies ran while one was open for 0% of the time, Pallas kernels for 33%

profile of v7, /device:TPU:0, one launch (start us, length us, event | category | flops | bytes accessed | tf_op | source)
XLA Modules:
  0.0 69.6 jit_solution(1058326133964703286)
XLA Ops:
  0.0 1.1 %pack.1.refs_0_ = f32[8,64,256]{2,1,0:T(8,128)S(1)} custom-call(f32[8,64,256]{2,1,0:T(8,128)} %window_ref.1, f32[8,64,256]{2,1,0:T(8,128)} %inverse_ref.1), custom_call_target="tpu_custom_call" | custom-call | tf_op jit(solution)/shard_map/pack/pallas_call | solution.py:264
  1.1 0.0 copy-start.1
  1.1 0.5 collective-permute-start.6
  1.7 2.6 %collective-permute-start.1 = (f32[8,64,256]{2,1,0:T(8,128)S(1)}, f32[8,64,256]{2,1,0:T(8,128)S(1)}, u32[]{:S(2)}, u32[]{:S(2)}) collective-permute-start(f32[8,64,256]{2,1,0:T(8,128)S(1)} %pack.1.refs_0_), channel_id=1, source_target_pairs={{0,16},{16,0},{1,17},{17,1},{2,18},{18,2},{3,19},{19,3},{4,20},{20... | collective-permute-start | bytes 1572872 | tf_op jit(solution)/shard_map/ppermute | solution.py:275
  4.3 1.5 %collective-permute-start = (f32[8,64,256]{2,1,0:T(8,128)S(1)}, f32[8,64,256]{2,1,0:T(8,128)S(1)}, u32[]{:S(2)}, u32[]{:S(2)}) collective-permute-start(f32[8,64,256]{2,1,0:T(8,128)S(1)} %pack.1.refs_0_), channel_id=1, source_target_pairs={{0,1},{1,0},{2,3},{3,2},{4,5},{5,4},{6,7},{7,6},{8,9},{9,8},{10,11... | collective-permute-start | bytes 1572872 | tf_op jit(solution)/shard_map/ppermute | solution.py:274
  5.7 14.9 %earlier.1 = f32[4,128,128]{2,1,0:T(8,128)} custom-call(s32[1]{0:T(128)} %bitcast.first_ref, f32[512,16128]{1,0:T(8,128)} %bitcast.11, f32[16128,128]{1,0:T(8,128)} %solved_ref.1, f32[512,128]{1,0:T(8,128)} %bitcast.12), custom_call_target="tpu_custom_call" | custom-call | flops 8455716864 | bytes 41287680 | tf_op jit(solution)/shard_map/earlier/pallas_call | solution.py:87
  20.7 0.0 collective-permute-done.1.second_ref.refs_2_
  20.7 0.0 copy-start.2
  20.7 0.0 collective-permute-done.first_ref.refs_1_
  20.7 0.0 copy-start.3
  20.7 0.1 collective-permute-start.7
  20.8 0.6 collective-permute-start.8
  21.4 0.5 collective-permute-start.2
  21.9 0.1 collective-permute-start.3
  22.0 6.3 %all-to-all-start = ((f32[32,16,128]{2,1,0:T(8,128)}), f32[32,16,128]{2,1,0:T(8,128)S(1)}, u32[]{:S(2)}, u32[]{:S(2)}) async-start(f32[32,16,128]{2,1,0:T(8,128)} %bitcast.3), calls=%async_computation | async-start | bytes 524288 | tf_op jit(solution)/shard_map/all_to_all | solution.py:288
  28.3 1.5 %collective-permute-done.2.refs_0_ = f32[4,64,256]{2,1,0:T(8,128)} collective-permute-done((f32[4,64,256]{2,1,0:T(8,128)S(1)}, f32[4,64,256]{2,1,0:T(8,128)}, u32[]{:S(2)}, u32[]{:S(2)}) %collective-permute-start.2) | collective-permute-done | bytes 262176 | tf_op jit(solution)/shard_map/ppermute | solution.py:286
  29.8 0.0 collective-permute-start.4
  29.8 0.2 collective-permute-done.3.refs_1_
  30.0 0.3 collective-permute-start.5
  30.3 0.0 collective-permute-done.6.refs_3_
  30.3 0.0 copy-start.4
  30.3 0.0 collective-permute-done.7.refs_4_
  30.3 0.0 copy-done.3
  30.3 0.8 %copy-done.4 = f32[8,64,256]{2,1,0:T(8,128)} copy-done((f32[8,64,256]{2,1,0:T(8,128)}, f32[8,64,256]{2,1,0:T(8,128)S(1)}, u32[]{:S(2)}) %copy-start.4) | copy-done | bytes 524312
  31.1 0.0 copy-start.5
  31.1 0.8 %copy-done.5 = f32[8,64,256]{2,1,0:T(8,128)} copy-done((f32[8,64,256]{2,1,0:T(8,128)}, f32[8,64,256]{2,1,0:T(8,128)S(1)}, u32[]{:S(2)}) %copy-start.5) | copy-done | bytes 524312
  31.9 0.0 collective-permute-done.8.refs_5_
  31.9 0.0 copy-done.1
  31.9 0.0 copy-done.2
  31.9 1.9 %arrange.1 = (bf16[2,512,512]{2,1,0:T(8,128)(2,1)S(1)}, bf16[2,512,512]{2,1,0:T(8,128)(2,1)S(1)}, bf16[2,512,512]{2,1,0:T(8,128)(2,1)S(1)}, bf16[2,512,512]{2,1,0:T(8,128)(2,1)S(1)}) custom-call(f32[8,64,256]{2,1,0:T(8,128)} %copy-done.1, f32[8,64,256]{2,1,0:T(8,128)} %copy-done.3, f32[8,64,256]{2,1,0:T(8,128)} %copy-done.2, f32[8,64,256]{2,1,0:T(8,128)} %copy-done.4, ...), custom_call_target="tpu_custom_call" | custom-call | tf_op jit(solution)/shard_map/arrange/pallas_call | solution.py:148
  33.9 0.0 collective-permute-done.4.refs_2_
  33.9 0.0 collective-permute-done.5.refs_3_
  33.9 1.2 %arrange_corner.1 = (bf16[2,512,512]{2,1,0:T(8,128)(2,1)S(1)}, bf16[2,512,512]{2,1,0:T(8,128)(2,1)S(1)}, bf16[2,512,512]{2,1,0:T(8,128)(2,1)S(1)}, bf16[2,512,512]{2,1,0:T(8,128)(2,1)S(1)}) custom-call(f32[4,64,256]{2,1,0:T(8,128)} %collective-permute-done.2.refs_0_, ...), custom_call_target="tpu_custom_call", output_to_operand_aliasing={{0}: (4, {}), {1}: (5, {}), {2}: (6, {}), {3}: (7, {})} | custom-call | tf_op jit(solution)/shard_map/arrange_corner/pallas_call | solution.py:148
  35.1 0.0 copy-start
  35.1 1.0 %copy-done = bf16[2,512,512]{2,1,0:T(8,128)(2,1)} copy-done((bf16[2,512,512]{2,1,0:T(8,128)(2,1)}, bf16[2,512,512]{2,1,0:T(8,128)(2,1)S(1)}, u32[]{:S(2)}) %copy-start) | copy-done | bytes 1048600
  36.1 0.7 invert.1.inverse_ref
  36.8 2.2 %all-to-all-done = f32[32,16,128]{2,1,0:T(8,128)S(1)} async-done(((f32[32,16,128]{2,1,0:T(8,128)}), f32[32,16,128]{2,1,0:T(8,128)S(1)}, u32[]{:S(2)}, u32[]{:S(2)}) %all-to-all-start) | async-done | bytes 262176 | tf_op jit(solution)/shard_map/all_to_all | solution.py:288
  39.0 1.0 %chain_first.1 = (f32[16,512]{1,0:T(8,128)S(1)}, f32[16,512]{1,0:T(8,128)S(1)}, f32[2,16,512]{2,1,0:T(8,128)S(1)}) custom-call(f32[4,4,2,16,128]{4,3,2,1,0:T(8,128)S(1)} %bitcast.10, bf16[2,512,512]{2,1,0:T(8,128)(2,1)S(1)} %invert.1.inverse_ref, bf16[2,512,512]{2,1,0:T(8,128)(2,1)S(1)} %get-tuple-element.37.near_ref, ...), custom_call_target="tpu_custom_call" | custom-call | tf_op jit(solution)/shard_map/chain_first/pallas_call | solution.py:248
  40.0 1.7 %collective-permute-start.9 = (f32[2,16,512]{2,1,0:T(8,128)S(1)}, f32[2,16,512]{2,1,0:T(8,128)S(1)}, u32[]{:S(2)}, u32[]{:S(2)}) collective-permute-start(f32[2,16,512]{2,1,0:T(8,128)S(1)} %get-tuple-element.40), channel_id=1, source_target_pairs={{0,2},{1,3},{8,10},{9,11},{16,18},{17,19},{24,26},{25,27}} | collective-permute-start | bytes 196616 | tf_op jit(solution)/shard_map/ppermute | solution.py:313
  41.7 1.8 %combine.1 = (bf16[2,512,512]{2,1,0:T(8,128)(2,1)S(1)}, bf16[2,512,512]{2,1,0:T(8,128)(2,1)S(1)}) custom-call(bf16[2,512,512]{2,1,0:T(8,128)(2,1)S(1)} %invert.1.inverse_ref, bf16[2,512,512]{2,1,0:T(8,128)(2,1)S(1)} %get-tuple-element.37.near_ref, bf16[2,512,512]{2,1,0:T(8,128)(2,1)S(1)} %get-tuple-element.38.far_ref), custom_call_target="tpu_custom_call" | custom-call | flops 1610612736 | bytes 2097152 | tf_op jit(solution)/shard_map/combine/pallas_call | solution.py:248
  43.5 0.6 collective-permute-done.9.received_ref
  44.2 0.4 chain_middle.2
  44.5 0.7 collective-permute-start.10
  45.2 1.6 %chain_direct.1 = f32[16,512]{1,0:T(8,128)S(1)} custom-call(f32[16,512]{1,0:T(8,128)S(1)} %get-tuple-element.46.solved_ref, bf16[2,512,512]{2,1,0:T(8,128)(2,1)} %copy-done), custom_call_target="tpu_custom_call" | custom-call | flops 25165824 | bytes 2097152 | tf_op jit(solution)/shard_map/chain_direct/pallas_call | solution.py:248
  46.9 1.7 %collective-permute-start.12 = (f32[16,512]{1,0:T(8,128)S(1)}, f32[16,512]{1,0:T(8,128)S(1)}, u32[]{:S(2)}, u32[]{:S(2)}) collective-permute-start(f32[16,512]{1,0:T(8,128)S(1)} %chain_direct.1), channel_id=1, source_target_pairs={{0,6},{1,7},{8,14},{9,15},{16,22},{17,23},{24,30},{25,31}} | collective-permute-start | bytes 98312 | tf_op jit(solution)/shard_map/ppermute | solution.py:310
  48.5 0.4 chain_second_direct.1
  48.9 0.7 collective-permute-start.13
  49.6 0.0 collective-permute-done.10.received_ref
  49.6 0.4 chain_middle.3
  50.0 0.7 collective-permute-start.11
  50.7 0.0 collective-permute-done.12.direct_ref
  50.7 0.0 collective-permute-done.13.second_ref
  50.7 0.0 collective-permute-done.11.received_ref
  50.7 0.5 chain_last.1
  51.2 17.6 %all_to_all.10 = f32[32,16,128]{2,1,0:T(8,128)S(1)} all-to-all(f32[32,16,128]{2,1,0:T(8,128)S(1)} %bitcast.9), channel_id=1, replica_groups=mesh['y'=2,'core'=2,'z'=4,'x'=2] {'z','y','core','x'}, dimensions={0} | all-to-all | bytes 524288 | tf_op jit(solution)/shard_map/all_to_all | solution.py:323
  68.8 0.8 %turn.1 = f32[4,128,128]{2,1,0:T(8,128)} custom-call(f32[4,128,128]{2,1,0:T(8,128)S(1)} %bitcast.8), custom_call_target="tpu_custom_call" | custom-call | tf_op jit(solution)/shard_map/turn/pallas_call | solution.py:248
  (1 shorter events, 0.0 us)
Async XLA Ops:
  1.1 30.8 %copy-start.1 = (f32[8,64,256]{2,1,0:T(8,128)}, f32[8,64,256]{2,1,0:T(8,128)S(1)}, u32[]{:S(2)}) copy-start(f32[8,64,256]{2,1,0:T(8,128)S(1)} %pack.1.refs_0_) | copy-start | bytes 1572868
  1.1 29.2 %collective-permute-start.6 = (f32[8,64,256]{2,1,0:T(8,128)S(1)}, f32[8,64,256]{2,1,0:T(8,128)S(1)}, u32[]{:S(2)}, u32[]{:S(2)}) collective-permute-start(f32[8,64,256]{2,1,0:T(8,128)S(1)} %pack.1.refs_0_), channel_id=1, source_target_pairs={{0,8},{8,0},{1,9},{9,1},{2,10},{10,2},{3,11},{11,3},{4,12},{12,4},... | collective-permute-start | bytes 1572872 | tf_op jit(solution)/shard_map/ppermute | solution.py:276
  1.7 19.0 %collective-permute-start.1 = (f32[8,64,256]{2,1,0:T(8,128)S(1)}, f32[8,64,256]{2,1,0:T(8,128)S(1)}, u32[]{:S(2)}, u32[]{:S(2)}) collective-permute-start(f32[8,64,256]{2,1,0:T(8,128)S(1)} %pack.1.refs_0_), channel_id=1, source_target_pairs={{0,16},{16,0},{1,17},{17,1},{2,18},{18,2},{3,19},{19,3},{4,20},{20... | collective-permute-start | bytes 1572872 | tf_op jit(solution)/shard_map/ppermute | solution.py:275
  4.3 16.4 %collective-permute-start = (f32[8,64,256]{2,1,0:T(8,128)S(1)}, f32[8,64,256]{2,1,0:T(8,128)S(1)}, u32[]{:S(2)}, u32[]{:S(2)}) collective-permute-start(f32[8,64,256]{2,1,0:T(8,128)S(1)} %pack.1.refs_0_), channel_id=1, source_target_pairs={{0,1},{1,0},{2,3},{3,2},{4,5},{5,4},{6,7},{7,6},{8,9},{9,8},{10,11... | collective-permute-start | bytes 1572872 | tf_op jit(solution)/shard_map/ppermute | solution.py:274
  20.7 11.2 %copy-start.2 = (f32[8,64,256]{2,1,0:T(8,128)}, f32[8,64,256]{2,1,0:T(8,128)S(1)}, u32[]{:S(2)}) copy-start(f32[8,64,256]{2,1,0:T(8,128)S(1)} %collective-permute-done.1.second_ref.refs_2_) | copy-start | bytes 1572868
  20.7 9.6 %copy-start.3 = (f32[8,64,256]{2,1,0:T(8,128)}, f32[8,64,256]{2,1,0:T(8,128)S(1)}, u32[]{:S(2)}) copy-start(f32[8,64,256]{2,1,0:T(8,128)S(1)} %collective-permute-done.first_ref.refs_1_) | copy-start | bytes 1572868
  20.7 9.6 %collective-permute-start.7 = (f32[8,64,256]{2,1,0:T(8,128)S(1)}, f32[8,64,256]{2,1,0:T(8,128)S(1)}, u32[]{:S(2)}, u32[]{:S(2)}) collective-permute-start(f32[8,64,256]{2,1,0:T(8,128)S(1)} %collective-permute-done.first_ref.refs_1_), channel_id=1, source_target_pairs={{0,8},{8,0},{1,9},{9,1},{2,10},{10,2},{3,11},{11,3},{4,12},{12,4},... | collective-permute-start | bytes 1572872 | tf_op jit(solution)/shard_map/ppermute | solution.py:287
  20.8 11.1 %collective-permute-start.8 = (f32[8,64,256]{2,1,0:T(8,128)S(1)}, f32[8,64,256]{2,1,0:T(8,128)}, u32[]{:S(2)}, u32[]{:S(2)}) collective-permute-start(f32[8,64,256]{2,1,0:T(8,128)S(1)} %collective-permute-done.1.second_ref.refs_2_), channel_id=1, source_target_pairs={{0,8},{8,0},{1,9},{9,1},{2,10},{10,2},{3,11},{11,3},{4,12},{12,4},... | collective-permute-start | bytes 1572872 | tf_op jit(solution)/shard_map/ppermute | solution.py:287
  21.4 8.4 %collective-permute-start.2 = (f32[4,64,256]{2,1,0:T(8,128)S(1)}, f32[4,64,256]{2,1,0:T(8,128)}, u32[]{:S(2)}, u32[]{:S(2)}) collective-permute-start(f32[4,64,256]{2,1,0:T(8,128)S(1)} %get-tuple-element.30), channel_id=1, source_target_pairs={{0,16},{16,0},{1,17},{17,1},{2,18},{18,2},{3,19},{19,3},{4,20},{20... | collective-permute-start | bytes 786440 | tf_op jit(solution)/shard_map/ppermute | solution.py:286
  21.9 8.1 %collective-permute-start.3 = (f32[4,64,256]{2,1,0:T(8,128)S(1)}, f32[4,64,256]{2,1,0:T(8,128)}, u32[]{:S(2)}, u32[]{:S(2)}) collective-permute-start(f32[4,64,256]{2,1,0:T(8,128)S(1)} %get-tuple-element.31), channel_id=1, source_target_pairs={{0,1},{1,0},{2,3},{3,2},{4,5},{5,4},{6,7},{7,6},{8,9},{9,8},{10,11... | collective-permute-start | bytes 786440 | tf_op jit(solution)/shard_map/ppermute | solution.py:286
  22.0 17.0 %all-to-all-start = ((f32[32,16,128]{2,1,0:T(8,128)}), f32[32,16,128]{2,1,0:T(8,128)S(1)}, u32[]{:S(2)}, u32[]{:S(2)}) async-start(f32[32,16,128]{2,1,0:T(8,128)} %bitcast.3), calls=%async_computation | async-start | bytes 524288 | tf_op jit(solution)/shard_map/all_to_all | solution.py:288
  29.8 4.1 %collective-permute-start.4 = (f32[4,64,256]{2,1,0:T(8,128)}, f32[4,64,256]{2,1,0:T(8,128)S(1)}, u32[]{:S(2)}, u32[]{:S(2)}) collective-permute-start(f32[4,64,256]{2,1,0:T(8,128)} %collective-permute-done.2.refs_0_), channel_id=1, source_target_pairs={{0,8},{8,0},{1,9},{9,1},{2,10},{10,2},{3,11},{11,3},{4,12},{12,4},... | collective-permute-start | bytes 786440 | tf_op jit(solution)/shard_map/ppermute | solution.py:289
  30.0 3.9 %collective-permute-start.5 = (f32[4,64,256]{2,1,0:T(8,128)}, f32[4,64,256]{2,1,0:T(8,128)S(1)}, u32[]{:S(2)}, u32[]{:S(2)}) collective-permute-start(f32[4,64,256]{2,1,0:T(8,128)} %collective-permute-done.3.refs_1_), channel_id=1, source_target_pairs={{0,8},{8,0},{1,9},{9,1},{2,10},{10,2},{3,11},{11,3},{4,12},{12,4},... | collective-permute-start | bytes 786440 | tf_op jit(solution)/shard_map/ppermute | solution.py:289
  30.3 0.8 %copy-start.4 = (f32[8,64,256]{2,1,0:T(8,128)}, f32[8,64,256]{2,1,0:T(8,128)S(1)}, u32[]{:S(2)}) copy-start(f32[8,64,256]{2,1,0:T(8,128)S(1)} %collective-permute-done.6.refs_3_) | copy-start | bytes 1572868
  31.1 0.8 %copy-start.5 = (f32[8,64,256]{2,1,0:T(8,128)}, f32[8,64,256]{2,1,0:T(8,128)S(1)}, u32[]{:S(2)}) copy-start(f32[8,64,256]{2,1,0:T(8,128)S(1)} %collective-permute-done.7.refs_4_) | copy-start | bytes 1572868
  35.1 1.0 %copy-start = (bf16[2,512,512]{2,1,0:T(8,128)(2,1)}, bf16[2,512,512]{2,1,0:T(8,128)(2,1)S(1)}, u32[]{:S(2)}) copy-start(bf16[2,512,512]{2,1,0:T(8,128)(2,1)S(1)} %get-tuple-element.47.farthest_ref) | copy-start | bytes 3145732
  40.0 4.2 %collective-permute-start.9 = (f32[2,16,512]{2,1,0:T(8,128)S(1)}, f32[2,16,512]{2,1,0:T(8,128)S(1)}, u32[]{:S(2)}, u32[]{:S(2)}) collective-permute-start(f32[2,16,512]{2,1,0:T(8,128)S(1)} %get-tuple-element.40), channel_id=1, source_target_pairs={{0,2},{1,3},{8,10},{9,11},{16,18},{17,19},{24,26},{25,27}} | collective-permute-start | bytes 196616 | tf_op jit(solution)/shard_map/ppermute | solution.py:313
  44.5 5.1 %collective-permute-start.10 = (f32[1,16,512]{2,1,0:T(8,128)S(1)}, f32[1,16,512]{2,1,0:T(8,128)S(1)}, u32[]{:S(2)}, u32[]{:S(2)}) collective-permute-start(f32[1,16,512]{2,1,0:T(8,128)S(1)} %get-tuple-element.43), channel_id=1, source_target_pairs={{2,4},{3,5},{10,12},{11,13},{18,20},{19,21},{26,28},{27,29}} | collective-permute-start | bytes 98312 | tf_op jit(solution)/shard_map/ppermute | solution.py:313
  46.9 3.8 %collective-permute-start.12 = (f32[16,512]{1,0:T(8,128)S(1)}, f32[16,512]{1,0:T(8,128)S(1)}, u32[]{:S(2)}, u32[]{:S(2)}) collective-permute-start(f32[16,512]{1,0:T(8,128)S(1)} %chain_direct.1), channel_id=1, source_target_pairs={{0,6},{1,7},{8,14},{9,15},{16,22},{17,23},{24,30},{25,31}} | collective-permute-start | bytes 98312 | tf_op jit(solution)/shard_map/ppermute | solution.py:310
  48.9 1.8 %collective-permute-start.13 = (f32[16,512]{1,0:T(8,128)S(1)}, f32[16,512]{1,0:T(8,128)S(1)}, u32[]{:S(2)}, u32[]{:S(2)}) collective-permute-start(f32[16,512]{1,0:T(8,128)S(1)} %chain_second_direct.1), channel_id=1, source_target_pairs={{2,6},{3,7},{10,14},{11,15},{18,22},{19,23},{26,30},{27,31}} | collective-permute-start | bytes 98312 | tf_op jit(solution)/shard_map/ppermute | solution.py:319
  50.0 0.7 %collective-permute-start.11 = (f32[1,16,512]{2,1,0:T(8,128)S(1)}, f32[1,16,512]{2,1,0:T(8,128)S(1)}, u32[]{:S(2)}, u32[]{:S(2)}) collective-permute-start(f32[1,16,512]{2,1,0:T(8,128)S(1)} %get-tuple-element.45), channel_id=1, source_target_pairs={{4,6},{5,7},{12,14},{13,15},{20,22},{21,23},{28,30},{29,31}} | collective-permute-start | bytes 98312 | tf_op jit(solution)/shard_map/ppermute | solution.py:320

commit v8 on v7

--- a/solution.py
+++ b/solution.py
@@ -190,7 +190,7 @@
     return first[:count] + first[count:] + dot_rows(high, weight_ref[1])
 
 
-def chain_first(parts_ref, inverse_ref, near_ref, far_ref, residual_ref, solved_ref, out_ref):
+def chain_first(parts_ref, inverse_ref, near_ref, residual_ref, solved_ref, out_ref):
     by_rows = []
     for row_part in range(4):
         terms = [parts_ref[z, row_part, x] for z in range(PLANES) for x in range(2)]
@@ -202,7 +202,6 @@
     solved = apply(residual, inverse_ref)
     solved_ref[...] = solved
     out_ref[0] = apply(solved, near_ref)
-    out_ref[1] = apply(solved, far_ref)
 
 
 def chain_direct(solved_ref, farthest_ref, out_ref, held, sem):
@@ -212,11 +211,14 @@
     out_ref[...] = apply(solved_ref[...], held)
 
 
-def chain_middle(residual_ref, received_ref, near_ref, next_ref, out_ref):
-    residual = residual_ref[...] - received_ref[0]
+def chain_middle(residual_ref, received_ref, *refs):
+    more_refs, (near_ref, next_ref, out_ref) = refs[:-3], refs[-3:]
+    earlier = received_ref[0]
+    for more_ref in more_refs:
+        earlier += more_ref[...]
+    residual = residual_ref[...] - earlier
     next_ref[...] = residual
-    term = apply(residual, near_ref)
-    out_ref[0] = received_ref[1] + term if received_ref.shape[0] > 1 else term
+    out_ref[0] = apply(residual, near_ref)
 
 
 def chain_second_direct(residual_ref, far_ref, out_ref):
@@ -302,16 +304,18 @@
 
     parts = parts.reshape(4, 4, 2, RHS_PART, 128)
     scratch = [pltpu.VMEM((2, SUPER, SUPER), BF16), pltpu.SemaphoreType.DMA]
-    outs = [vectors(), vectors(), vectors(2)]
-    residual, solved, sent = call(chain_first, "chain_first", outs, parts, inverse, near, far)
+    outs = [vectors(), vectors(), vectors(1)]
+    residual, solved, sent = call(chain_first, "chain_first", outs, parts, inverse, near)
     (direct,) = call(
         chain_direct, "chain_direct", [vectors()], solved, large=[farthest], scratch=scratch, flops=6 * 16 * SUPER**2
     )
     direct = lax.ppermute(direct, "z", [(0, 3)])
+    (third,) = call(chain_second_direct, "chain_third_direct", [vectors()], solved, far, flops=6 * 16 * SUPER**2)
+    third = lax.ppermute(third, "z", [(0, 2)])
     combined = call(combine, "combine", [weight] * 2, inverse, near, far, flops=6 * SUPER**3 * 2)
     for step in (1, 2):
         received = lax.ppermute(sent, "z", [(step - 1, step)])
-        residual, sent = call(chain_middle, "chain_middle", [vectors(), vectors(1)], residual, received, combined[0])
+        residual, sent = call(chain_middle, "chain_middle", [vectors(), vectors(1)], residual, received, *([third] if step == 2 else []), combined[0])
         if step == 1:
             (second,) = call(
                 chain_second_direct, "chain_second_direct", [vectors()], residual, combined[1], flops=6 * 16 * SUPER**2

time: 70 us -> 69.8 us (level)
  starting transfers between devices: 17.8 us -> 19.3 us
  blocking collectives: 17.6 us -> 16.4 us
    ppermute x0 -> x1, starting transfers between devices: none -> 1.82 us  [local(): third = lax.ppermute(third, 'z', [(0, 2)])]
    all_to_all x1, blocking collectives: 17.6 us -> 16.4 us  [local(): lax.all_to_all(chunks.reshape(32, RHS_PART, 128), EVERY, 0, 0, tiled=True)]
    pallas_call x10 -> x11, Pallas kernels: 7.61 us -> 7.71 us  [call(): pl.pallas_call(kernel, out_shape=[jax.ShapeDtypeStruct(*o) for o in outs]...]
  transfers between devices with their start and end apart: 15 -> 16, of which waited for: 4 -> 3; matrix products, arithmetic and copies ran while one was open for 0% -> 0% of each run, Pallas kernels for 33% -> 34%
where the time goes in v8:
time: 69.8 us; the launch traced here: 69.4 us
  Pallas kernels  26.9 us (39%)
  starting transfers between devices  19.3 us (28%)
  blocking collectives  16.4 us (23%)
  waiting for transfers between devices  3.99 us (6%)
  local copies, waits for them, and re-layouts  2.58 us (4%)
    all_to_all x1, blocking collectives, local(): lax.all_to_all(chunks.reshape(32, RHS_PART, 128), EVERY, 0, 0, tiled=True)  16.4 us
    pallas_call x1, Pallas kernels, earlier_residual(): pl.pallas_call(functools.partial(earlier_sums, tile), out_shape=jax.Shape...  14.9 us
    pallas_call x11, Pallas kernels, call(): pl.pallas_call(kernel, out_shape=[jax.ShapeDtypeStruct(*o) for o in outs]...  7.71 us
    all_to_all x1, starting transfers between devices, local(): lax.all_to_all(parts.reshape(32, RHS_PART, 128), EVERY, 0, 0, tiled=True)  6.28 us
    pallas_call x2, Pallas kernels, arranged(): pl.pallas_call(functools.partial(arrange, spots, len(weights)), out_shape...  3.12 us
    ppermute x1, starting transfers between devices, local(): from_y = swap(message, 'y')  2.59 us
    unnamed x12, local copies, waits for them, and re-layouts  2.58 us
    ppermute x2, starting transfers between devices, local(): received = lax.ppermute(sent, 'z', [(step - 1, step)])  2.39 us
  transfers between devices with their start and end apart: 16, of which 3 were waited for; matrix products, arithmetic and copies ran while one was open for 0% of the time, Pallas kernels for 34%

profile of v8, /device:TPU:0, one launch (start us, length us, event | category | flops | bytes accessed | tf_op | source)
XLA Modules:
  0.0 69.4 jit_solution(10076282569461501300)
XLA Ops:
  0.0 1.1 %pack.1.refs_0_ = f32[8,64,256]{2,1,0:T(8,128)S(1)} custom-call(f32[8,64,256]{2,1,0:T(8,128)} %window_ref.1, f32[8,64,256]{2,1,0:T(8,128)} %inverse_ref.1), custom_call_target="tpu_custom_call" | custom-call | tf_op jit(solution)/shard_map/pack/pallas_call | solution.py:266
  1.1 0.0 copy-start.1
  1.1 0.5 collective-permute-start.6
  1.7 2.6 %collective-permute-start.1 = (f32[8,64,256]{2,1,0:T(8,128)S(1)}, f32[8,64,256]{2,1,0:T(8,128)S(1)}, u32[]{:S(2)}, u32[]{:S(2)}) collective-permute-start(f32[8,64,256]{2,1,0:T(8,128)S(1)} %pack.1.refs_0_), channel_id=1, source_target_pairs={{0,16},{16,0},{1,17},{17,1},{2,18},{18,2},{3,19},{19,3},{4,20},{20... | collective-permute-start | bytes 1572872 | tf_op jit(solution)/shard_map/ppermute | solution.py:277
  4.3 1.5 %collective-permute-start = (f32[8,64,256]{2,1,0:T(8,128)S(1)}, f32[8,64,256]{2,1,0:T(8,128)S(1)}, u32[]{:S(2)}, u32[]{:S(2)}) collective-permute-start(f32[8,64,256]{2,1,0:T(8,128)S(1)} %pack.1.refs_0_), channel_id=1, source_target_pairs={{0,1},{1,0},{2,3},{3,2},{4,5},{5,4},{6,7},{7,6},{8,9},{9,8},{10,11... | collective-permute-start | bytes 1572872 | tf_op jit(solution)/shard_map/ppermute | solution.py:276
  5.7 14.9 %earlier.1 = f32[4,128,128]{2,1,0:T(8,128)} custom-call(s32[1]{0:T(128)} %bitcast.first_ref, f32[512,16128]{1,0:T(8,128)} %bitcast.11, f32[16128,128]{1,0:T(8,128)} %solved_ref.1, f32[512,128]{1,0:T(8,128)} %bitcast.12), custom_call_target="tpu_custom_call" | custom-call | flops 8455716864 | bytes 41287680 | tf_op jit(solution)/shard_map/earlier/pallas_call | solution.py:87
  20.7 0.0 collective-permute-done.1.second_ref.refs_2_
  20.7 0.0 copy-start.2
  20.7 0.0 collective-permute-done.first_ref.refs_1_
  20.7 0.0 copy-start.3
  20.7 0.1 collective-permute-start.7
  20.8 0.6 collective-permute-start.8
  21.4 0.5 collective-permute-start.2
  21.9 0.1 collective-permute-start.3
  22.0 6.3 %all-to-all-start = ((f32[32,16,128]{2,1,0:T(8,128)}), f32[32,16,128]{2,1,0:T(8,128)S(1)}, u32[]{:S(2)}, u32[]{:S(2)}) async-start(f32[32,16,128]{2,1,0:T(8,128)} %bitcast.3), calls=%async_computation | async-start | bytes 524288 | tf_op jit(solution)/shard_map/all_to_all | solution.py:290
  28.3 1.5 %collective-permute-done.2.refs_0_ = f32[4,64,256]{2,1,0:T(8,128)} collective-permute-done((f32[4,64,256]{2,1,0:T(8,128)S(1)}, f32[4,64,256]{2,1,0:T(8,128)}, u32[]{:S(2)}, u32[]{:S(2)}) %collective-permute-start.2) | collective-permute-done | bytes 262176 | tf_op jit(solution)/shard_map/ppermute | solution.py:288
  29.8 0.0 collective-permute-start.4
  29.8 0.2 collective-permute-done.3.refs_1_
  30.0 0.3 collective-permute-start.5
  30.3 0.0 collective-permute-done.6.refs_3_
  30.3 0.0 copy-start.4
  30.3 0.0 collective-permute-done.7.refs_4_
  30.3 0.0 copy-done.3
  30.3 0.8 %copy-done.4 = f32[8,64,256]{2,1,0:T(8,128)} copy-done((f32[8,64,256]{2,1,0:T(8,128)}, f32[8,64,256]{2,1,0:T(8,128)S(1)}, u32[]{:S(2)}) %copy-start.4) | copy-done | bytes 524312
  31.1 0.0 copy-start.5
  31.1 0.8 %copy-done.5 = f32[8,64,256]{2,1,0:T(8,128)} copy-done((f32[8,64,256]{2,1,0:T(8,128)}, f32[8,64,256]{2,1,0:T(8,128)S(1)}, u32[]{:S(2)}) %copy-start.5) | copy-done | bytes 524312
  31.9 0.0 collective-permute-done.8.refs_5_
  31.9 0.0 copy-done.1
  31.9 0.0 copy-done.2
  31.9 1.9 %arrange.1 = (bf16[2,512,512]{2,1,0:T(8,128)(2,1)S(1)}, bf16[2,512,512]{2,1,0:T(8,128)(2,1)S(1)}, bf16[2,512,512]{2,1,0:T(8,128)(2,1)S(1)}, bf16[2,512,512]{2,1,0:T(8,128)(2,1)S(1)}) custom-call(f32[8,64,256]{2,1,0:T(8,128)} %copy-done.1, f32[8,64,256]{2,1,0:T(8,128)} %copy-done.3, f32[8,64,256]{2,1,0:T(8,128)} %copy-done.2, f32[8,64,256]{2,1,0:T(8,128)} %copy-done.4, ...), custom_call_target="tpu_custom_call" | custom-call | tf_op jit(solution)/shard_map/arrange/pallas_call | solution.py:148
  33.9 0.0 collective-permute-done.4.refs_2_
  33.9 0.0 collective-permute-done.5.refs_3_
  33.9 1.2 %arrange_corner.1 = (bf16[2,512,512]{2,1,0:T(8,128)(2,1)S(1)}, bf16[2,512,512]{2,1,0:T(8,128)(2,1)S(1)}, bf16[2,512,512]{2,1,0:T(8,128)(2,1)S(1)}, bf16[2,512,512]{2,1,0:T(8,128)(2,1)S(1)}) custom-call(f32[4,64,256]{2,1,0:T(8,128)} %collective-permute-done.2.refs_0_, ...), custom_call_target="tpu_custom_call", output_to_operand_aliasing={{0}: (4, {}), {1}: (5, {}), {2}: (6, {}), {3}: (7, {})} | custom-call | tf_op jit(solution)/shard_map/arrange_corner/pallas_call | solution.py:148
  35.1 0.0 copy-start
  35.1 1.0 %copy-done = bf16[2,512,512]{2,1,0:T(8,128)(2,1)} copy-done((bf16[2,512,512]{2,1,0:T(8,128)(2,1)}, bf16[2,512,512]{2,1,0:T(8,128)(2,1)S(1)}, u32[]{:S(2)}) %copy-start) | copy-done | bytes 1048600
  36.1 0.7 invert.1.inverse_ref
  36.8 2.2 %all-to-all-done = f32[32,16,128]{2,1,0:T(8,128)S(1)} async-done(((f32[32,16,128]{2,1,0:T(8,128)}), f32[32,16,128]{2,1,0:T(8,128)S(1)}, u32[]{:S(2)}, u32[]{:S(2)}) %all-to-all-start) | async-done | bytes 262176 | tf_op jit(solution)/shard_map/all_to_all | solution.py:290
  39.0 0.7 %chain_first.1 = (f32[16,512]{1,0:T(8,128)S(1)}, f32[16,512]{1,0:T(8,128)S(1)}, f32[1,16,512]{2,1,0:T(8,128)S(1)}) custom-call(f32[4,4,2,16,128]{4,3,2,1,0:T(8,128)S(1)} %bitcast.8, bf16[2,512,512]{2,1,0:T(8,128)(2,1)S(1)} %invert.1.inverse_ref, bf16[2,512,512]{2,1,0:T(8,128)(2,1)S(1)} %get-tuple-element.37.near_ref), custom_call_target="tpu_custom_call" | custom-call | tf_op jit(solution)/shard_map/chain_first/pallas_call | solution.py:250
  39.7 1.7 %collective-permute-start.9 = (f32[1,16,512]{2,1,0:T(8,128)S(1)}, f32[1,16,512]{2,1,0:T(8,128)S(1)}, u32[]{:S(2)}, u32[]{:S(2)}) collective-permute-start(f32[1,16,512]{2,1,0:T(8,128)S(1)} %get-tuple-element.39), channel_id=1, source_target_pairs={{0,2},{1,3},{8,10},{9,11},{16,18},{17,19},{24,26},{25,27}} | collective-permute-start | bytes 98312 | tf_op jit(solution)/shard_map/ppermute | solution.py:317
  41.4 1.8 %combine.1 = (bf16[2,512,512]{2,1,0:T(8,128)(2,1)S(1)}, bf16[2,512,512]{2,1,0:T(8,128)(2,1)S(1)}) custom-call(bf16[2,512,512]{2,1,0:T(8,128)(2,1)S(1)} %invert.1.inverse_ref, bf16[2,512,512]{2,1,0:T(8,128)(2,1)S(1)} %get-tuple-element.37.near_ref, bf16[2,512,512]{2,1,0:T(8,128)(2,1)S(1)} %get-tuple-element.40.far_ref), custom_call_target="tpu_custom_call" | custom-call | flops 1610612736 | bytes 2097152 | tf_op jit(solution)/shard_map/combine/pallas_call | solution.py:250
  43.2 0.4 chain_third_direct.1
  43.6 1.8 %collective-permute-start.11 = (f32[16,512]{1,0:T(8,128)S(1)}, f32[16,512]{1,0:T(8,128)S(1)}, u32[]{:S(2)}, u32[]{:S(2)}) collective-permute-start(f32[16,512]{1,0:T(8,128)S(1)} %chain_third_direct.1), channel_id=1, source_target_pairs={{0,4},{1,5},{8,12},{9,13},{16,20},{17,21},{24,28},{25,29}} | collective-permute-start | bytes 98312 | tf_op jit(solution)/shard_map/ppermute | solution.py:314
  45.5 0.0 collective-permute-done.9.received_ref
  45.5 0.4 chain_middle.2
  45.8 0.7 collective-permute-start.10
  46.5 1.6 %chain_direct.1 = f32[16,512]{1,0:T(8,128)S(1)} custom-call(f32[16,512]{1,0:T(8,128)S(1)} %get-tuple-element.44.residual_ref.solved_ref, bf16[2,512,512]{2,1,0:T(8,128)(2,1)} %copy-done), custom_call_target="tpu_custom_call" | custom-call | flops 25165824 | bytes 2097152 | tf_op jit(solution)/shard_map/chain_direct/pallas_call | solution.py:250
  48.2 1.3 %collective-permute-start.13 = (f32[16,512]{1,0:T(8,128)S(1)}, f32[16,512]{1,0:T(8,128)S(1)}, u32[]{:S(2)}, u32[]{:S(2)}) collective-permute-start(f32[16,512]{1,0:T(8,128)S(1)} %chain_direct.1), channel_id=1, source_target_pairs={{0,6},{1,7},{8,14},{9,15},{16,22},{17,23},{24,30},{25,31}} | collective-permute-start | bytes 98312 | tf_op jit(solution)/shard_map/ppermute | solution.py:312
  49.5 0.4 chain_second_direct.1
  49.9 0.7 collective-permute-start.14
  50.5 0.0 collective-permute-done.11.refs_0_
  50.5 0.0 collective-permute-done.10.received_ref
  50.6 0.4 chain_middle.3
  50.9 0.7 collective-permute-start.12
  51.6 0.0 collective-permute-done.13.direct_ref
  51.6 0.0 collective-permute-done.14.second_ref
  51.6 0.0 collective-permute-done.12.received_ref
  51.6 0.5 chain_last.1
  52.1 16.4 %all_to_all.10 = f32[32,16,128]{2,1,0:T(8,128)S(1)} all-to-all(f32[32,16,128]{2,1,0:T(8,128)S(1)} %bitcast.10), channel_id=1, replica_groups=mesh['y'=2,'core'=2,'z'=4,'x'=2] {'z','y','core','x'}, dimensions={0} | all-to-all | bytes 524288 | tf_op jit(solution)/shard_map/all_to_all | solution.py:327
  68.6 0.8 %turn.1 = f32[4,128,128]{2,1,0:T(8,128)} custom-call(f32[4,128,128]{2,1,0:T(8,128)S(1)} %bitcast.9), custom_call_target="tpu_custom_call" | custom-call | tf_op jit(solution)/shard_map/turn/pallas_call | solution.py:250
  (1 shorter events, 0.0 us)
Async XLA Ops:
  1.1 30.8 %copy-start.1 = (f32[8,64,256]{2,1,0:T(8,128)}, f32[8,64,256]{2,1,0:T(8,128)S(1)}, u32[]{:S(2)}) copy-start(f32[8,64,256]{2,1,0:T(8,128)S(1)} %pack.1.refs_0_) | copy-start | bytes 1572868
  1.1 29.2 %collective-permute-start.6 = (f32[8,64,256]{2,1,0:T(8,128)S(1)}, f32[8,64,256]{2,1,0:T(8,128)S(1)}, u32[]{:S(2)}, u32[]{:S(2)}) collective-permute-start(f32[8,64,256]{2,1,0:T(8,128)S(1)} %pack.1.refs_0_), channel_id=1, source_target_pairs={{0,8},{8,0},{1,9},{9,1},{2,10},{10,2},{3,11},{11,3},{4,12},{12,4},... | collective-permute-start | bytes 1572872 | tf_op jit(solution)/shard_map/ppermute | solution.py:278
  1.7 19.0 %collective-permute-start.1 = (f32[8,64,256]{2,1,0:T(8,128)S(1)}, f32[8,64,256]{2,1,0:T(8,128)S(1)}, u32[]{:S(2)}, u32[]{:S(2)}) collective-permute-start(f32[8,64,256]{2,1,0:T(8,128)S(1)} %pack.1.refs_0_), channel_id=1, source_target_pairs={{0,16},{16,0},{1,17},{17,1},{2,18},{18,2},{3,19},{19,3},{4,20},{20... | collective-permute-start | bytes 1572872 | tf_op jit(solution)/shard_map/ppermute | solution.py:277
  4.3 16.4 %collective-permute-start = (f32[8,64,256]{2,1,0:T(8,128)S(1)}, f32[8,64,256]{2,1,0:T(8,128)S(1)}, u32[]{:S(2)}, u32[]{:S(2)}) collective-permute-start(f32[8,64,256]{2,1,0:T(8,128)S(1)} %pack.1.refs_0_), channel_id=1, source_target_pairs={{0,1},{1,0},{2,3},{3,2},{4,5},{5,4},{6,7},{7,6},{8,9},{9,8},{10,11... | collective-permute-start | bytes 1572872 | tf_op jit(solution)/shard_map/ppermute | solution.py:276
  20.7 11.2 %copy-start.2 = (f32[8,64,256]{2,1,0:T(8,128)}, f32[8,64,256]{2,1,0:T(8,128)S(1)}, u32[]{:S(2)}) copy-start(f32[8,64,256]{2,1,0:T(8,128)S(1)} %collective-permute-done.1.second_ref.refs_2_) | copy-start | bytes 1572868
  20.7 9.6 %copy-start.3 = (f32[8,64,256]{2,1,0:T(8,128)}, f32[8,64,256]{2,1,0:T(8,128)S(1)}, u32[]{:S(2)}) copy-start(f32[8,64,256]{2,1,0:T(8,128)S(1)} %collective-permute-done.first_ref.refs_1_) | copy-start | bytes 1572868
  20.7 9.6 %collective-permute-start.7 = (f32[8,64,256]{2,1,0:T(8,128)S(1)}, f32[8,64,256]{2,1,0:T(8,128)S(1)}, u32[]{:S(2)}, u32[]{:S(2)}) collective-permute-start(f32[8,64,256]{2,1,0:T(8,128)S(1)} %collective-permute-done.first_ref.refs_1_), channel_id=1, source_target_pairs={{0,8},{8,0},{1,9},{9,1},{2,10},{10,2},{3,11},{11,3},{4,12},{12,4},... | collective-permute-start | bytes 1572872 | tf_op jit(solution)/shard_map/ppermute | solution.py:289
  20.8 11.1 %collective-permute-start.8 = (f32[8,64,256]{2,1,0:T(8,128)S(1)}, f32[8,64,256]{2,1,0:T(8,128)}, u32[]{:S(2)}, u32[]{:S(2)}) collective-permute-start(f32[8,64,256]{2,1,0:T(8,128)S(1)} %collective-permute-done.1.second_ref.refs_2_), channel_id=1, source_target_pairs={{0,8},{8,0},{1,9},{9,1},{2,10},{10,2},{3,11},{11,3},{4,12},{12,4},... | collective-permute-start | bytes 1572872 | tf_op jit(solution)/shard_map/ppermute | solution.py:289
  21.4 8.4 %collective-permute-start.2 = (f32[4,64,256]{2,1,0:T(8,128)S(1)}, f32[4,64,256]{2,1,0:T(8,128)}, u32[]{:S(2)}, u32[]{:S(2)}) collective-permute-start(f32[4,64,256]{2,1,0:T(8,128)S(1)} %get-tuple-element.30), channel_id=1, source_target_pairs={{0,16},{16,0},{1,17},{17,1},{2,18},{18,2},{3,19},{19,3},{4,20},{20... | collective-permute-start | bytes 786440 | tf_op jit(solution)/shard_map/ppermute | solution.py:288
  21.9 8.1 %collective-permute-start.3 = (f32[4,64,256]{2,1,0:T(8,128)S(1)}, f32[4,64,256]{2,1,0:T(8,128)}, u32[]{:S(2)}, u32[]{:S(2)}) collective-permute-start(f32[4,64,256]{2,1,0:T(8,128)S(1)} %get-tuple-element.31), channel_id=1, source_target_pairs={{0,1},{1,0},{2,3},{3,2},{4,5},{5,4},{6,7},{7,6},{8,9},{9,8},{10,11... | collective-permute-start | bytes 786440 | tf_op jit(solution)/shard_map/ppermute | solution.py:288
  22.0 17.0 %all-to-all-start = ((f32[32,16,128]{2,1,0:T(8,128)}), f32[32,16,128]{2,1,0:T(8,128)S(1)}, u32[]{:S(2)}, u32[]{:S(2)}) async-start(f32[32,16,128]{2,1,0:T(8,128)} %bitcast.3), calls=%async_computation | async-start | bytes 524288 | tf_op jit(solution)/shard_map/all_to_all | solution.py:290
  29.8 4.1 %collective-permute-start.4 = (f32[4,64,256]{2,1,0:T(8,128)}, f32[4,64,256]{2,1,0:T(8,128)S(1)}, u32[]{:S(2)}, u32[]{:S(2)}) collective-permute-start(f32[4,64,256]{2,1,0:T(8,128)} %collective-permute-done.2.refs_0_), channel_id=1, source_target_pairs={{0,8},{8,0},{1,9},{9,1},{2,10},{10,2},{3,11},{11,3},{4,12},{12,4},... | collective-permute-start | bytes 786440 | tf_op jit(solution)/shard_map/ppermute | solution.py:291
  30.0 3.9 %collective-permute-start.5 = (f32[4,64,256]{2,1,0:T(8,128)}, f32[4,64,256]{2,1,0:T(8,128)S(1)}, u32[]{:S(2)}, u32[]{:S(2)}) collective-permute-start(f32[4,64,256]{2,1,0:T(8,128)} %collective-permute-done.3.refs_1_), channel_id=1, source_target_pairs={{0,8},{8,0},{1,9},{9,1},{2,10},{10,2},{3,11},{11,3},{4,12},{12,4},... | collective-permute-start | bytes 786440 | tf_op jit(solution)/shard_map/ppermute | solution.py:291
  30.3 0.8 %copy-start.4 = (f32[8,64,256]{2,1,0:T(8,128)}, f32[8,64,256]{2,1,0:T(8,128)S(1)}, u32[]{:S(2)}) copy-start(f32[8,64,256]{2,1,0:T(8,128)S(1)} %collective-permute-done.6.refs_3_) | copy-start | bytes 1572868
  31.1 0.8 %copy-start.5 = (f32[8,64,256]{2,1,0:T(8,128)}, f32[8,64,256]{2,1,0:T(8,128)S(1)}, u32[]{:S(2)}) copy-start(f32[8,64,256]{2,1,0:T(8,128)S(1)} %collective-permute-done.7.refs_4_) | copy-start | bytes 1572868
  35.1 1.0 %copy-start = (bf16[2,512,512]{2,1,0:T(8,128)(2,1)}, bf16[2,512,512]{2,1,0:T(8,128)(2,1)S(1)}, u32[]{:S(2)}) copy-start(bf16[2,512,512]{2,1,0:T(8,128)(2,1)S(1)} %get-tuple-element.47.farthest_ref) | copy-start | bytes 3145732
  39.7 5.7 %collective-permute-start.9 = (f32[1,16,512]{2,1,0:T(8,128)S(1)}, f32[1,16,512]{2,1,0:T(8,128)S(1)}, u32[]{:S(2)}, u32[]{:S(2)}) collective-permute-start(f32[1,16,512]{2,1,0:T(8,128)S(1)} %get-tuple-element.39), channel_id=1, source_target_pairs={{0,2},{1,3},{8,10},{9,11},{16,18},{17,19},{24,26},{25,27}} | collective-permute-start | bytes 98312 | tf_op jit(solution)/shard_map/ppermute | solution.py:317
  43.6 6.9 %collective-permute-start.11 = (f32[16,512]{1,0:T(8,128)S(1)}, f32[16,512]{1,0:T(8,128)S(1)}, u32[]{:S(2)}, u32[]{:S(2)}) collective-permute-start(f32[16,512]{1,0:T(8,128)S(1)} %chain_third_direct.1), channel_id=1, source_target_pairs={{0,4},{1,5},{8,12},{9,13},{16,20},{17,21},{24,28},{25,29}} | collective-permute-start | bytes 98312 | tf_op jit(solution)/shard_map/ppermute | solution.py:314
  45.8 4.7 %collective-permute-start.10 = (f32[1,16,512]{2,1,0:T(8,128)S(1)}, f32[1,16,512]{2,1,0:T(8,128)S(1)}, u32[]{:S(2)}, u32[]{:S(2)}) collective-permute-start(f32[1,16,512]{2,1,0:T(8,128)S(1)} %get-tuple-element.43), channel_id=1, source_target_pairs={{2,4},{3,5},{10,12},{11,13},{18,20},{19,21},{26,28},{27,29}} | collective-permute-start | bytes 98312 | tf_op jit(solution)/shard_map/ppermute | solution.py:317
  48.2 3.4 %collective-permute-start.13 = (f32[16,512]{1,0:T(8,128)S(1)}, f32[16,512]{1,0:T(8,128)S(1)}, u32[]{:S(2)}, u32[]{:S(2)}) collective-permute-start(f32[16,512]{1,0:T(8,128)S(1)} %chain_direct.1), channel_id=1, source_target_pairs={{0,6},{1,7},{8,14},{9,15},{16,22},{17,23},{24,30},{25,31}} | collective-permute-start | bytes 98312 | tf_op jit(solution)/shard_map/ppermute | solution.py:312
  49.9 1.8 %collective-permute-start.14 = (f32[16,512]{1,0:T(8,128)S(1)}, f32[16,512]{1,0:T(8,128)S(1)}, u32[]{:S(2)}, u32[]{:S(2)}) collective-permute-start(f32[16,512]{1,0:T(8,128)S(1)} %chain_second_direct.1), channel_id=1, source_target_pairs={{2,6},{3,7},{10,14},{11,15},{18,22},{19,23},{26,30},{27,31}} | collective-permute-start | bytes 98312 | tf_op jit(solution)/shard_map/ppermute | solution.py:323
  50.9 0.7 %collective-permute-start.12 = (f32[1,16,512]{2,1,0:T(8,128)S(1)}, f32[1,16,512]{2,1,0:T(8,128)S(1)}, u32[]{:S(2)}, u32[]{:S(2)}) collective-permute-start(f32[1,16,512]{2,1,0:T(8,128)S(1)} %get-tuple-element.46), channel_id=1, source_target_pairs={{4,6},{5,7},{12,14},{13,15},{20,22},{21,23},{28,30},{29,31}} | collective-permute-start | bytes 98312 | tf_op jit(solution)/shard_map/ppermute | solution.py:324
